TPU v7x, 256 devices: a whole 4x4x8 slice. The times are simulated.
256 devices in a mesh: chan: 8 (over z_lo, y), win: 32 (over x, z_hi, core).
Axes of the slice: x: 4, y: 4, z: 8 (z_hi: 4, z_lo: 2; z = z_hi * 2 + z_lo), core: 2. Of those that a mesh axis runs over, the one named last changes fastest.
Arguments:
- raw_traces: bfloat16 [32, 2048, 512], P('win', 'chan'), may hold values from -6 to 6
- fir_taps: float32 [65], replicated, may hold values from -0.75 to 0.75
- source_blocks: int32 [2], replicated, may hold values from 0 to 31
- valid_counts: int32 [32, 2048], P('win', 'chan'), may hold values from 0 to 512, as said below
Outputs:
- stack: float32 [128, 201, 2048], P('win', None, 'chan')
Inputs may be any that keep to these rules, and one draw needn't show every extreme that they name: `valid_counts`: 0 marks a dead channel, and every window has one.
All inputs are finite; a program needn't handle non-finite values.
Results may differ from a plain program's by a relative error of at most 0.0028.
Values may be sent and summed in bfloat16 or wider, within the bound.
No kernel may reach another device: no remote copies, remote signals or barrier semaphores. Data moves between devices by JAX's collectives and lax.ppermute only.
A program may use at most 192 MiB of HBM per device.

v0:
```python
import math

import jax
import jax.numpy as jnp
from jax import lax
from jax.experimental import pallas as pl
from jax.experimental.pallas import tpu as pltpu
from jax.sharding import Mesh, PartitionSpec as P

BLK = 64
NBLK = 2
SAMP = 512
TAPS = 65
HALFTAPS = 32
HALFRUN = 64
MAXLAG = 100
NLAG = 2 * MAXLAG + 1
LAGPAD = 208
SRC_PAIR = 8
CHUNKS = ((0, 256), (256, 256))


def split_terms(x):
    hi = x.astype(jnp.bfloat16)
    rest = x - hi.astype(jnp.float32)
    mid = rest.astype(jnp.bfloat16)
    lo = (rest - mid.astype(jnp.float32)).astype(jnp.bfloat16)
    return hi, mid, lo


def dot_t(a, b):
    return lax.dot_general(a, b, (((1,), (1,)), ((), ())), preferred_element_type=jnp.float32)


def prep_body(blocks_ref, chan_ref, raw_ref, taps_ref, counts_ref, *refs):
    out_refs, contrib_ref, full_ref = refs[:-2], refs[-2], refs[-1]
    channels = raw_ref.shape[0]
    side = jnp.zeros((channels, 128), jnp.bfloat16)
    raw = jnp.concatenate([side, raw_ref[...], side], axis=1)
    rows = jnp.broadcast_to(taps_ref[...], (256, 512))
    strips = split_terms(pltpu.roll(rows, 0, 1, stride=1, stride_axis=0))
    filtered = []
    for m in range(2):
        part = raw[:, 256 * m : 256 * m + 512]
        filtered.append(dot_t(part, strips[0]) + (dot_t(part, strips[1]) + dot_t(part, strips[2])))
    filtered = jnp.concatenate(filtered, axis=1)
    at_row = lax.broadcasted_iota(jnp.int32, (256, 512), 0) + 128
    at_col = lax.broadcasted_iota(jnp.int32, (256, 512), 1)
    band = jnp.where(jnp.abs(at_row - at_col) <= HALFRUN, 1.0, 0.0).astype(jnp.bfloat16)
    pieces = [jnp.concatenate([side, t, side], axis=1) for t in split_terms(jnp.abs(filtered))]
    summed = []
    for m in range(2):
        cut = [p[:, 256 * m : 256 * m + 512] for p in pieces]
        summed.append(dot_t(cut[0], band) + (dot_t(cut[1], band) + dot_t(cut[2], band)))
    summed = jnp.concatenate(summed, axis=1)
    at = lax.broadcasted_iota(jnp.int32, (1, SAMP), 1)
    counted = jnp.minimum(at + HALFRUN, SAMP - 1) - jnp.maximum(at - HALFRUN, 0) + 1
    envelope = summed / counted.astype(jnp.float32)
    whitened = filtered / (envelope + 1e-06)
    counts = jnp.broadcast_to(counts_ref[...].astype(jnp.float32), (128, channels)).T
    counts = jnp.concatenate([counts] * (SAMP // 128), axis=1)
    live = at.astype(jnp.float32) < counts
    whitened = jnp.where(live, whitened, 0.0)
    rounded = whitened.astype(jnp.bfloat16)
    for ref, (start, width) in zip(out_refs, CHUNKS):
        ref[...] = rounded[:, start : start + width]
    full_ref[...] = rounded
    held = channels // BLK
    for number in range(NBLK):
        local = blocks_ref[number] - chan_ref[0] * held
        owned = jnp.logical_and(local >= 0, local < held)
        start = pl.multiple_of(jnp.clip(local, 0, held - 1) * BLK, BLK)
        rows = full_ref[pl.ds(start, BLK), :].astype(jnp.float32)
        rows = jnp.where(owned, rows, 0.0)
        contrib_ref[number * BLK : (number + 1) * BLK, :] = rows.astype(jnp.bfloat16)


def prep(raw, fir_taps, source_blocks, counts, chan):
    channels = raw.shape[0]
    taps = jnp.pad(fir_taps.reshape(1, TAPS), ((0, 0), (128 - HALFTAPS, 512 - TAPS - 128 + HALFTAPS)))
    smem = pl.BlockSpec(memory_space=pltpu.SMEM)
    vmem = pl.BlockSpec(memory_space=pltpu.VMEM)
    return pl.pallas_call(
        prep_body,
        in_specs=[smem, smem, vmem, vmem, vmem],
        out_specs=[vmem] * (len(CHUNKS) + 1),
        out_shape=[jax.ShapeDtypeStruct((channels, width), jnp.bfloat16) for _, width in CHUNKS]
        + [jax.ShapeDtypeStruct((NBLK * BLK, SAMP), jnp.bfloat16)],
        scratch_shapes=[pltpu.VMEM((channels, SAMP), jnp.bfloat16)],
        name="prep",
    )(source_blocks, chan, raw, taps, counts)


def fill_lagged(rows, first, lagged_ref, start, width):
    low, high = start - 256, start + width + 128
    parts = []
    if low < 0:
        parts.append(jnp.zeros((SRC_PAIR, -low), jnp.float32))
    parts.append(rows[:, max(low, 0) : min(high, SAMP)])
    if high > SAMP:
        parts.append(jnp.zeros((SRC_PAIR, high - SAMP), jnp.float32))
    around = jnp.concatenate(parts, axis=1) if len(parts) > 1 else parts[0]
    span = high - low
    shift = 128 - MAXLAG - 256
    around = pltpu.roll(around, shift % 8, 1)
    shift = (shift - shift % 8) % span
    for at in range(SRC_PAIR // 2):
        row = jnp.broadcast_to(around[first + at : first + at + 1, :], (128, span))
        rolled = pltpu.roll(row, shift, 1, stride=1, stride_axis=0).astype(jnp.bfloat16)
        lagged_ref[at * LAGPAD : at * LAGPAD + 128, :] = rolled[:, 128 : 128 + width]
        lagged_ref[at * LAGPAD + 128 : (at + 1) * LAGPAD, :] = rolled[: LAGPAD - 128, :width]


def correlate_body(start, width, has_prev, is_last, *refs):
    refs = list(refs)
    core_ref = refs.pop(0) if is_last else None
    src_ref, recv_ref = refs.pop(0), refs.pop(0)
    prev_ref = refs.pop(0) if has_prev else None
    if is_last:
        mine_ref, other_ref, acc_ref, first_ref, second_ref = refs
    else:
        acc_ref, first_ref, second_ref = refs
    window = pl.program_id(0)

    @pl.when(window == 0)
    def _():
        acc_ref[...] = prev_ref[...] if has_prev else jnp.zeros(acc_ref.shape, jnp.float32)

    rows = src_ref[0].astype(jnp.float32)
    receivers = recv_ref[0]
    half = SRC_PAIR // 2
    for number, lagged_ref in enumerate((first_ref, second_ref)):
        fill_lagged(rows, number * half, lagged_ref, start, width)
        got = dot_t(lagged_ref[...], receivers).reshape(half, LAGPAD, receivers.shape[0])
        acc_ref[number * half : (number + 1) * half] += got

    if is_last:

        @pl.when(window == pl.num_programs(0) - 1)
        def _():
            core = core_ref[0]
            mine_ref[...] = acc_ref[pl.ds(core * half, half), :NLAG, :]
            other_ref[...] = acc_ref[pl.ds((1 - core) * half, half), :NLAG, :]


def correlate(sources, receivers, prev, core, number):
    start, width = CHUNKS[number]
    is_last = number == len(CHUNKS) - 1
    windows, local_width = receivers.shape[0], receivers.shape[1]
    acc_shape = (SRC_PAIR, LAGPAD, local_width)
    whole = lambda shape: pl.BlockSpec(shape, lambda w: (0,) * len(shape))
    half_shape = (SRC_PAIR // 2, NLAG, local_width)
    in_specs = [
        pl.BlockSpec((1, SRC_PAIR, SAMP), lambda w: (w, 0, 0)),
        pl.BlockSpec((1, local_width, width), lambda w: (w, 0, 0)),
    ]
    operands = [sources, receivers]
    if is_last:
        in_specs.insert(0, pl.BlockSpec(memory_space=pltpu.SMEM))
        operands.insert(0, core)
    if prev is not None:
        in_specs.append(whole(acc_shape))
        operands.append(prev)
    scratch = [pltpu.VMEM((SRC_PAIR // 2 * LAGPAD, width), jnp.bfloat16)] * 2
    if is_last:
        out_specs = [whole(half_shape)] * 2
        out_shape = [jax.ShapeDtypeStruct(half_shape, jnp.float32)] * 2
        scratch = [pltpu.VMEM(acc_shape, jnp.float32)] + scratch
    else:
        out_specs = whole(acc_shape)
        out_shape = jax.ShapeDtypeStruct(acc_shape, jnp.float32)

    def body(*refs):
        correlate_body(start, width, prev is not None, is_last, *refs)

    return pl.pallas_call(
        body,
        grid=(windows,),
        in_specs=in_specs,
        out_specs=out_specs,
        out_shape=out_shape,
        scratch_shapes=scratch,
        name=f"correlate_{number}",
    )(*operands)


def shards(raw_traces, fir_taps, source_blocks, valid_counts):
    chan = lax.axis_index("chan").astype(jnp.int32)
    core = lax.axis_index("core").astype(jnp.int32).reshape(1)
    chans = lax.axis_size("chan")
    spread = lax.axis_size("spread")
    *chunks, mine = prep(raw_traces[0], fir_taps, source_blocks, valid_counts, chan.reshape(1))
    gathered = [lax.all_gather(c, "spread", axis=0) for c in chunks]
    step = 1
    while step < chans:
        mine = mine + lax.ppermute(mine, "chan", [(i, i ^ step) for i in range(chans)])
        step *= 2
    mine = mine.reshape(spread, SRC_PAIR, SAMP)
    sources = lax.all_to_all(mine, "spread", split_axis=0, concat_axis=0, tiled=True)
    total = None
    for number, receivers in enumerate(gathered):
        total = correlate(sources, receivers, total, core, number)
    kept, passed = total
    got = lax.ppermute(passed, "core", [(0, 1), (1, 0)])
    factor = 1.0 / math.sqrt(SAMP * raw_traces.shape[0] * spread * 2)
    return (kept + got) * factor


def solution(mesh):
    chans, wins = mesh.devices.shape
    finer = Mesh(mesh.devices.reshape(chans, wins // 2, 2), ("chan", "spread", "core"))
    win = ("spread", "core")
    return jax.shard_map(
        shards,
        mesh=finer,
        in_specs=(P(win, "chan", None), P(), P(), P(win, "chan")),
        out_specs=P(win, None, "chan"),
        check_vma=False,
    )
```

profile of v0, /device:TPU:1, one launch (start us, length us, event | category | flops | bytes accessed | tf_op | source)
XLA Modules:
  0.0 161.4 jit_solution(11449377061148840086)
XLA Ops:
  6.5 0.0 all-gather.7.cloned.1.call-start
  6.5 1.3 pad.4.taps_ref
  7.9 3.0 %prep.1 = (bf16[256,256]{1,0:T(8,128)(2,1)}, bf16[256,256]{1,0:T(8,128)(2,1)}, bf16[128,512]{1,0:T(8,128)(2,1)}) custom-call(s32[2]{0:T(128)} %blocks_ref.1, s32[1]{0:T(128)} %bitcast.1.chan_ref, bf16[256,512]{1,0:T(8,128)(2,1)} %bitcast.10, f32[1,512]{1,0:T(1,128)} %pad.4.taps_ref, s32[1,256]{1,0:T(1,128)} %counts_ref.1), custom_call_target="tpu_custom_call" | custom-call | tf_op jit(solution)/shard_map/prep/pallas_call | solution.py:83
  10.8 0.0 all-gather.7.cloned.1.call-update
  10.9 0.0 all-gather.5.cloned.1.call-start
  10.9 0.7 all-gather.5.cloned.1.call-update
  11.6 2.2 %collective-permute-start = (bf16[128,512]{1,0:T(8,128)(2,1)}, bf16[128,512]{1,0:T(8,128)(2,1)S(1)}, u32[]{:S(2)}, u32[]{:S(2)}) collective-permute-start(bf16[128,512]{1,0:T(8,128)(2,1)} %get-tuple-element.10), channel_id=1, source_target_pairs={{0,32},{32,0},{64,96},{96,64},{128,160},{160,128},{192,224},{224,1... | collective-permute-start | bytes 393224 | tf_op jit(solution)/shard_map/ppermute | solution.py:196
  13.8 2.6 %collective-permute-done = bf16[128,512]{1,0:T(8,128)(2,1)S(1)} collective-permute-done((bf16[128,512]{1,0:T(8,128)(2,1)}, bf16[128,512]{1,0:T(8,128)(2,1)S(1)}, u32[]{:S(2)}, u32[]{:S(2)}) %collective-permute-start) | collective-permute-done | bytes 131104 | tf_op jit(solution)/shard_map/ppermute | solution.py:196
  16.4 0.9 add.14
  17.3 3.7 %collective-permute-start.1 = (bf16[128,512]{1,0:T(8,128)(2,1)S(1)}, bf16[128,512]{1,0:T(8,128)(2,1)S(1)}, u32[]{:S(2)}, u32[]{:S(2)}) collective-permute-start(bf16[128,512]{1,0:T(8,128)(2,1)S(1)} %add.14), channel_id=1, source_target_pairs={{0,64},{32,96},{64,0},{96,32},{128,192},{160,224},{192,128},{224,1... | collective-permute-start | bytes 393224 | tf_op jit(solution)/shard_map/ppermute | solution.py:196
  21.1 2.4 %collective-permute-done.1 = bf16[128,512]{1,0:T(8,128)(2,1)S(1)} collective-permute-done((bf16[128,512]{1,0:T(8,128)(2,1)S(1)}, bf16[128,512]{1,0:T(8,128)(2,1)S(1)}, u32[]{:S(2)}, u32[]{:S(2)}) %collective-permute-start.1) | collective-permute-done | bytes 131104 | tf_op jit(solution)/shard_map/ppermute | solution.py:196
  23.5 1.8 %collective-permute-start.2 = (bf16[128,512]{1,0:T(8,128)(2,1)S(1)}, bf16[128,512]{1,0:T(8,128)(2,1)S(1)}, u32[]{:S(2)}, u32[]{:S(2)}) collective-permute-start(bf16[128,512]{1,0:T(8,128)(2,1)S(1)} %add.15), channel_id=1, source_target_pairs={{0,128},{32,160},{64,192},{96,224},{128,0},{160,32},{192,64},{224,... | collective-permute-start | bytes 393224 | tf_op jit(solution)/shard_map/ppermute | solution.py:196
  25.2 2.4 %collective-permute-done.2 = bf16[128,512]{1,0:T(8,128)(2,1)S(1)} collective-permute-done((bf16[128,512]{1,0:T(8,128)(2,1)S(1)}, bf16[128,512]{1,0:T(8,128)(2,1)S(1)}, u32[]{:S(2)}, u32[]{:S(2)}) %collective-permute-start.2) | collective-permute-done | bytes 131104 | tf_op jit(solution)/shard_map/ppermute | solution.py:196
  27.6 0.7 add_bitcast_fusion
  28.2 11.5 %all-to-all-start = ((bf16[16,8,512]{2,1,0:T(8,128)(2,1)}), bf16[16,8,512]{2,1,0:T(8,128)(2,1)S(1)}, u32[]{:S(2)}, u32[]{:S(2)}) async-start(bf16[16,8,512]{2,1,0:T(8,128)(2,1)} %add_bitcast_fusion), calls=%async_computation | async-start | bytes 262144 | tf_op jit(solution)/shard_map/all_to_all | solution.py:199
  39.7 9.5 %all-to-all-done.refs_0_.refs_1_ = bf16[16,8,512]{2,1,0:T(8,128)(2,1)S(1)} async-done(((bf16[16,8,512]{2,1,0:T(8,128)(2,1)}), bf16[16,8,512]{2,1,0:T(8,128)(2,1)S(1)}, u32[]{:S(2)}, u32[]{:S(2)}) %all-to-all-start) | async-done | bytes 131104 | tf_op jit(solution)/shard_map/all_to_all | solution.py:199
  49.3 0.0 copy-start
  49.3 24.6 %all-gather.7.cloned.1.call-done = bf16[4096,256]{1,0:T(8,128)(2,1)} async-done(((bf16[256,256]{1,0:T(8,128)(2,1)}), bf16[4096,256]{1,0:T(8,128)(2,1)}) %all-gather.7.cloned.1.call-update) | async-done | bytes 2097168 | tf_op jit(solution)/shard_map/all_gather | solution.py:193
  73.9 0.0 copy-done
  73.9 13.8 %correlate_0.1.refs_3_ = f32[8,208,256]{2,1,0:T(8,128)} custom-call(bf16[16,8,512]{2,1,0:T(8,128)(2,1)} %copy-done, bf16[16,256,256]{2,1,0:T(8,128)(2,1)} %bitcast.9), custom_call_target="tpu_custom_call" | custom-call | tf_op jit(solution)/shard_map/correlate_0/pallas_call | solution.py:176
  87.7 46.0 %all-gather.5.cloned.1.call-done = bf16[4096,256]{1,0:T(8,128)(2,1)} async-done(((bf16[256,256]{1,0:T(8,128)(2,1)}), bf16[4096,256]{1,0:T(8,128)(2,1)}) %all-gather.5.cloned.1.call-update) | async-done | bytes 2097168 | tf_op jit(solution)/shard_map/all_gather | solution.py:193
  133.7 14.6 %correlate_1.1 = (f32[4,201,256]{2,1,0:T(8,128)}, f32[4,201,256]{2,1,0:T(8,128)}) custom-call(s32[1]{0:T(128)} %bitcast.refs_0_, bf16[16,8,512]{2,1,0:T(8,128)(2,1)} %copy-done, bf16[16,256,256]{2,1,0:T(8,128)(2,1)} %bitcast.8, f32[8,208,256]{2,1,0:T(8,128)} %correlate_0.1.refs_3_), custom_call_target="tpu_custom_call" | custom-call | tf_op jit(solution)/shard_map/correlate_1/pallas_call | solution.py:176
  148.3 0.0 copy-start.1
  148.3 1.8 %copy.6 = f32[4,201,256]{2,0,1:T(4,128)S(1)} copy(f32[4,201,256]{2,1,0:T(8,128)} %get-tuple-element.14) | data formatting | bytes 1646592 | tf_op jit(solution)/shard_map/correlate_1/pallas_call | solution.py:176
  150.1 0.9 collective-permute-start.3
  151.0 2.0 %collective-permute-done.3 = f32[4,201,256]{2,0,1:T(4,128)S(1)} collective-permute-done((f32[4,201,256]{2,0,1:T(4,128)S(1)}, f32[4,201,256]{2,0,1:T(4,128)S(1)}, u32[]{:S(2)}, u32[]{:S(2)}) %collective-permute-start.3) | collective-permute-done | bytes 823328 | tf_op jit(solution)/shard_map/ppermute | solution.py:204
  153.0 0.0 copy-done.1
  153.0 0.2 fusion
  153.2 1.4 copy.8
  (1 shorter events, 0.0 us)
Async XLA Ops:
  6.5 67.3 %all-gather.7.cloned.1.call-start = ((), (), s32[]{:S(2)}) async-start(), calls=%async_computation.2 | async-start | bytes 2228224 | tf_op jit(solution)/shard_map/all_gather | solution.py:193
  10.9 122.9 %all-gather.5.cloned.1.call-start = ((), (), s32[]{:S(2)}) async-start(), calls=%async_computation.1 | async-start | bytes 2228224 | tf_op jit(solution)/shard_map/all_gather | solution.py:193
  11.6 4.8 %collective-permute-start = (bf16[128,512]{1,0:T(8,128)(2,1)}, bf16[128,512]{1,0:T(8,128)(2,1)S(1)}, u32[]{:S(2)}, u32[]{:S(2)}) collective-permute-start(bf16[128,512]{1,0:T(8,128)(2,1)} %get-tuple-element.10), channel_id=1, source_target_pairs={{0,32},{32,0},{64,96},{96,64},{128,160},{160,128},{192,224},{224,1... | collective-permute-start | bytes 393224 | tf_op jit(solution)/shard_map/ppermute | solution.py:196
  17.3 6.1 %collective-permute-start.1 = (bf16[128,512]{1,0:T(8,128)(2,1)S(1)}, bf16[128,512]{1,0:T(8,128)(2,1)S(1)}, u32[]{:S(2)}, u32[]{:S(2)}) collective-permute-start(bf16[128,512]{1,0:T(8,128)(2,1)S(1)} %add.14), channel_id=1, source_target_pairs={{0,64},{32,96},{64,0},{96,32},{128,192},{160,224},{192,128},{224,1... | collective-permute-start | bytes 393224 | tf_op jit(solution)/shard_map/ppermute | solution.py:196
  23.5 4.1 %collective-permute-start.2 = (bf16[128,512]{1,0:T(8,128)(2,1)S(1)}, bf16[128,512]{1,0:T(8,128)(2,1)S(1)}, u32[]{:S(2)}, u32[]{:S(2)}) collective-permute-start(bf16[128,512]{1,0:T(8,128)(2,1)S(1)} %add.15), channel_id=1, source_target_pairs={{0,128},{32,160},{64,192},{96,224},{128,0},{160,32},{192,64},{224,... | collective-permute-start | bytes 393224 | tf_op jit(solution)/shard_map/ppermute | solution.py:196
  28.2 21.0 %all-to-all-start = ((bf16[16,8,512]{2,1,0:T(8,128)(2,1)}), bf16[16,8,512]{2,1,0:T(8,128)(2,1)S(1)}, u32[]{:S(2)}, u32[]{:S(2)}) async-start(bf16[16,8,512]{2,1,0:T(8,128)(2,1)} %add_bitcast_fusion), calls=%async_computation | async-start | bytes 262144 | tf_op jit(solution)/shard_map/all_to_all | solution.py:199
  49.3 24.6 %copy-start = (bf16[16,8,512]{2,1,0:T(8,128)(2,1)}, bf16[16,8,512]{2,1,0:T(8,128)(2,1)S(1)}, u32[]{:S(2)}) copy-start(bf16[16,8,512]{2,1,0:T(8,128)(2,1)S(1)} %all-to-all-done.refs_0_.refs_1_) | copy-start | bytes 393220
  148.3 4.6 %copy-start.1 = (f32[4,201,256]{2,1,0:T(8,128)S(1)}, f32[4,201,256]{2,1,0:T(8,128)}, u32[]{:S(2)}) copy-start(f32[4,201,256]{2,1,0:T(8,128)} %get-tuple-element.13) | copy-start | bytes 2469892
  150.1 2.9 %collective-permute-start.3 = (f32[4,201,256]{2,0,1:T(4,128)S(1)}, f32[4,201,256]{2,0,1:T(4,128)S(1)}, u32[]{:S(2)}, u32[]{:S(2)}) collective-permute-start(f32[4,201,256]{2,0,1:T(4,128)S(1)} %copy.6), channel_id=1, source_target_pairs={{0,1},{1,0},{2,3},{3,2},{4,5},{5,4},{6,7},{7,6},{8,9},{9,8},{10,11... | collective-permute-start | bytes 2469896 | tf_op jit(solution)/shard_map/ppermute | solution.py:204
Sparse Core Ops, SparseCore 0:
  11.0 62.8 all-gather.6
  76.3 57.3 all-gather.4
where the time goes:
time: 162 us; the launch traced here: 161 us
  waiting for transfers between devices  90.1 us (56%)
  Pallas kernels  31.4 us (19%)
  starting transfers between devices  20.1 us (12%)
  between operations  13.4 us (8%)
  local copies, waits for them, and re-layouts  4.52 us (3%)
  other arithmetic  1.85 us (1%)
    all_gather x2, waiting for transfers between devices, shards(): gathered = [lax.all_gather(c, 'spread', axis=0) for c in chunks]  70.6 us
    pallas_call x2, Pallas kernels, correlate(): pl.pallas_call(body, grid=(windows,), in_specs=in_specs, out_specs=out_sp...  28.5 us
    all_to_all x1, starting transfers between devices, shards(): lax.all_to_all(mine, 'spread', split_axis=0, concat_axis=0, tiled=True)  11.5 us
    all_to_all x1, waiting for transfers between devices, shards(): lax.all_to_all(mine, 'spread', split_axis=0, concat_axis=0, tiled=True)  9.51 us
    ppermute x3, starting transfers between devices, shards(): lax.ppermute(mine, 'chan', [(i, i ^ step) for i in range(chans)])  7.7 us
    ppermute x3, waiting for transfers between devices, shards(): lax.ppermute(mine, 'chan', [(i, i ^ step) for i in range(chans)])  7.28 us
  transfers between devices with their start and end apart: 7, of which 7 were waited for; matrix products, arithmetic and copies ran while one was open for 1% of the time, Pallas kernels for 9%

commit v1 on v0

--- a/solution.py
+++ b/solution.py
@@ -17,7 +17,7 @@
 NLAG = 2 * MAXLAG + 1
 LAGPAD = 208
 SRC_PAIR = 8
-CHUNKS = ((0, 256), (256, 256))
+CHUNKS = ((0, 512),)
 
 
 def split_terms(x):
@@ -113,8 +113,8 @@
 
 def correlate_body(start, width, has_prev, is_last, *refs):
     refs = list(refs)
-    core_ref = refs.pop(0) if is_last else None
-    src_ref, recv_ref = refs.pop(0), refs.pop(0)
+    _, core_ref, src_ref, recv_ref = refs[:4]
+    refs = refs[4:]
     prev_ref = refs.pop(0) if has_prev else None
     if is_last:
         mine_ref, other_ref, acc_ref, first_ref, second_ref = refs
@@ -143,21 +143,17 @@
             other_ref[...] = acc_ref[pl.ds((1 - core) * half, half), :NLAG, :]
 
 
-def correlate(sources, receivers, prev, core, number):
-    start, width = CHUNKS[number]
-    is_last = number == len(CHUNKS) - 1
+def correlate(sources, receivers, windows_of, base, prev, core, chunk, is_last):
+    start, width = chunk
     windows, local_width = receivers.shape[0], receivers.shape[1]
     acc_shape = (SRC_PAIR, LAGPAD, local_width)
-    whole = lambda shape: pl.BlockSpec(shape, lambda w: (0,) * len(shape))
+    whole = lambda shape: pl.BlockSpec(shape, lambda w, table, core: (0,) * len(shape))
     half_shape = (SRC_PAIR // 2, NLAG, local_width)
     in_specs = [
-        pl.BlockSpec((1, SRC_PAIR, SAMP), lambda w: (w, 0, 0)),
-        pl.BlockSpec((1, local_width, width), lambda w: (w, 0, 0)),
+        pl.BlockSpec((1, SRC_PAIR, SAMP), lambda w, table, core: (table[base + w], 0, 0)),
+        pl.BlockSpec((1, local_width, width), lambda w, table, core: (w, 0, 0)),
     ]
     operands = [sources, receivers]
-    if is_last:
-        in_specs.insert(0, pl.BlockSpec(memory_space=pltpu.SMEM))
-        operands.insert(0, core)
     if prev is not None:
         in_specs.append(whole(acc_shape))
         operands.append(prev)
@@ -175,41 +171,81 @@
 
     return pl.pallas_call(
         body,
-        grid=(windows,),
-        in_specs=in_specs,
-        out_specs=out_specs,
+        grid_spec=pltpu.PrefetchScalarGridSpec(
+            num_scalar_prefetch=2,
+            grid=(windows,),
+            in_specs=in_specs,
+            out_specs=out_specs,
+            scratch_shapes=scratch,
+        ),
         out_shape=out_shape,
-        scratch_shapes=scratch,
-        name=f"correlate_{number}",
-    )(*operands)
+        name="correlate",
+    )(windows_of, core, *operands)
+
+
+def ring_offset(step):
+    return jnp.where(step == 3, 2, jnp.where(step == 2, 1, -step))
+
+
+def shifted(value, axis, by):
+    size = lax.axis_size(axis)
+    return lax.ppermute(value, axis, [(i, (i + by) % size) for i in range(size)])
+
+
+def along_z(own):
+    below, above = shifted(own, "z_hi", 1), shifted(own, "z_hi", -1)
+    half = own.shape[0] // 2
+    low = shifted(below[:half], "z_hi", 1)
+    high = shifted(above[half:], "z_hi", -1)
+    return jnp.stack([own, below, above, jnp.concatenate([low, high], axis=0)])
+
+
+def along_x(bundle, before, after):
+    half = bundle.shape[0] // 2
+    low = shifted(before[:half], "x", 1)
+    high = shifted(after[half:], "x", -1)
+    return [bundle, before, after, low, high]
 
 
 def shards(raw_traces, fir_taps, source_blocks, valid_counts):
     chan = lax.axis_index("chan").astype(jnp.int32)
     core = lax.axis_index("core").astype(jnp.int32).reshape(1)
-    chans = lax.axis_size("chan")
-    spread = lax.axis_size("spread")
+    at_x = lax.axis_index("x").astype(jnp.int32)
+    at_z = lax.axis_index("z_hi").astype(jnp.int32)
+    chans, size_x, size_z = lax.axis_size("chan"), lax.axis_size("x"), lax.axis_size("z_hi")
     *chunks, mine = prep(raw_traces[0], fir_taps, source_blocks, valid_counts, chan.reshape(1))
-    gathered = [lax.all_gather(c, "spread", axis=0) for c in chunks]
+    bundles = [along_z(c) for c in chunks]
     step = 1
     while step < chans:
         mine = mine + lax.ppermute(mine, "chan", [(i, i ^ step) for i in range(chans)])
         step *= 2
-    mine = mine.reshape(spread, SRC_PAIR, SAMP)
-    sources = lax.all_to_all(mine, "spread", split_axis=0, concat_axis=0, tiled=True)
-    total = None
-    for number, receivers in enumerate(gathered):
-        total = correlate(sources, receivers, total, core, number)
+    mine, *bundles = lax.optimization_barrier((mine, *bundles))
+    mine = mine.reshape(size_x * size_z, SRC_PAIR, SAMP)
+    sources = lax.all_to_all(mine, ("x", "z_hi"), split_axis=0, concat_axis=0, tiled=True)
+    sent = [(shifted(b, "x", 1), shifted(b, "x", -1)) for b in bundles]
+    sources, sent = lax.optimization_barrier((sources, sent))
+    bundles = [along_x(b, *pair) for b, pair in zip(bundles, sent)]
+    steps = jnp.arange(size_x * size_z, dtype=jnp.int32)
+    off_x, off_z = ring_offset(steps >> 2), ring_offset(steps & 3)
+    windows_of = ((at_x + off_x) & (size_x - 1)) * size_z + ((at_z + off_z) & (size_z - 1))
+    work = [(c, piece) for c, pieces in zip(CHUNKS, bundles) for piece in pieces]
+    total, base = None, 0
+    for number, (chunk, receivers) in enumerate(work):
+        is_last = number == len(work) - 1
+        total = correlate(sources, receivers, windows_of, base, total, core, chunk, is_last)
+        base = (base + receivers.shape[0]) % (size_x * size_z)
     kept, passed = total
-    got = lax.ppermute(passed, "core", [(0, 1), (1, 0)])
-    factor = 1.0 / math.sqrt(SAMP * raw_traces.shape[0] * spread * 2)
+    got = shifted(passed, "core", 1)
+    factor = 1.0 / math.sqrt(SAMP * size_x * size_z * 2)
     return (kept + got) * factor
 
 
 def solution(mesh):
     chans, wins = mesh.devices.shape
-    finer = Mesh(mesh.devices.reshape(chans, wins // 2, 2), ("chan", "spread", "core"))
-    win = ("spread", "core")
+    finer = Mesh(
+        mesh.devices.reshape(chans, 4, wins // 8, 2), ("chan", "x", "z_hi", "core")
+    )
+    win = ("x", "z_hi", "core")
     return jax.shard_map(
         shards,
         mesh=finer,

time: 162 us -> 109 us (0.67)
  waiting for transfers between devices: 90.1 us -> 14.3 us
  blocking collectives: 0 us -> 24.3 us
  between operations: 13.4 us -> 0.09 us
  starting transfers between devices: 20.1 us -> 27.4 us
  Pallas kernels: 31.4 us -> 33.9 us
  local copies, waits for them, and re-layouts: 4.52 us -> 6.27 us
    all_gather x2 -> x0, waiting for transfers between devices: 70.6 us -> none  [shards(): gathered = [lax.all_gather(c, 'spread', axis=0) for c in chunks]]
    all_to_all x0 -> x1, blocking collectives: none -> 24.3 us  [shards(): lax.all_to_all(mine, ('x', 'z_hi'), split_axis=0, concat_axis=0, tiled=True)]
    ppermute x1 -> x9, starting transfers between devices: 0.89 us -> 22.1 us  [shifted(): lax.ppermute(value, axis, [(i, (i + by) % size) for i in range(size)])]
    all_to_all x1 -> x0, starting transfers between devices: 11.5 us -> none  [shards(): lax.all_to_all(mine, 'spread', split_axis=0, concat_axis=0, tiled=True)]
    all_to_all x1 -> x0, waiting for transfers between devices: 9.51 us -> none  [shards(): lax.all_to_all(mine, 'spread', split_axis=0, concat_axis=0, tiled=True)]
    ppermute x1 -> x9, waiting for transfers between devices: 1.96 us -> 7.05 us  [shifted(): lax.ppermute(value, axis, [(i, (i + by) % size) for i in range(size)])]
    pallas_call x2 -> x5, Pallas kernels: 28.5 us -> 30.9 us  [correlate(): pl.pallas_call(body, grid_spec=pltpu.PrefetchScalarGridSpec(num_scalar_pr...]
    ppermute x3, starting transfers between devices: 7.7 us -> 5.34 us  [shards(): lax.ppermute(mine, 'chan', [(i, i ^ step) for i in range(chans)])]
  transfers between devices with their start and end apart: 7 -> 12, of which waited for: 7 -> 5; matrix products, arithmetic and copies ran while one was open for 1% -> 2% of each run, Pallas kernels for 9% -> 24%
where the time goes in v1:
time: 109 us; the launch traced here: 108 us
  Pallas kernels  33.9 us (31%)
  starting transfers between devices  27.4 us (25%)
  blocking collectives  24.3 us (22%)
  waiting for transfers between devices  14.3 us (13%)
  local copies, waits for them, and re-layouts  6.27 us (6%)
  other arithmetic  1.92 us (2%)
    pallas_call x5, Pallas kernels, correlate(): pl.pallas_call(body, grid_spec=pltpu.PrefetchScalarGridSpec(num_scalar_pr...  30.9 us
    all_to_all x1, blocking collectives, shards(): lax.all_to_all(mine, ('x', 'z_hi'), split_axis=0, concat_axis=0, tiled=True)  24.3 us
    ppermute x9, starting transfers between devices, shifted(): lax.ppermute(value, axis, [(i, (i + by) % size) for i in range(size)])  22.1 us
    ppermute x3, waiting for transfers between devices, shards(): lax.ppermute(mine, 'chan', [(i, i ^ step) for i in range(chans)])  7.24 us
    ppermute x9, waiting for transfers between devices, shifted(): lax.ppermute(value, axis, [(i, (i + by) % size) for i in range(size)])  7.05 us
    ppermute x3, starting transfers between devices, shards(): lax.ppermute(mine, 'chan', [(i, i ^ step) for i in range(chans)])  5.34 us
    pallas_call x1, Pallas kernels, prep(): pl.pallas_call(prep_body, in_specs=[smem, smem, vmem, vmem, vmem], out_sp...  3.01 us
  transfers between devices with their start and end apart: 12, of which 5 were waited for; matrix products, arithmetic and copies ran while one was open for 2% of the time, Pallas kernels for 24%

profile of v1, /device:TPU:1, one launch (start us, length us, event | category | flops | bytes accessed | tf_op | source)
XLA Modules:
  0.0 108.2 jit_solution(2070589152411175908)
XLA Ops:
  0.0 1.3 %pad.4.taps_ref = f32[1,512]{1,0:T(1,128)} pad(f32[1,65]{1,0:T(1,128)} %bitcast.15, f32[]{:T(128)} %constant.28.clone.1), padding=0_0x96_351 | pad | bytes 2312 | tf_op jit(solution)/shard_map/jit(_pad)/pad | solution.py:80
  1.3 3.0 %prep.1 = (bf16[256,512]{1,0:T(8,128)(2,1)}, bf16[128,512]{1,0:T(8,128)(2,1)}) custom-call(s32[2]{0:T(128)} %blocks_ref.1, s32[1]{0:T(128)} %bitcast.1.chan_ref, bf16[256,512]{1,0:T(8,128)(2,1)} %bitcast.13, f32[1,512]{1,0:T(1,128)} %pad.4.taps_ref, s32[1,256]{1,0:T(1,128)} %counts_ref.1), custom_call_target="tpu_custom_call" | custom-call | tf_op jit(solution)/shard_map/prep/pallas_call | solution.py:83
  4.3 3.8 %collective-permute-start.3 = (bf16[256,512]{1,0:T(8,128)(2,1)}, bf16[256,512]{1,0:T(8,128)(2,1)S(1)}, u32[]{:S(2)}, u32[]{:S(2)}) collective-permute-start(bf16[256,512]{1,0:T(8,128)(2,1)} %get-tuple-element.15), channel_id=1, source_target_pairs={{0,2},{2,4},{4,6},{6,0},{1,3},{3,5},{5,7},{7,1},{8,10},{10,12},{12... | collective-permute-start | bytes 786440 | tf_op jit(solution)/shard_map/ppermute | solution.py:192
  8.1 3.1 %collective-permute-start.4 = (bf16[256,512]{1,0:T(8,128)(2,1)}, bf16[256,512]{1,0:T(8,128)(2,1)S(1)}, u32[]{:S(2)}, u32[]{:S(2)}) collective-permute-start(bf16[256,512]{1,0:T(8,128)(2,1)} %get-tuple-element.15), channel_id=1, source_target_pairs={{0,6},{2,0},{4,2},{6,4},{1,7},{3,1},{5,3},{7,5},{8,14},{10,8},{12,... | collective-permute-start | bytes 786440 | tf_op jit(solution)/shard_map/ppermute | solution.py:192
  11.2 1.3 %collective-permute-start = (bf16[128,512]{1,0:T(8,128)(2,1)}, bf16[128,512]{1,0:T(8,128)(2,1)S(1)}, u32[]{:S(2)}, u32[]{:S(2)}) collective-permute-start(bf16[128,512]{1,0:T(8,128)(2,1)} %get-tuple-element.14), channel_id=1, source_target_pairs={{0,32},{32,0},{64,96},{96,64},{128,160},{160,128},{192,224},{224,1... | collective-permute-start | bytes 393224 | tf_op jit(solution)/shard_map/ppermute | solution.py:220
  12.5 3.0 %collective-permute-done = bf16[128,512]{1,0:T(8,128)(2,1)S(1)} collective-permute-done((bf16[128,512]{1,0:T(8,128)(2,1)}, bf16[128,512]{1,0:T(8,128)(2,1)S(1)}, u32[]{:S(2)}, u32[]{:S(2)}) %collective-permute-start) | collective-permute-done | bytes 131104 | tf_op jit(solution)/shard_map/ppermute | solution.py:220
  15.6 0.9 add.34
  16.5 3.0 %collective-permute-start.1 = (bf16[128,512]{1,0:T(8,128)(2,1)S(1)}, bf16[128,512]{1,0:T(8,128)(2,1)S(1)}, u32[]{:S(2)}, u32[]{:S(2)}) collective-permute-start(bf16[128,512]{1,0:T(8,128)(2,1)S(1)} %add.34), channel_id=1, source_target_pairs={{0,64},{32,96},{64,0},{96,32},{128,192},{160,224},{192,128},{224,1... | collective-permute-start | bytes 393224 | tf_op jit(solution)/shard_map/ppermute | solution.py:220
  19.5 4.3 %collective-permute-start.5 = (bf16[128,512]{1,0:T(8,128)(2,1)S(1)}, bf16[128,512]{1,0:T(8,128)(2,1)S(1)}, u32[]{:S(2)}, u32[]{:S(2)}) collective-permute-start(bf16[128,512]{1,0:T(8,128)(2,1)S(1)} %slice.16), channel_id=1, source_target_pairs={{0,2},{2,4},{4,6},{6,0},{1,3},{3,5},{5,7},{7,1},{8,10},{10,12},{12... | collective-permute-start | bytes 393224 | tf_op jit(solution)/shard_map/ppermute | solution.py:192
  23.8 0.7 collective-permute-done.4
  24.5 2.4 %collective-permute-start.6 = (bf16[128,512]{1,0:T(8,128)(2,1)S(1)}, bf16[128,512]{1,0:T(8,128)(2,1)S(1)}, u32[]{:S(2)}, u32[]{:S(2)}) collective-permute-start(bf16[128,512]{1,0:T(8,128)(2,1)S(1)} %slice.17), channel_id=1, source_target_pairs={{0,6},{2,0},{4,2},{6,4},{1,7},{3,1},{5,3},{7,5},{8,14},{10,8},{12,... | collective-permute-start | bytes 393224 | tf_op jit(solution)/shard_map/ppermute | solution.py:192
  27.0 1.0 collective-permute-start.2
  28.0 4.4 %collective-permute-done.6 = bf16[128,512]{1,0:T(8,128)(2,1)S(1)} collective-permute-done((bf16[128,512]{1,0:T(8,128)(2,1)S(1)}, bf16[128,512]{1,0:T(8,128)(2,1)S(1)}, u32[]{:S(2)}, u32[]{:S(2)}) %collective-permute-start.6) | collective-permute-done | bytes 131104 | tf_op jit(solution)/shard_map/ppermute | solution.py:192
  32.6 4.2 %collective-permute-done.2 = bf16[128,512]{1,0:T(8,128)(2,1)S(1)} collective-permute-done((bf16[128,512]{1,0:T(8,128)(2,1)S(1)}, bf16[128,512]{1,0:T(8,128)(2,1)S(1)}, u32[]{:S(2)}, u32[]{:S(2)}) %collective-permute-start.2) | collective-permute-done | bytes 131104 | tf_op jit(solution)/shard_map/ppermute | solution.py:220
  36.9 1.3 %collective-permute-start.7 = (bf16[4,256,512]{2,1,0:T(8,128)(2,1)S(1)}, bf16[4,256,512]{2,1,0:T(8,128)(2,1)S(1)}, u32[]{:S(2)}, u32[]{:S(2)}) collective-permute-start(bf16[4,256,512]{2,1,0:T(8,128)(2,1)S(1)} %pad_maximum_fusion.refs_3_), channel_id=1, source_target_pairs={{0,8},{8,16},{16,24},{24,0},{1,9},{9,17},{17,25},{25,1},{2,10},{10... | collective-permute-start | bytes 3145736 | tf_op jit(solution)/shard_map/ppermute | solution.py:192
  38.2 1.5 %collective-permute-start.8 = (bf16[4,256,512]{2,1,0:T(8,128)(2,1)S(1)}, bf16[4,256,512]{2,1,0:T(8,128)(2,1)S(1)}, u32[]{:S(2)}, u32[]{:S(2)}) collective-permute-start(bf16[4,256,512]{2,1,0:T(8,128)(2,1)S(1)} %pad_maximum_fusion.refs_3_), channel_id=1, source_target_pairs={{0,24},{8,0},{16,8},{24,16},{1,25},{9,1},{17,9},{25,17},{2,26},{10... | collective-permute-start | bytes 3145736 | tf_op jit(solution)/shard_map/ppermute | solution.py:192
  39.6 24.3 %all_to_all.5.refs_2_ = bf16[16,8,512]{2,1,0:T(8,128)(2,1)} all-to-all(bf16[16,8,512]{2,1,0:T(8,128)(2,1)S(1)} %bitcast.12), channel_id=1, replica_groups=mesh['chan'=8,'x'=4,'z_hi'=4,'core'=2] {'x','z_hi'}, dimensions={0} | all-to-all | bytes 262144 | tf_op jit(solution)/shard_map/all_to_all | solution.py:224
  63.9 0.9 slice.15
  64.8 0.4 collective-permute-start.10
  65.2 0.8 slice.14
  66.1 2.3 %collective-permute-start.9 = (bf16[2,256,512]{2,1,0:T(8,128)(2,1)}, bf16[2,256,512]{2,1,0:T(8,128)(2,1)}, u32[]{:S(2)}, u32[]{:S(2)}) collective-permute-start(bf16[2,256,512]{2,1,0:T(8,128)(2,1)} %slice.14), channel_id=1, source_target_pairs={{0,24},{8,0},{16,8},{24,16},{1,25},{9,1},{17,9},{25,17},{2,26},{10... | collective-permute-start | bytes 1572872 | tf_op jit(solution)/shard_map/ppermute | solution.py:192
  68.3 0.6 and_add_fusion.refs_0_
  68.9 6.4 %correlate.5.refs_4_ = f32[8,208,256]{2,1,0:T(8,128)} custom-call(s32[16]{0:T(128)} %and_add_fusion.refs_0_, s32[1]{0:T(128)} %bitcast.refs_1_, bf16[16,8,512]{2,1,0:T(8,128)(2,1)} %all_to_all.5.refs_2_, bf16[4,256,512]{2,1,0:T(8,128)(2,1)} %copy-done), custom_call_target="tpu_custom_call" | custom-call | tf_op jit(solution)/shard_map/correlate/pallas_call | solution.py:172
  75.3 7.0 %correlate.6.refs_4_ = f32[8,208,256]{2,1,0:T(8,128)} custom-call(s32[16]{0:T(128)} %and_add_fusion.refs_0_, s32[1]{0:T(128)} %bitcast.refs_1_, bf16[16,8,512]{2,1,0:T(8,128)(2,1)} %all_to_all.5.refs_2_, bf16[4,256,512]{2,1,0:T(8,128)(2,1)} %copy-done.1, f32[8,208,256]{2,1,0:T(8,128)} %correlate.5.refs_4_), custom_call_target="tpu_custom_call" | custom-call | tf_op jit(solution)/shard_map/correlate/pallas_call | solution.py:172
  82.3 7.0 %correlate.7.refs_4_ = f32[8,208,256]{2,1,0:T(8,128)} custom-call(s32[16]{0:T(128)} %and_add_fusion.refs_0_, s32[1]{0:T(128)} %bitcast.refs_1_, bf16[16,8,512]{2,1,0:T(8,128)(2,1)} %all_to_all.5.refs_2_, bf16[4,256,512]{2,1,0:T(8,128)(2,1)} %copy-done.2, f32[8,208,256]{2,1,0:T(8,128)} %correlate.6.refs_4_), custom_call_target="tpu_custom_call" | custom-call | tf_op jit(solution)/shard_map/correlate/pallas_call | solution.py:172
  89.3 5.2 %correlate.8.refs_4_ = f32[8,208,256]{2,1,0:T(8,128)} custom-call(s32[16]{0:T(128)} %and_add_fusion.refs_0_, s32[1]{0:T(128)} %bitcast.refs_1_, bf16[16,8,512]{2,1,0:T(8,128)(2,1)} %all_to_all.5.refs_2_, bf16[2,256,512]{2,1,0:T(8,128)(2,1)} %collective-permute-done.10.refs_3_, f32[8,208,256]{2,1,0:T(8,128)} %correlate.7.refs_4_), custom_call_target="tpu_custom_call" | custom-call | tf_op jit(solution)/shard_map/correlate/pallas_call | solution.py:172
  94.5 5.3 %correlate.9 = (f32[4,201,256]{2,1,0:T(8,128)}, f32[4,201,256]{2,1,0:T(8,128)}) custom-call(s32[16]{0:T(128)} %and_add_fusion.refs_0_, s32[1]{0:T(128)} %bitcast.refs_1_, bf16[16,8,512]{2,1,0:T(8,128)(2,1)} %all_to_all.5.refs_2_, bf16[2,256,512]{2,1,0:T(8,128)(2,1)} %collective-permute-done.9.refs_3_, f32[8,208,256]{2,1,0:T(8,128)} %correlate.8.refs_4_), custom_call_target="tpu_custom_call" | custom-call | tf_op jit(solution)/shard_map/correlate/pallas_call | solution.py:172
  99.8 1.8 %copy.6 = f32[4,201,256]{2,0,1:T(4,128)S(1)} copy(f32[4,201,256]{2,1,0:T(8,128)} %get-tuple-element.22) | data formatting | bytes 1646592 | tf_op jit(solution)/shard_map/correlate/pallas_call | solution.py:172
  101.6 3.0 %collective-permute-start.11 = (f32[4,201,256]{2,0,1:T(4,128)S(1)}, f32[4,201,256]{2,0,1:T(4,128)S(1)}, u32[]{:S(2)}, u32[]{:S(2)}) collective-permute-start(f32[4,201,256]{2,0,1:T(4,128)S(1)} %copy.6), channel_id=1, source_target_pairs={{0,1},{1,0},{2,3},{3,2},{4,5},{5,4},{6,7},{7,6},{8,9},{9,8},{10,11... | collective-permute-start | bytes 2469896 | tf_op jit(solution)/shard_map/ppermute | solution.py:192
  104.5 2.0 %collective-permute-done.11 = f32[4,201,256]{2,0,1:T(4,128)S(1)} collective-permute-done((f32[4,201,256]{2,0,1:T(4,128)S(1)}, f32[4,201,256]{2,0,1:T(4,128)S(1)}, u32[]{:S(2)}, u32[]{:S(2)}) %collective-permute-start.11) | collective-permute-done | bytes 823328 | tf_op jit(solution)/shard_map/ppermute | solution.py:192
  106.5 0.2 fusion
  106.7 1.4 %copy.8 = f32[4,201,256]{2,0,1:T(4,128)} copy(f32[4,201,256]{2,1,0:T(8,128)S(1)} %fusion) | data formatting | bytes 1646592 | tf_op jit(solution)/shard_map/mul | solution.py:240
  (23 shorter events, 0.3 us)
Async XLA Ops:
  4.3 28.2 %copy-start.4 = (bf16[256,512]{1,0:T(8,128)(2,1)S(1)}, bf16[256,512]{1,0:T(8,128)(2,1)}, u32[]{:S(2)}) copy-start(bf16[256,512]{1,0:T(8,128)(2,1)} %get-tuple-element.15) | copy-start | bytes 786436
  4.3 15.2 %collective-permute-start.3 = (bf16[256,512]{1,0:T(8,128)(2,1)}, bf16[256,512]{1,0:T(8,128)(2,1)S(1)}, u32[]{:S(2)}, u32[]{:S(2)}) collective-permute-start(bf16[256,512]{1,0:T(8,128)(2,1)} %get-tuple-element.15), channel_id=1, source_target_pairs={{0,2},{2,4},{4,6},{6,0},{1,3},{3,5},{5,7},{7,1},{8,10},{10,12},{12... | collective-permute-start | bytes 786440 | tf_op jit(solution)/shard_map/ppermute | solution.py:192
  8.1 16.4 %collective-permute-start.4 = (bf16[256,512]{1,0:T(8,128)(2,1)}, bf16[256,512]{1,0:T(8,128)(2,1)S(1)}, u32[]{:S(2)}, u32[]{:S(2)}) collective-permute-start(bf16[256,512]{1,0:T(8,128)(2,1)} %get-tuple-element.15), channel_id=1, source_target_pairs={{0,6},{2,0},{4,2},{6,4},{1,7},{3,1},{5,3},{7,5},{8,14},{10,8},{12,... | collective-permute-start | bytes 786440 | tf_op jit(solution)/shard_map/ppermute | solution.py:192
  11.2 4.3 %collective-permute-start = (bf16[128,512]{1,0:T(8,128)(2,1)}, bf16[128,512]{1,0:T(8,128)(2,1)S(1)}, u32[]{:S(2)}, u32[]{:S(2)}) collective-permute-start(bf16[128,512]{1,0:T(8,128)(2,1)} %get-tuple-element.14), channel_id=1, source_target_pairs={{0,32},{32,0},{64,96},{96,64},{128,160},{160,128},{192,224},{224,1... | collective-permute-start | bytes 393224 | tf_op jit(solution)/shard_map/ppermute | solution.py:220
  16.5 10.5 %collective-permute-start.1 = (bf16[128,512]{1,0:T(8,128)(2,1)S(1)}, bf16[128,512]{1,0:T(8,128)(2,1)S(1)}, u32[]{:S(2)}, u32[]{:S(2)}) collective-permute-start(bf16[128,512]{1,0:T(8,128)(2,1)S(1)} %add.34), channel_id=1, source_target_pairs={{0,64},{32,96},{64,0},{96,32},{128,192},{160,224},{192,128},{224,1... | collective-permute-start | bytes 393224 | tf_op jit(solution)/shard_map/ppermute | solution.py:220
  19.5 8.5 %collective-permute-start.5 = (bf16[128,512]{1,0:T(8,128)(2,1)S(1)}, bf16[128,512]{1,0:T(8,128)(2,1)S(1)}, u32[]{:S(2)}, u32[]{:S(2)}) collective-permute-start(bf16[128,512]{1,0:T(8,128)(2,1)S(1)} %slice.16), channel_id=1, source_target_pairs={{0,2},{2,4},{4,6},{6,0},{1,3},{3,5},{5,7},{7,1},{8,10},{10,12},{12... | collective-permute-start | bytes 393224 | tf_op jit(solution)/shard_map/ppermute | solution.py:192
  24.5 7.9 %collective-permute-start.6 = (bf16[128,512]{1,0:T(8,128)(2,1)S(1)}, bf16[128,512]{1,0:T(8,128)(2,1)S(1)}, u32[]{:S(2)}, u32[]{:S(2)}) collective-permute-start(bf16[128,512]{1,0:T(8,128)(2,1)S(1)} %slice.17), channel_id=1, source_target_pairs={{0,6},{2,0},{4,2},{6,4},{1,7},{3,1},{5,3},{7,5},{8,14},{10,8},{12,... | collective-permute-start | bytes 393224 | tf_op jit(solution)/shard_map/ppermute | solution.py:192
  27.0 9.9 %collective-permute-start.2 = (bf16[128,512]{1,0:T(8,128)(2,1)S(1)}, bf16[128,512]{1,0:T(8,128)(2,1)S(1)}, u32[]{:S(2)}, u32[]{:S(2)}) collective-permute-start(bf16[128,512]{1,0:T(8,128)(2,1)S(1)} %add.35), channel_id=1, source_target_pairs={{0,128},{32,160},{64,192},{96,224},{128,0},{160,32},{192,64},{224,... | collective-permute-start | bytes 393224 | tf_op jit(solution)/shard_map/ppermute | solution.py:220
  32.6 36.3 %copy-start = (bf16[4,256,512]{2,1,0:T(8,128)(2,1)}, bf16[4,256,512]{2,1,0:T(8,128)(2,1)S(1)}, u32[]{:S(2)}) copy-start(bf16[4,256,512]{2,1,0:T(8,128)(2,1)S(1)} %pad_maximum_fusion.refs_3_) | copy-start | bytes 3145732
  36.9 27.0 %collective-permute-start.7 = (bf16[4,256,512]{2,1,0:T(8,128)(2,1)S(1)}, bf16[4,256,512]{2,1,0:T(8,128)(2,1)S(1)}, u32[]{:S(2)}, u32[]{:S(2)}) collective-permute-start(bf16[4,256,512]{2,1,0:T(8,128)(2,1)S(1)} %pad_maximum_fusion.refs_3_), channel_id=1, source_target_pairs={{0,8},{8,16},{16,24},{24,0},{1,9},{9,17},{17,25},{25,1},{2,10},{10... | collective-permute-start | bytes 3145736 | tf_op jit(solution)/shard_map/ppermute | solution.py:192
  38.2 25.7 %collective-permute-start.8 = (bf16[4,256,512]{2,1,0:T(8,128)(2,1)S(1)}, bf16[4,256,512]{2,1,0:T(8,128)(2,1)S(1)}, u32[]{:S(2)}, u32[]{:S(2)}) collective-permute-start(bf16[4,256,512]{2,1,0:T(8,128)(2,1)S(1)} %pad_maximum_fusion.refs_3_), channel_id=1, source_target_pairs={{0,24},{8,0},{16,8},{24,16},{1,25},{9,1},{17,9},{25,17},{2,26},{10... | collective-permute-start | bytes 3145736 | tf_op jit(solution)/shard_map/ppermute | solution.py:192
  63.9 11.4 %copy-start.1 = (bf16[4,256,512]{2,1,0:T(8,128)(2,1)}, bf16[4,256,512]{2,1,0:T(8,128)(2,1)S(1)}, u32[]{:S(2)}) copy-start(bf16[4,256,512]{2,1,0:T(8,128)(2,1)S(1)} %collective-permute-done.7.refs_3_) | copy-start | bytes 3145732
  63.9 11.4 %copy-start.2 = (bf16[4,256,512]{2,1,0:T(8,128)(2,1)}, bf16[4,256,512]{2,1,0:T(8,128)(2,1)S(1)}, u32[]{:S(2)}) copy-start(bf16[4,256,512]{2,1,0:T(8,128)(2,1)S(1)} %collective-permute-done.8.refs_3_) | copy-start | bytes 3145732
  64.8 24.4 %collective-permute-start.10 = (bf16[2,256,512]{2,1,0:T(8,128)(2,1)}, bf16[2,256,512]{2,1,0:T(8,128)(2,1)}, u32[]{:S(2)}, u32[]{:S(2)}) collective-permute-start(bf16[2,256,512]{2,1,0:T(8,128)(2,1)} %slice.15), channel_id=1, source_target_pairs={{0,8},{8,16},{16,24},{24,0},{1,9},{9,17},{17,25},{25,1},{2,10},{10... | collective-permute-start | bytes 1572872 | tf_op jit(solution)/shard_map/ppermute | solution.py:192
  66.1 28.4 %collective-permute-start.9 = (bf16[2,256,512]{2,1,0:T(8,128)(2,1)}, bf16[2,256,512]{2,1,0:T(8,128)(2,1)}, u32[]{:S(2)}, u32[]{:S(2)}) collective-permute-start(bf16[2,256,512]{2,1,0:T(8,128)(2,1)} %slice.14), channel_id=1, source_target_pairs={{0,24},{8,0},{16,8},{24,16},{1,25},{9,1},{17,9},{25,17},{2,26},{10... | collective-permute-start | bytes 1572872 | tf_op jit(solution)/shard_map/ppermute | solution.py:192
  99.8 6.7 %copy-start.3 = (f32[4,201,256]{2,1,0:T(8,128)S(1)}, f32[4,201,256]{2,1,0:T(8,128)}, u32[]{:S(2)}) copy-start(f32[4,201,256]{2,1,0:T(8,128)} %get-tuple-element.21) | copy-start | bytes 2469892
  101.6 5.0 %collective-permute-start.11 = (f32[4,201,256]{2,0,1:T(4,128)S(1)}, f32[4,201,256]{2,0,1:T(4,128)S(1)}, u32[]{:S(2)}, u32[]{:S(2)}) collective-permute-start(f32[4,201,256]{2,0,1:T(4,128)S(1)} %copy.6), channel_id=1, source_target_pairs={{0,1},{1,0},{2,3},{3,2},{4,5},{5,4},{6,7},{7,6},{8,9},{9,8},{10,11... | collective-permute-start | bytes 2469896 | tf_op jit(solution)/shard_map/ppermute | solution.py:192

commit v2 on v1

v2 whole, which is shorter than its diff:
```python
import math

import jax
import jax.numpy as jnp
from jax import lax
from jax.experimental import pallas as pl
from jax.experimental.pallas import tpu as pltpu
from jax.sharding import Mesh, PartitionSpec as P

BLK = 64
NBLK = 2
SAMP = 512
TAPS = 65
HALFTAPS = 32
HALFRUN = 64
MAXLAG = 100
NLAG = 2 * MAXLAG + 1
LAGPAD = 208
SRC_PAIR = 8


def split_terms(x):
    hi = x.astype(jnp.bfloat16)
    rest = x - hi.astype(jnp.float32)
    mid = rest.astype(jnp.bfloat16)
    lo = (rest - mid.astype(jnp.float32)).astype(jnp.bfloat16)
    return hi, mid, lo


def dot_t(a, b):
    return lax.dot_general(a, b, (((1,), (1,)), ((), ())), preferred_element_type=jnp.float32)


def prep_body(blocks_ref, chan_ref, raw_ref, taps_ref, counts_ref, *refs):
    out_ref, contrib_ref, padded_ref = refs
    full_ref = out_ref
    channels = raw_ref.shape[0]
    side = jnp.zeros((channels, 128), jnp.bfloat16)
    raw = jnp.concatenate([side, raw_ref[...], side], axis=1)
    padded_ref[...] = jnp.zeros(padded_ref.shape, jnp.float32)
    padded_ref[:, :TAPS] = taps_ref[...]
    rows = jnp.broadcast_to(padded_ref[...], (256, 512))
    strips = split_terms(pltpu.roll(rows, 128 - HALFTAPS, 1, stride=1, stride_axis=0))
    filtered = []
    for m in range(2):
        part = raw[:, 256 * m : 256 * m + 512]
        filtered.append(dot_t(part, strips[0]) + (dot_t(part, strips[1]) + dot_t(part, strips[2])))
    filtered = jnp.concatenate(filtered, axis=1)
    at_row = lax.broadcasted_iota(jnp.int32, (256, 512), 0) + 128
    at_col = lax.broadcasted_iota(jnp.int32, (256, 512), 1)
    band = jnp.where(jnp.abs(at_row - at_col) <= HALFRUN, 1.0, 0.0).astype(jnp.bfloat16)
    pieces = [jnp.concatenate([side, t, side], axis=1) for t in split_terms(jnp.abs(filtered))]
    summed = []
    for m in range(2):
        cut = [p[:, 256 * m : 256 * m + 512] for p in pieces]
        summed.append(dot_t(cut[0], band) + (dot_t(cut[1], band) + dot_t(cut[2], band)))
    summed = jnp.concatenate(summed, axis=1)
    at = lax.broadcasted_iota(jnp.int32, (1, SAMP), 1)
    counted = jnp.minimum(at + HALFRUN, SAMP - 1) - jnp.maximum(at - HALFRUN, 0) + 1
    envelope = summed / counted.astype(jnp.float32)
    whitened = filtered / (envelope + 1e-06)
    counts = jnp.broadcast_to(counts_ref[...].astype(jnp.float32), (128, channels)).T
    counts = jnp.concatenate([counts] * (SAMP // 128), axis=1)
    live = at.astype(jnp.float32) < counts
    whitened = jnp.where(live, whitened, 0.0)
    rounded = whitened.astype(jnp.bfloat16)
    out_ref[...] = rounded
    held = channels // BLK
    for number in range(NBLK):
        local = blocks_ref[number] - chan_ref[0] * held
        owned = jnp.logical_and(local >= 0, local < held)
        start = pl.multiple_of(jnp.clip(local, 0, held - 1) * BLK, BLK)
        rows = full_ref[pl.ds(start, BLK), :].astype(jnp.float32)
        rows = jnp.where(owned, rows, 0.0)
        contrib_ref[number * BLK : (number + 1) * BLK, :] = rows.astype(jnp.bfloat16)


def prep(raw, fir_taps, source_blocks, counts, chan):
    channels = raw.shape[0]
    smem = pl.BlockSpec(memory_space=pltpu.SMEM)
    vmem = pl.BlockSpec(memory_space=pltpu.VMEM)
    return pl.pallas_call(
        prep_body,
        in_specs=[smem, smem, vmem, vmem, vmem],
        out_specs=[vmem, vmem],
        out_shape=[
            jax.ShapeDtypeStruct((channels, SAMP), jnp.bfloat16),
            jax.ShapeDtypeStruct((NBLK * BLK, SAMP), jnp.bfloat16),
        ],
        scratch_shapes=[pltpu.VMEM((1, 512), jnp.float32)],
        name="prep",
    )(source_blocks, chan, raw, fir_taps.reshape(1, TAPS), counts)


def fill_lagged(rows, first, lagged_ref):
    span = SAMP + 128
    around = jnp.concatenate([rows, jnp.zeros((SRC_PAIR, 128), jnp.float32)], axis=1)
    shift = 128 - MAXLAG
    around = pltpu.roll(around, shift % 8, 1)
    for at in range(SRC_PAIR // 2):
        row = jnp.broadcast_to(around[first + at : first + at + 1, :], (128, span))
        rolled = pltpu.roll(row, shift - shift % 8, 1, stride=1, stride_axis=0)
        rolled = rolled.astype(jnp.bfloat16)
        lagged_ref[at * LAGPAD : at * LAGPAD + 128, :] = rolled[:, 128:]
        lagged_ref[at * LAGPAD + 128 : (at + 1) * LAGPAD, :] = rolled[: LAGPAD - 128, :SAMP]


def correlate_body(has_prev, is_last, *refs):
    refs = list(refs)
    core_ref, src_ref, recv_ref = refs[:3]
    refs = refs[3:]
    prev_ref = refs.pop(0) if has_prev else None
    if is_last:
        mine_ref, other_ref, acc_ref, first_ref, second_ref = refs
    else:
        acc_ref, first_ref, second_ref = refs
    window = pl.program_id(0)

    @pl.when(window == 0)
    def _():
        acc_ref[...] = prev_ref[...] if has_prev else jnp.zeros(acc_ref.shape, jnp.float32)

    rows = src_ref[0].astype(jnp.float32)
    receivers = recv_ref[0]
    half = SRC_PAIR // 2
    for number, lagged_ref in enumerate((first_ref, second_ref)):
        fill_lagged(rows, number * half, lagged_ref)
        got = dot_t(lagged_ref[...], receivers).reshape(half, LAGPAD, receivers.shape[0])
        acc_ref[number * half : (number + 1) * half] += got

    if is_last:

        @pl.when(window == pl.num_programs(0) - 1)
        def _():
            core = core_ref[0]
            mine_ref[...] = acc_ref[pl.ds(core * half, half), :NLAG, :]
            other_ref[...] = acc_ref[pl.ds((1 - core) * half, half), :NLAG, :]


def correlate(sources, receivers, off_x, base, prev, core, is_last):
    windows, local_width = receivers.shape[0], receivers.shape[1]
    acc_shape = (SRC_PAIR, LAGPAD, local_width)
    whole = lambda shape: pl.BlockSpec(shape, lambda w, core: (0,) * len(shape))
    half_shape = (SRC_PAIR // 2, NLAG, local_width)
    in_specs = [
        pl.BlockSpec((1, SRC_PAIR, SAMP), lambda w, core: (4 * (base + w) + off_x, 0, 0)),
        pl.BlockSpec((1, local_width, SAMP), lambda w, core: (w, 0, 0)),
    ]
    operands = [sources, receivers]
    if prev is not None:
        in_specs.append(whole(acc_shape))
        operands.append(prev)
    scratch = [pltpu.VMEM((SRC_PAIR // 2 * LAGPAD, SAMP), jnp.bfloat16)] * 2
    if is_last:
        out_specs = [whole(half_shape)] * 2
        out_shape = [jax.ShapeDtypeStruct(half_shape, jnp.float32)] * 2
        scratch = [pltpu.VMEM(acc_shape, jnp.float32)] + scratch
    else:
        out_specs = whole(acc_shape)
        out_shape = jax.ShapeDtypeStruct(acc_shape, jnp.float32)

    def body(*refs):
        correlate_body(prev is not None, is_last, *refs)

    return pl.pallas_call(
        body,
        grid_spec=pltpu.PrefetchScalarGridSpec(
            num_scalar_prefetch=1,
            grid=(windows,),
            in_specs=in_specs,
            out_specs=out_specs,
            scratch_shapes=scratch,
        ),
        out_shape=out_shape,
        name="correlate",
    )(core, *operands)


def deal_body(at_ref, *refs):
    at = at_ref[0]
    in_refs, out_refs = refs[:-4], refs[-4:]
    for by, out_ref in enumerate(out_refs):
        picked = (at + by) & 3
        if len(in_refs) == 2:
            both = [ref[picked].astype(jnp.float32) for ref in in_refs]
            out_ref[...] = (both[0] + both[1]).astype(jnp.bfloat16)
        else:
            for number, ref in enumerate(in_refs):
                out_ref[number] = ref[picked]


def deal(at, arrays):
    smem = pl.BlockSpec(memory_space=pltpu.SMEM)
    vmem = pl.BlockSpec(memory_space=pltpu.VMEM)
    return pl.pallas_call(
        deal_body,
        in_specs=[smem] + [vmem] * len(arrays),
        out_specs=[vmem] * 4,
        out_shape=[jax.ShapeDtypeStruct((4, SRC_PAIR, SAMP), jnp.bfloat16)] * 4,
        name="deal",
    )(at, *arrays)


def shifted(value, axis, by):
    size = lax.axis_size(axis)
    return lax.ppermute(value, axis, [(i, (i + by) % size) for i in range(size)])


def along_z(own):
    below, above = shifted(own, "z_hi", 1), shifted(own, "z_hi", -1)
    half = own.shape[0] // 2
    low = shifted(below[:half], "z_hi", 1)
    high = shifted(above[half:], "z_hi", -1)
    return jnp.stack([own, below, above, jnp.concatenate([low, high], axis=0)])


def shards(raw_traces, fir_taps, source_blocks, valid_counts):
    chan = lax.axis_index("chan").astype(jnp.int32)
    core = lax.axis_index("core").astype(jnp.int32).reshape(1)
    at_x = lax.axis_index("x").astype(jnp.int32)
    at_z = lax.axis_index("z_hi").astype(jnp.int32)
    chans, size_x, size_z = lax.axis_size("chan"), lax.axis_size("x"), lax.axis_size("z_hi")
    own, mine = prep(raw_traces[0], fir_taps, source_blocks, valid_counts, chan.reshape(1))
    bundle = along_z(own)
    step = 1
    while step < chans // 2:
        mine = mine + lax.ppermute(mine, "chan", [(i, i ^ step) for i in range(chans)])
        step *= 2
    theirs = lax.ppermute(mine, "chan", [(i, i ^ step) for i in range(chans)])
    mine, theirs, bundle = lax.optimization_barrier((mine, theirs, bundle))
    before, after = shifted(bundle, "x", 1), shifted(bundle, "x", -1)
    grouped = (size_x, size_z, SRC_PAIR, SAMP)
    parts = [v.reshape(grouped) for v in (mine, theirs)]
    dealt = deal(at_x.reshape(1), parts)
    dealt = [dealt[0]] + [shifted(dealt[by], "x", by) for by in range(1, 4)]
    dealt = deal(at_z.reshape(1), dealt)
    dealt = [dealt[0]] + [shifted(dealt[by], "z_hi", by) for by in range(1, 4)]
    sources = jnp.concatenate([dealt[0], dealt[1], dealt[3], dealt[2]], axis=0)
    total = correlate(sources, bundle, 0, 0, None, core, False)
    total, before, after = lax.optimization_barrier((total, before, after))
    half = bundle.shape[0] // 2
    low, high = shifted(before[:half], "x", 1), shifted(after[half:], "x", -1)
    total = correlate(sources, before, 1, 0, total, core, False)
    total = correlate(sources, after, 3, 0, total, core, False)
    total = correlate(sources, low, 2, 0, total, core, False)
    total = correlate(sources, high, 2, half, total, core, True)
    kept, passed = total
    got = shifted(passed, "core", 1)
    factor = 1.0 / math.sqrt(SAMP * size_x * size_z * 2)
    return (kept + got) * factor


def solution(mesh):
    chans, wins = mesh.devices.shape
    finer = Mesh(
        mesh.devices.reshape(chans, 4, wins // 8, 2), ("chan", "x", "z_hi", "core")
    )
    win = ("x", "z_hi", "core")
    return jax.shard_map(
        shards,
        mesh=finer,
        in_specs=(P(win, "chan", None), P(), P(), P(win, "chan")),
        out_specs=P(win, None, "chan"),
        check_vma=False,
    )
```

time: 109 us -> 121 us (1.11)
  waiting for transfers between devices: 14.3 us -> 41 us
  blocking collectives: 24.3 us -> 0 us
  starting transfers between devices: 27.4 us -> 36 us
  local copies, waits for them, and re-layouts: 6.27 us -> 8.56 us
    ppermute x9 -> x15, waiting for transfers between devices: 7.05 us -> 38 us  [shifted(): lax.ppermute(value, axis, [(i, (i + by) % size) for i in range(size)])]
    all_to_all x1 -> x0, blocking collectives: 24.3 us -> none  [shards(): lax.all_to_all(mine, ('x', 'z_hi'), split_axis=0, concat_axis=0, tiled=True)]
    ppermute x9 -> x15, starting transfers between devices: 22.1 us -> 31.2 us  [shifted(): lax.ppermute(value, axis, [(i, (i + by) % size) for i in range(size)])]
    ppermute x3 -> x2, waiting for transfers between devices: 7.24 us -> 3.03 us  [shards(): lax.ppermute(mine, 'chan', [(i, i ^ step) for i in range(chans)])]
    pallas_call x5, Pallas kernels: 30.9 us -> 27.1 us  [correlate(): pl.pallas_call(body, grid_spec=pltpu.PrefetchScalarGridSpec(num_scalar_pr...]
    unnamed x10 -> x29, local copies, waits for them, and re-layouts: 0.02 us -> 3.63 us
    pallas_call x0 -> x2, Pallas kernels: none -> 3.13 us  [deal(): pl.pallas_call(deal_body, in_specs=[smem] + [vmem] * len(arrays), out_spe...]
    pad x1 -> x0, local copies, waits for them, and re-layouts: 1.31 us -> none  [prep(): jnp.pad(fir_taps.reshape(1, TAPS), ((0, 0), (128 - HALFTAPS, 512 - TAPS -...]
  transfers between devices with their start and end apart: 12 -> 18, of which waited for: 5 -> 8; matrix products, arithmetic and copies ran while one was open for 2% -> 2% of each run, Pallas kernels for 24% -> 21%
where the time goes in v2:
time: 121 us; the launch traced here: 120 us
  waiting for transfers between devices  41 us (34%)
  starting transfers between devices  36 us (30%)
  Pallas kernels  33.2 us (27%)
  local copies, waits for them, and re-layouts  8.56 us (7%)
  other arithmetic  1.34 us (1%)
    ppermute x15, waiting for transfers between devices, shifted(): lax.ppermute(value, axis, [(i, (i + by) % size) for i in range(size)])  38 us
    ppermute x15, starting transfers between devices, shifted(): lax.ppermute(value, axis, [(i, (i + by) % size) for i in range(size)])  31.2 us
    pallas_call x5, Pallas kernels, correlate(): pl.pallas_call(body, grid_spec=pltpu.PrefetchScalarGridSpec(num_scalar_pr...  27.1 us
    ppermute x2, starting transfers between devices, shards(): lax.ppermute(mine, 'chan', [(i, i ^ step) for i in range(chans)])  4.3 us
    unnamed x29, local copies, waits for them, and re-layouts  3.63 us
    pallas_call x2, Pallas kernels, deal(): pl.pallas_call(deal_body, in_specs=[smem] + [vmem] * len(arrays), out_spe...  3.13 us
    ppermute x2, waiting for transfers between devices, shards(): lax.ppermute(mine, 'chan', [(i, i ^ step) for i in range(chans)])  3.03 us
    pallas_call x1, Pallas kernels, prep(): pl.pallas_call(prep_body, in_specs=[smem, smem, vmem, vmem, vmem], out_sp...  3 us
  transfers between devices with their start and end apart: 18, of which 8 were waited for; matrix products, arithmetic and copies ran while one was open for 2% of the time, Pallas kernels for 21%

profile of v2, /device:TPU:1, one launch (start us, length us, event | category | flops | bytes accessed | tf_op | source)
XLA Modules:
  0.0 120.4 jit_solution(17008055372894370765)
XLA Ops:
  0.0 3.0 %prep.1 = (bf16[256,512]{1,0:T(8,128)(2,1)}, bf16[128,512]{1,0:T(8,128)(2,1)}) custom-call(s32[2]{0:T(128)} %blocks_ref.1, s32[1]{0:T(128)} %bitcast.3.chan_ref, bf16[256,512]{1,0:T(8,128)(2,1)} %bitcast.16, f32[1,65]{1,0:T(1,128)} %bitcast.19, s32[1,256]{1,0:T(1,128)} %counts_ref.1), custom_call_target="tpu_custom_call" | custom-call | tf_op jit(solution)/shard_map/prep/pallas_call | solution.py:82
  3.0 6.8 %collective-permute-start.4 = (bf16[256,512]{1,0:T(8,128)(2,1)}, bf16[256,512]{1,0:T(8,128)(2,1)S(1)}, u32[]{:S(2)}, u32[]{:S(2)}) collective-permute-start(bf16[256,512]{1,0:T(8,128)(2,1)} %get-tuple-element.24), channel_id=1, source_target_pairs={{0,6},{2,0},{4,2},{6,4},{1,7},{3,1},{5,3},{7,5},{8,14},{10,8},{12,... | collective-permute-start | bytes 786440 | tf_op jit(solution)/shard_map/ppermute | solution.py:206
  9.9 1.3 %collective-permute-start = (bf16[128,512]{1,0:T(8,128)(2,1)}, bf16[128,512]{1,0:T(8,128)(2,1)S(1)}, u32[]{:S(2)}, u32[]{:S(2)}) collective-permute-start(bf16[128,512]{1,0:T(8,128)(2,1)} %get-tuple-element.23), channel_id=1, source_target_pairs={{0,32},{32,0},{64,96},{96,64},{128,160},{160,128},{192,224},{224,1... | collective-permute-start | bytes 393224 | tf_op jit(solution)/shard_map/ppermute | solution.py:227
  11.2 3.0 %collective-permute-done = bf16[128,512]{1,0:T(8,128)(2,1)S(1)} collective-permute-done((bf16[128,512]{1,0:T(8,128)(2,1)}, bf16[128,512]{1,0:T(8,128)(2,1)S(1)}, u32[]{:S(2)}, u32[]{:S(2)}) %collective-permute-start) | collective-permute-done | bytes 131104 | tf_op jit(solution)/shard_map/ppermute | solution.py:227
  14.2 0.9 add.9
  15.1 3.0 %collective-permute-start.1 = (bf16[128,512]{1,0:T(8,128)(2,1)S(1)}, bf16[128,512]{1,0:T(8,128)(2,1)S(1)}, u32[]{:S(2)}, u32[]{:S(2)}) collective-permute-start(bf16[128,512]{1,0:T(8,128)(2,1)S(1)} %add.9), channel_id=1, source_target_pairs={{0,64},{32,96},{64,0},{96,32},{128,192},{160,224},{192,128},{224,1... | collective-permute-start | bytes 393224 | tf_op jit(solution)/shard_map/ppermute | solution.py:227
  18.1 0.8 collective-permute-done.4
  18.9 6.6 %collective-permute-start.6 = (bf16[128,512]{1,0:T(8,128)(2,1)S(1)}, bf16[128,512]{1,0:T(8,128)(2,1)S(1)}, u32[]{:S(2)}, u32[]{:S(2)}) collective-permute-start(bf16[128,512]{1,0:T(8,128)(2,1)S(1)} %slice.17), channel_id=1, source_target_pairs={{0,6},{2,0},{4,2},{6,4},{1,7},{3,1},{5,3},{7,5},{8,14},{10,8},{12,... | collective-permute-start | bytes 393224 | tf_op jit(solution)/shard_map/ppermute | solution.py:206
  26.2 3.5 %collective-permute-done.6 = bf16[128,512]{1,0:T(8,128)(2,1)S(1)} collective-permute-done((bf16[128,512]{1,0:T(8,128)(2,1)S(1)}, bf16[128,512]{1,0:T(8,128)(2,1)S(1)}, u32[]{:S(2)}, u32[]{:S(2)}) %collective-permute-start.6) | collective-permute-done | bytes 131104 | tf_op jit(solution)/shard_map/ppermute | solution.py:206
  29.7 5.6 %collective-permute-done.5 = bf16[128,512]{1,0:T(8,128)(2,1)S(1)} collective-permute-done((bf16[128,512]{1,0:T(8,128)(2,1)S(1)}, bf16[128,512]{1,0:T(8,128)(2,1)S(1)}, u32[]{:S(2)}, u32[]{:S(2)}) %collective-permute-start.5) | collective-permute-done | bytes 131104 | tf_op jit(solution)/shard_map/ppermute | solution.py:206
  35.5 2.6 %collective-permute-start.14 = (bf16[4,256,512]{2,1,0:T(8,128)(2,1)S(1)}, bf16[4,256,512]{2,1,0:T(8,128)(2,1)S(1)}, u32[]{:S(2)}, u32[]{:S(2)}) collective-permute-start(bf16[4,256,512]{2,1,0:T(8,128)(2,1)S(1)} %pad_maximum_fusion.refs_2_), channel_id=1, source_target_pairs={{0,24},{8,0},{16,8},{24,16},{1,25},{9,1},{17,9},{25,17},{2,26},{10... | collective-permute-start | bytes 3145736 | tf_op jit(solution)/shard_map/ppermute | solution.py:206
  38.1 1.7 %deal.2 = (bf16[4,8,512]{2,1,0:T(8,128)(2,1)}, bf16[4,8,512]{2,1,0:T(8,128)(2,1)}, bf16[4,8,512]{2,1,0:T(8,128)(2,1)}, bf16[4,8,512]{2,1,0:T(8,128)(2,1)}) custom-call(s32[1]{0:T(128)} %bitcast.2.at_ref, bf16[4,4,8,512]{3,2,1,0:T(8,128)(2,1)} %bitcast.15, bf16[4,4,8,512]{3,2,1,0:T(8,128)(2,1)} %bitcast.18), custom_call_target="tpu_custom_call" | custom-call | tf_op jit(solution)/shard_map/deal/pallas_call | solution.py:195
  39.9 3.7 %collective-permute-start.8 = (bf16[4,8,512]{2,1,0:T(8,128)(2,1)}, bf16[4,8,512]{2,1,0:T(8,128)(2,1)S(1)}, u32[]{:S(2)}, u32[]{:S(2)}) collective-permute-start(bf16[4,8,512]{2,1,0:T(8,128)(2,1)} %get-tuple-element.29), channel_id=1, source_target_pairs={{0,16},{8,24},{16,0},{24,8},{1,17},{9,25},{17,1},{25,9},{2,18},{10... | collective-permute-start | bytes 98312 | tf_op jit(solution)/shard_map/ppermute | solution.py:206
  43.6 20.5 %collective-permute-done.7.refs_1_ = bf16[4,8,512]{2,1,0:T(8,128)(2,1)S(1)} collective-permute-done((bf16[4,8,512]{2,1,0:T(8,128)(2,1)}, bf16[4,8,512]{2,1,0:T(8,128)(2,1)S(1)}, u32[]{:S(2)}, u32[]{:S(2)}) %collective-permute-start.7) | collective-permute-done | bytes 32800 | tf_op jit(solution)/shard_map/ppermute | solution.py:206
  64.7 1.5 %deal.3 = (bf16[4,8,512]{2,1,0:T(8,128)(2,1)}, bf16[4,8,512]{2,1,0:T(8,128)(2,1)}, bf16[4,8,512]{2,1,0:T(8,128)(2,1)}, bf16[4,8,512]{2,1,0:T(8,128)(2,1)}) custom-call(s32[1]{0:T(128)} %bitcast.1.at_ref, bf16[4,8,512]{2,1,0:T(8,128)(2,1)} %get-tuple-element.27.refs_0_, bf16[4,8,512]{2,1,0:T(8,128)(2,1)} %copy-done.10, bf16[4,8,512]{2,1,0:T(8,128)(2,1)} %copy-done.11, ...), custom_call_target="tpu_custom_call" | custom-call | tf_op jit(solution)/shard_map/deal/pallas_call | solution.py:195
  66.2 3.6 %collective-permute-start.11 = (bf16[4,8,512]{2,1,0:T(8,128)(2,1)}, bf16[4,8,512]{2,1,0:T(8,128)(2,1)S(1)}, u32[]{:S(2)}, u32[]{:S(2)}) collective-permute-start(bf16[4,8,512]{2,1,0:T(8,128)(2,1)} %get-tuple-element.33), channel_id=1, source_target_pairs={{0,6},{2,0},{4,2},{6,4},{1,7},{3,1},{5,3},{7,5},{8,14},{10,8},{12,... | collective-permute-start | bytes 98312 | tf_op jit(solution)/shard_map/ppermute | solution.py:206
  70.2 0.8 constant_dynamic-update-slice_fusion.3
  71.3 5.4 %collective-permute-done.12 = bf16[4,8,512]{2,1,0:T(8,128)(2,1)S(1)} collective-permute-done((bf16[4,8,512]{2,1,0:T(8,128)(2,1)}, bf16[4,8,512]{2,1,0:T(8,128)(2,1)S(1)}, u32[]{:S(2)}, u32[]{:S(2)}) %collective-permute-start.12) | collective-permute-done | bytes 32800 | tf_op jit(solution)/shard_map/ppermute | solution.py:206
  77.4 5.6 %correlate.5.refs_3_ = f32[8,208,256]{2,1,0:T(8,128)} custom-call(s32[1]{0:T(128)} %bitcast.refs_0_, bf16[16,8,512]{2,1,0:T(8,128)(2,1)} %copy-done.1, bf16[4,256,512]{2,1,0:T(8,128)(2,1)} %copy-done), custom_call_target="tpu_custom_call" | custom-call | tf_op jit(solution)/shard_map/correlate/pallas_call | solution.py:165
  83.0 0.9 slice.15
  83.9 0.8 slice.14
  84.7 2.7 %collective-permute-start.15 = (bf16[2,256,512]{2,1,0:T(8,128)(2,1)}, bf16[2,256,512]{2,1,0:T(8,128)(2,1)S(1)}, u32[]{:S(2)}, u32[]{:S(2)}) collective-permute-start(bf16[2,256,512]{2,1,0:T(8,128)(2,1)} %slice.14), channel_id=1, source_target_pairs={{0,24},{8,0},{16,8},{24,16},{1,25},{9,1},{17,9},{25,17},{2,26},{10... | collective-permute-start | bytes 1572872 | tf_op jit(solution)/shard_map/ppermute | solution.py:206
  87.4 6.3 %correlate.6.refs_3_ = f32[8,208,256]{2,1,0:T(8,128)} custom-call(s32[1]{0:T(128)} %bitcast.refs_0_, bf16[16,8,512]{2,1,0:T(8,128)(2,1)} %copy-done.1, bf16[4,256,512]{2,1,0:T(8,128)(2,1)} %copy-done.3, f32[8,208,256]{2,1,0:T(8,128)} %correlate.5.refs_3_), custom_call_target="tpu_custom_call" | custom-call | tf_op jit(solution)/shard_map/correlate/pallas_call | solution.py:165
  93.7 6.3 %correlate.7.refs_3_ = f32[8,208,256]{2,1,0:T(8,128)} custom-call(s32[1]{0:T(128)} %bitcast.refs_0_, bf16[16,8,512]{2,1,0:T(8,128)(2,1)} %copy-done.1, bf16[4,256,512]{2,1,0:T(8,128)(2,1)} %copy-done.2, f32[8,208,256]{2,1,0:T(8,128)} %correlate.6.refs_3_), custom_call_target="tpu_custom_call" | custom-call | tf_op jit(solution)/shard_map/correlate/pallas_call | solution.py:165
  99.9 0.8 copy-done.6
  100.7 4.4 %correlate.8.refs_3_ = f32[8,208,256]{2,1,0:T(8,128)} custom-call(s32[1]{0:T(128)} %bitcast.refs_0_, bf16[16,8,512]{2,1,0:T(8,128)(2,1)} %copy-done.1, bf16[2,256,512]{2,1,0:T(8,128)(2,1)} %copy-done.6, f32[8,208,256]{2,1,0:T(8,128)} %correlate.7.refs_3_), custom_call_target="tpu_custom_call" | custom-call | tf_op jit(solution)/shard_map/correlate/pallas_call | solution.py:165
  105.1 0.8 copy-done.5
  105.9 4.5 %correlate.9 = (f32[4,201,256]{2,1,0:T(8,128)}, f32[4,201,256]{2,1,0:T(8,128)}) custom-call(s32[1]{0:T(128)} %bitcast.refs_0_, bf16[16,8,512]{2,1,0:T(8,128)(2,1)} %copy-done.1, bf16[2,256,512]{2,1,0:T(8,128)(2,1)} %copy-done.5, f32[8,208,256]{2,1,0:T(8,128)} %correlate.8.refs_3_), custom_call_target="tpu_custom_call" | custom-call | tf_op jit(solution)/shard_map/correlate/pallas_call | solution.py:165
  110.5 1.8 %copy.6 = f32[4,201,256]{2,0,1:T(4,128)S(1)} copy(f32[4,201,256]{2,1,0:T(8,128)} %get-tuple-element.40) | data formatting | bytes 1646592 | tf_op jit(solution)/shard_map/correlate/pallas_call | solution.py:165
  112.2 4.5 %collective-permute-start.17 = (f32[4,201,256]{2,0,1:T(4,128)S(1)}, f32[4,201,256]{2,0,1:T(4,128)S(1)}, u32[]{:S(2)}, u32[]{:S(2)}) collective-permute-start(f32[4,201,256]{2,0,1:T(4,128)S(1)} %copy.6), channel_id=1, source_target_pairs={{0,1},{1,0},{2,3},{3,2},{4,5},{5,4},{6,7},{7,6},{8,9},{9,8},{10,11... | collective-permute-start | bytes 2469896 | tf_op jit(solution)/shard_map/ppermute | solution.py:206
  116.8 2.0 %collective-permute-done.17 = f32[4,201,256]{2,0,1:T(4,128)S(1)} collective-permute-done((f32[4,201,256]{2,0,1:T(4,128)S(1)}, f32[4,201,256]{2,0,1:T(4,128)S(1)}, u32[]{:S(2)}, u32[]{:S(2)}) %collective-permute-start.17) | collective-permute-done | bytes 823328 | tf_op jit(solution)/shard_map/ppermute | solution.py:206
  118.9 1.4 %copy.8 = f32[4,201,256]{2,0,1:T(4,128)} copy(f32[4,201,256]{2,1,0:T(8,128)S(1)} %fusion) | data formatting | bytes 1646592 | tf_op jit(solution)/shard_map/mul | solution.py:250
  (53 shorter events, 3.3 us)
Async XLA Ops:
  3.0 32.3 %copy-start.8 = (bf16[256,512]{1,0:T(8,128)(2,1)S(1)}, bf16[256,512]{1,0:T(8,128)(2,1)}, u32[]{:S(2)}) copy-start(bf16[256,512]{1,0:T(8,128)(2,1)} %get-tuple-element.24) | copy-start | bytes 786436
  3.0 15.9 %collective-permute-start.4 = (bf16[256,512]{1,0:T(8,128)(2,1)}, bf16[256,512]{1,0:T(8,128)(2,1)S(1)}, u32[]{:S(2)}, u32[]{:S(2)}) collective-permute-start(bf16[256,512]{1,0:T(8,128)(2,1)} %get-tuple-element.24), channel_id=1, source_target_pairs={{0,6},{2,0},{4,2},{6,4},{1,7},{3,1},{5,3},{7,5},{8,14},{10,8},{12,... | collective-permute-start | bytes 786440 | tf_op jit(solution)/shard_map/ppermute | solution.py:206
  9.9 15.7 %collective-permute-start.3 = (bf16[256,512]{1,0:T(8,128)(2,1)}, bf16[256,512]{1,0:T(8,128)(2,1)S(1)}, u32[]{:S(2)}, u32[]{:S(2)}) collective-permute-start(bf16[256,512]{1,0:T(8,128)(2,1)} %get-tuple-element.24), channel_id=1, source_target_pairs={{0,2},{2,4},{4,6},{6,0},{1,3},{3,5},{5,7},{7,1},{8,10},{10,12},{12... | collective-permute-start | bytes 786440 | tf_op jit(solution)/shard_map/ppermute | solution.py:206
  9.9 4.3 %collective-permute-start = (bf16[128,512]{1,0:T(8,128)(2,1)}, bf16[128,512]{1,0:T(8,128)(2,1)S(1)}, u32[]{:S(2)}, u32[]{:S(2)}) collective-permute-start(bf16[128,512]{1,0:T(8,128)(2,1)} %get-tuple-element.23), channel_id=1, source_target_pairs={{0,32},{32,0},{64,96},{96,64},{128,160},{160,128},{192,224},{224,1... | collective-permute-start | bytes 393224 | tf_op jit(solution)/shard_map/ppermute | solution.py:227
  15.1 10.5 %collective-permute-start.1 = (bf16[128,512]{1,0:T(8,128)(2,1)S(1)}, bf16[128,512]{1,0:T(8,128)(2,1)S(1)}, u32[]{:S(2)}, u32[]{:S(2)}) collective-permute-start(bf16[128,512]{1,0:T(8,128)(2,1)S(1)} %add.9), channel_id=1, source_target_pairs={{0,64},{32,96},{64,0},{96,32},{128,192},{160,224},{192,128},{224,1... | collective-permute-start | bytes 393224 | tf_op jit(solution)/shard_map/ppermute | solution.py:227
  18.9 10.8 %collective-permute-start.6 = (bf16[128,512]{1,0:T(8,128)(2,1)S(1)}, bf16[128,512]{1,0:T(8,128)(2,1)S(1)}, u32[]{:S(2)}, u32[]{:S(2)}) collective-permute-start(bf16[128,512]{1,0:T(8,128)(2,1)S(1)} %slice.17), channel_id=1, source_target_pairs={{0,6},{2,0},{4,2},{6,4},{1,7},{3,1},{5,3},{7,5},{8,14},{10,8},{12,... | collective-permute-start | bytes 393224 | tf_op jit(solution)/shard_map/ppermute | solution.py:206
  25.6 9.8 %collective-permute-start.5 = (bf16[128,512]{1,0:T(8,128)(2,1)S(1)}, bf16[128,512]{1,0:T(8,128)(2,1)S(1)}, u32[]{:S(2)}, u32[]{:S(2)}) collective-permute-start(bf16[128,512]{1,0:T(8,128)(2,1)S(1)} %slice.16), channel_id=1, source_target_pairs={{0,2},{2,4},{4,6},{6,0},{1,3},{3,5},{5,7},{7,1},{8,10},{10,12},{12... | collective-permute-start | bytes 393224 | tf_op jit(solution)/shard_map/ppermute | solution.py:206
  25.7 12.4 %copy-start.7 = (bf16[128,512]{1,0:T(8,128)(2,1)}, bf16[128,512]{1,0:T(8,128)(2,1)S(1)}, u32[]{:S(2)}) copy-start(bf16[128,512]{1,0:T(8,128)(2,1)S(1)} %add.10) | copy-start | bytes 393220
  25.7 9.8 %collective-permute-start.2 = (bf16[128,512]{1,0:T(8,128)(2,1)S(1)}, bf16[128,512]{1,0:T(8,128)(2,1)S(1)}, u32[]{:S(2)}, u32[]{:S(2)}) collective-permute-start(bf16[128,512]{1,0:T(8,128)(2,1)S(1)} %add.10), channel_id=1, source_target_pairs={{0,128},{32,160},{64,192},{96,224},{128,0},{160,32},{192,64},{224,... | collective-permute-start | bytes 393224 | tf_op jit(solution)/shard_map/ppermute | solution.py:229
  35.5 41.2 %copy-start = (bf16[4,256,512]{2,1,0:T(8,128)(2,1)}, bf16[4,256,512]{2,1,0:T(8,128)(2,1)S(1)}, u32[]{:S(2)}) copy-start(bf16[4,256,512]{2,1,0:T(8,128)(2,1)S(1)} %pad_maximum_fusion.refs_2_) | copy-start | bytes 3145732
  35.5 2.6 %copy-start.9 = (bf16[128,512]{1,0:T(8,128)(2,1)}, bf16[128,512]{1,0:T(8,128)(2,1)S(1)}, u32[]{:S(2)}) copy-start(bf16[128,512]{1,0:T(8,128)(2,1)S(1)} %collective-permute-done.2) | copy-start | bytes 393220
  35.5 47.4 %collective-permute-start.14 = (bf16[4,256,512]{2,1,0:T(8,128)(2,1)S(1)}, bf16[4,256,512]{2,1,0:T(8,128)(2,1)S(1)}, u32[]{:S(2)}, u32[]{:S(2)}) collective-permute-start(bf16[4,256,512]{2,1,0:T(8,128)(2,1)S(1)} %pad_maximum_fusion.refs_2_), channel_id=1, source_target_pairs={{0,24},{8,0},{16,8},{24,16},{1,25},{9,1},{17,9},{25,17},{2,26},{10... | collective-permute-start | bytes 3145736 | tf_op jit(solution)/shard_map/ppermute | solution.py:206
  38.1 44.9 %collective-permute-start.13 = (bf16[4,256,512]{2,1,0:T(8,128)(2,1)S(1)}, bf16[4,256,512]{2,1,0:T(8,128)(2,1)S(1)}, u32[]{:S(2)}, u32[]{:S(2)}) collective-permute-start(bf16[4,256,512]{2,1,0:T(8,128)(2,1)S(1)} %pad_maximum_fusion.refs_2_), channel_id=1, source_target_pairs={{0,8},{8,16},{16,24},{24,0},{1,9},{9,17},{17,25},{25,1},{2,10},{10... | collective-permute-start | bytes 3145736 | tf_op jit(solution)/shard_map/ppermute | solution.py:206
  39.8 24.3 %collective-permute-start.7 = (bf16[4,8,512]{2,1,0:T(8,128)(2,1)}, bf16[4,8,512]{2,1,0:T(8,128)(2,1)S(1)}, u32[]{:S(2)}, u32[]{:S(2)}) collective-permute-start(bf16[4,8,512]{2,1,0:T(8,128)(2,1)} %get-tuple-element.28), channel_id=1, source_target_pairs={{0,8},{8,16},{16,24},{24,0},{1,9},{9,17},{17,25},{25,1},{2,10},{10... | collective-permute-start | bytes 98312 | tf_op jit(solution)/shard_map/ppermute | solution.py:206
  39.9 24.1 %collective-permute-start.8 = (bf16[4,8,512]{2,1,0:T(8,128)(2,1)}, bf16[4,8,512]{2,1,0:T(8,128)(2,1)S(1)}, u32[]{:S(2)}, u32[]{:S(2)}) collective-permute-start(bf16[4,8,512]{2,1,0:T(8,128)(2,1)} %get-tuple-element.29), channel_id=1, source_target_pairs={{0,16},{8,24},{16,0},{24,8},{1,17},{9,25},{17,1},{25,9},{2,18},{10... | collective-permute-start | bytes 98312 | tf_op jit(solution)/shard_map/ppermute | solution.py:206
  43.6 20.5 %collective-permute-start.9 = (bf16[4,8,512]{2,1,0:T(8,128)(2,1)}, bf16[4,8,512]{2,1,0:T(8,128)(2,1)S(1)}, u32[]{:S(2)}, u32[]{:S(2)}) collective-permute-start(bf16[4,8,512]{2,1,0:T(8,128)(2,1)} %get-tuple-element.30), channel_id=1, source_target_pairs={{0,24},{8,0},{16,8},{24,16},{1,25},{9,1},{17,9},{25,17},{2,26},{10... | collective-permute-start | bytes 98312 | tf_op jit(solution)/shard_map/ppermute | solution.py:206
  64.1 0.6 copy-start.10
  64.1 0.6 copy-start.11
  64.1 0.6 copy-start.12
  66.2 5.1 %collective-permute-start.10 = (bf16[4,8,512]{2,1,0:T(8,128)(2,1)}, bf16[4,8,512]{2,1,0:T(8,128)(2,1)S(1)}, u32[]{:S(2)}, u32[]{:S(2)}) collective-permute-start(bf16[4,8,512]{2,1,0:T(8,128)(2,1)} %get-tuple-element.32), channel_id=1, source_target_pairs={{0,2},{2,4},{4,6},{6,0},{1,3},{3,5},{5,7},{7,1},{8,10},{10,12},{12... | collective-permute-start | bytes 98312 | tf_op jit(solution)/shard_map/ppermute | solution.py:206
  66.2 5.1 %collective-permute-start.11 = (bf16[4,8,512]{2,1,0:T(8,128)(2,1)}, bf16[4,8,512]{2,1,0:T(8,128)(2,1)S(1)}, u32[]{:S(2)}, u32[]{:S(2)}) collective-permute-start(bf16[4,8,512]{2,1,0:T(8,128)(2,1)} %get-tuple-element.33), channel_id=1, source_target_pairs={{0,6},{2,0},{4,2},{6,4},{1,7},{3,1},{5,3},{7,5},{8,14},{10,8},{12,... | collective-permute-start | bytes 98312 | tf_op jit(solution)/shard_map/ppermute | solution.py:206
  69.8 6.9 %collective-permute-start.12 = (bf16[4,8,512]{2,1,0:T(8,128)(2,1)}, bf16[4,8,512]{2,1,0:T(8,128)(2,1)S(1)}, u32[]{:S(2)}, u32[]{:S(2)}) collective-permute-start(bf16[4,8,512]{2,1,0:T(8,128)(2,1)} %get-tuple-element.34), channel_id=1, source_target_pairs={{0,4},{2,6},{4,0},{6,2},{1,5},{3,7},{5,1},{7,3},{8,12},{10,14},{12... | collective-permute-start | bytes 98312 | tf_op jit(solution)/shard_map/ppermute | solution.py:206
  76.7 0.6 copy-start.1
  83.0 10.7 %copy-start.2 = (bf16[4,256,512]{2,1,0:T(8,128)(2,1)}, bf16[4,256,512]{2,1,0:T(8,128)(2,1)S(1)}, u32[]{:S(2)}) copy-start(bf16[4,256,512]{2,1,0:T(8,128)(2,1)S(1)} %collective-permute-done.14.refs_2_) | copy-start | bytes 3145732
  83.0 4.4 %copy-start.3 = (bf16[4,256,512]{2,1,0:T(8,128)(2,1)}, bf16[4,256,512]{2,1,0:T(8,128)(2,1)S(1)}, u32[]{:S(2)}) copy-start(bf16[4,256,512]{2,1,0:T(8,128)(2,1)S(1)} %collective-permute-done.13.refs_2_) | copy-start | bytes 3145732
  83.9 16.1 %collective-permute-start.16 = (bf16[2,256,512]{2,1,0:T(8,128)(2,1)}, bf16[2,256,512]{2,1,0:T(8,128)(2,1)S(1)}, u32[]{:S(2)}, u32[]{:S(2)}) collective-permute-start(bf16[2,256,512]{2,1,0:T(8,128)(2,1)} %slice.15), channel_id=1, source_target_pairs={{0,8},{8,16},{16,24},{24,0},{1,9},{9,17},{17,25},{25,1},{2,10},{10... | collective-permute-start | bytes 1572872 | tf_op jit(solution)/shard_map/ppermute | solution.py:206
  84.7 20.4 %collective-permute-start.15 = (bf16[2,256,512]{2,1,0:T(8,128)(2,1)}, bf16[2,256,512]{2,1,0:T(8,128)(2,1)S(1)}, u32[]{:S(2)}, u32[]{:S(2)}) collective-permute-start(bf16[2,256,512]{2,1,0:T(8,128)(2,1)} %slice.14), channel_id=1, source_target_pairs={{0,24},{8,0},{16,8},{24,16},{1,25},{9,1},{17,9},{25,17},{2,26},{10... | collective-permute-start | bytes 1572872 | tf_op jit(solution)/shard_map/ppermute | solution.py:206
  99.9 0.8 copy-start.6
  105.1 0.8 copy-start.5
  110.5 8.2 %copy-start.4 = (f32[4,201,256]{2,1,0:T(8,128)S(1)}, f32[4,201,256]{2,1,0:T(8,128)}, u32[]{:S(2)}) copy-start(f32[4,201,256]{2,1,0:T(8,128)} %get-tuple-element.39) | copy-start | bytes 2469892
  112.2 6.5 %collective-permute-start.17 = (f32[4,201,256]{2,0,1:T(4,128)S(1)}, f32[4,201,256]{2,0,1:T(4,128)S(1)}, u32[]{:S(2)}, u32[]{:S(2)}) collective-permute-start(f32[4,201,256]{2,0,1:T(4,128)S(1)} %copy.6), channel_id=1, source_target_pairs={{0,1},{1,0},{2,3},{3,2},{4,5},{5,4},{6,7},{7,6},{8,9},{9,8},{10,11... | collective-permute-start | bytes 2469896 | tf_op jit(solution)/shard_map/ppermute | solution.py:206

commit v3 on v2

--- a/solution.py
+++ b/solution.py
@@ -17,6 +17,7 @@
 NLAG = 2 * MAXLAG + 1
 LAGPAD = 208
 SRC_PAIR = 8
+PAIR = 2
 
 
 def split_terms(x):
@@ -107,8 +108,8 @@
 
 def correlate_body(has_prev, is_last, *refs):
     refs = list(refs)
-    core_ref, src_ref, recv_ref = refs[:3]
-    refs = refs[3:]
+    core_ref, src_ref, early_ref, late_ref = refs[:4]
+    refs = refs[4:]
     prev_ref = refs.pop(0) if has_prev else None
     if is_last:
         mine_ref, other_ref, acc_ref, first_ref, second_ref = refs
@@ -121,7 +122,7 @@
         acc_ref[...] = prev_ref[...] if has_prev else jnp.zeros(acc_ref.shape, jnp.float32)
 
     rows = src_ref[0].astype(jnp.float32)
-    receivers = recv_ref[0]
+    receivers = jnp.where(window < PAIR, early_ref[0], late_ref[0])
     half = SRC_PAIR // 2
     for number, lagged_ref in enumerate((first_ref, second_ref)):
         fill_lagged(rows, number * half, lagged_ref)
@@ -137,16 +138,23 @@
             other_ref[...] = acc_ref[pl.ds((1 - core) * half, half), :NLAG, :]
 
 
-def correlate(sources, receivers, off_x, base, prev, core, is_last):
-    windows, local_width = receivers.shape[0], receivers.shape[1]
+def correlate(sources, early, late, prev, core, is_last):
+    (early_x, early_z, early), (late_x, late_z, late) = early, late
+    local_width = early.shape[1]
     acc_shape = (SRC_PAIR, LAGPAD, local_width)
     whole = lambda shape: pl.BlockSpec(shape, lambda w, core: (0,) * len(shape))
     half_shape = (SRC_PAIR // 2, NLAG, local_width)
+
+    def source_at(w, core):
+        at_early, at_late = 4 * (early_z + w) + early_x, 4 * (late_z + w - PAIR) + late_x
+        return jnp.where(w < PAIR, at_early, at_late), 0, 0
+
     in_specs = [
-        pl.BlockSpec((1, SRC_PAIR, SAMP), lambda w, core: (4 * (base + w) + off_x, 0, 0)),
-        pl.BlockSpec((1, local_width, SAMP), lambda w, core: (w, 0, 0)),
+        pl.BlockSpec((1, SRC_PAIR, SAMP), source_at),
+        pl.BlockSpec((1, local_width, SAMP), lambda w, core: (jnp.minimum(w, PAIR - 1), 0, 0)),
+        pl.BlockSpec((1, local_width, SAMP), lambda w, core: (jnp.maximum(w - PAIR, 0), 0, 0)),
     ]
-    operands = [sources, receivers]
+    operands = [sources, early, late]
     if prev is not None:
         in_specs.append(whole(acc_shape))
         operands.append(prev)
@@ -166,7 +174,7 @@
         body,
         grid_spec=pltpu.PrefetchScalarGridSpec(
             num_scalar_prefetch=1,
-            grid=(windows,),
+            grid=(2 * PAIR,),
             in_specs=in_specs,
             out_specs=out_specs,
             scratch_shapes=scratch,
@@ -206,14 +214,6 @@
     return lax.ppermute(value, axis, [(i, (i + by) % size) for i in range(size)])
 
 
-def along_z(own):
-    below, above = shifted(own, "z_hi", 1), shifted(own, "z_hi", -1)
-    half = own.shape[0] // 2
-    low = shifted(below[:half], "z_hi", 1)
-    high = shifted(above[half:], "z_hi", -1)
-    return jnp.stack([own, below, above, jnp.concatenate([low, high], axis=0)])
-
-
 def shards(raw_traces, fir_taps, source_blocks, valid_counts):
     chan = lax.axis_index("chan").astype(jnp.int32)
     core = lax.axis_index("core").astype(jnp.int32).reshape(1)
@@ -221,29 +221,39 @@
     at_z = lax.axis_index("z_hi").astype(jnp.int32)
     chans, size_x, size_z = lax.axis_size("chan"), lax.axis_size("x"), lax.axis_size("z_hi")
     own, mine = prep(raw_traces[0], fir_taps, source_blocks, valid_counts, chan.reshape(1))
-    bundle = along_z(own)
-    step = 1
-    while step < chans // 2:
-        mine = mine + lax.ppermute(mine, "chan", [(i, i ^ step) for i in range(chans)])
-        step *= 2
-    theirs = lax.ppermute(mine, "chan", [(i, i ^ step) for i in range(chans)])
-    mine, theirs, bundle = lax.optimization_barrier((mine, theirs, bundle))
-    before, after = shifted(bundle, "x", 1), shifted(bundle, "x", -1)
+    below, above = shifted(own, "z_hi", 1), shifted(own, "z_hi", -1)
+    half = own.shape[0] // 2
+    opposite = [shifted(below[:half], "z_hi", 1), shifted(above[half:], "z_hi", -1)]
+
+    def swap(value, step):
+        return lax.ppermute(value, "chan", [(i, i ^ step) for i in range(chans)])
+
+    step = chans // 2
+    mine = mine + swap(mine, step)
+    while step > 2:
+        step //= 2
+        mine = mine + swap(mine, step)
     grouped = (size_x, size_z, SRC_PAIR, SAMP)
-    parts = [v.reshape(grouped) for v in (mine, theirs)]
+    parts = [v.reshape(grouped) for v in (mine, swap(mine, step // 2))]
     dealt = deal(at_x.reshape(1), parts)
     dealt = [dealt[0]] + [shifted(dealt[by], "x", by) for by in range(1, 4)]
+    low = jnp.stack([own, below])
+    dealt, low = lax.optimization_barrier((dealt, low))
+    before_low, after_low = shifted(low, "x", 1), shifted(low, "x", -1)
+    high = jnp.stack([above, jnp.concatenate(opposite, axis=0)])
     dealt = deal(at_z.reshape(1), dealt)
     dealt = [dealt[0]] + [shifted(dealt[by], "z_hi", by) for by in range(1, 4)]
+    dealt, high = lax.optimization_barrier((dealt, high))
+    before_high, after_high = shifted(high, "x", 1), shifted(high, "x", -1)
     sources = jnp.concatenate([dealt[0], dealt[1], dealt[3], dealt[2]], axis=0)
-    total = correlate(sources, bundle, 0, 0, None, core, False)
-    total, before, after = lax.optimization_barrier((total, before, after))
-    half = bundle.shape[0] // 2
-    low, high = shifted(before[:half], "x", 1), shifted(after[half:], "x", -1)
-    total = correlate(sources, before, 1, 0, total, core, False)
-    total = correlate(sources, after, 3, 0, total, core, False)
-    total = correlate(sources, low, 2, 0, total, core, False)
-    total = correlate(sources, high, 2, half, total, core, True)
+    total = correlate(sources, (0, 0, low), (0, 2, high), None, core, False)
+    total, before_low, after_low = lax.optimization_barrier((total, before_low, after_low))
+    far_low = shifted(before_low, "x", 1)
+    total = correlate(sources, (1, 0, before_low), (3, 0, after_low), total, core, False)
+    total, before_high, after_high = lax.optimization_barrier((total, before_high, after_high))
+    far_high = shifted(after_high, "x", -1)
+    total = correlate(sources, (1, 2, before_high), (3, 2, after_high), total, core, False)
+    total = correlate(sources, (2, 0, far_low), (2, 2, far_high), total, core, True)
     kept, passed = total
     got = shifted(passed, "core", 1)
     factor = 1.0 / math.sqrt(SAMP * size_x * size_z * 2)

time: 121 us -> 101 us (0.83)
  waiting for transfers between devices: 41 us -> 15.5 us
  starting transfers between devices: 36 us -> 43.9 us
  Pallas kernels: 33.2 us -> 31.1 us
    ppermute x15 -> x17, waiting for transfers between devices: 38 us -> 13.1 us  [shifted(): lax.ppermute(value, axis, [(i, (i + by) % size) for i in range(size)])]
    ppermute x15 -> x17, starting transfers between devices: 31.2 us -> 36.7 us  [shifted(): lax.ppermute(value, axis, [(i, (i + by) % size) for i in range(size)])]
    ppermute x3, starting transfers between devices: 4.83 us -> 7.15 us  [swap(): return lax.ppermute(value, 'chan', [(i, i ^ step) for i in range(chans)])]
    pallas_call x5 -> x4, Pallas kernels: 27.1 us -> 25 us  [correlate(): pl.pallas_call(body, grid_spec=pltpu.PrefetchScalarGridSpec(num_scalar_pr...]
    slice x4 -> x2, local copies, waits for them, and re-layouts: 1.74 us -> 0.02 us  [the longest x1 0.01 us: shards(): above[half:]]
    unnamed x29 -> x33, local copies, waits for them, and re-layouts: 3.63 us -> 4.39 us
  transfers between devices with their start and end apart: 18 -> 20, of which waited for: 8 -> 7; matrix products, arithmetic and copies ran while one was open for 2% -> 3% of each run, Pallas kernels for 21% -> 20%
where the time goes in v3:
time: 101 us
  starting transfers between devices  43.9 us (43%)
  Pallas kernels  31.1 us (31%)
  waiting for transfers between devices  15.5 us (15%)
  local copies, waits for them, and re-layouts  7.6 us (8%)
  other arithmetic  2.25 us (2%)
    ppermute x17, starting transfers between devices, shifted(): lax.ppermute(value, axis, [(i, (i + by) % size) for i in range(size)])  36.7 us
    pallas_call x4, Pallas kernels, correlate(): pl.pallas_call(body, grid_spec=pltpu.PrefetchScalarGridSpec(num_scalar_pr...  25 us
    ppermute x17, waiting for transfers between devices, shifted(): lax.ppermute(value, axis, [(i, (i + by) % size) for i in range(size)])  13.1 us
    ppermute x3, starting transfers between devices, swap(): return lax.ppermute(value, 'chan', [(i, i ^ step) for i in range(chans)])  7.15 us
    unnamed x33, local copies, waits for them, and re-layouts  4.39 us
    pallas_call x2, Pallas kernels, deal(): pl.pallas_call(deal_body, in_specs=[smem] + [vmem] * len(arrays), out_spe...  3.1 us
    pallas_call x1, Pallas kernels, prep(): pl.pallas_call(prep_body, in_specs=[smem, smem, vmem, vmem, vmem], out_sp...  3 us
    ppermute x3, waiting for transfers between devices, swap(): return lax.ppermute(value, 'chan', [(i, i ^ step) for i in range(chans)])  2.41 us
  transfers between devices with their start and end apart: 20, of which 7 were waited for; matrix products, arithmetic and copies ran while one was open for 3% of the time, Pallas kernels for 20%

profile of v3, /device:TPU:1, one launch (start us, length us, event | category | flops | bytes accessed | tf_op | source)
XLA Modules:
  0.0 100.5 jit_solution(6002618820140295507)
XLA Ops:
  0.0 3.0 %prep.1 = (bf16[256,512]{1,0:T(8,128)(2,1)}, bf16[128,512]{1,0:T(8,128)(2,1)}) custom-call(s32[2]{0:T(128)} %blocks_ref.1, s32[1]{0:T(128)} %bitcast.3.chan_ref, bf16[256,512]{1,0:T(8,128)(2,1)} %bitcast.16, f32[1,65]{1,0:T(1,128)} %bitcast.19, s32[1,256]{1,0:T(1,128)} %counts_ref.1), custom_call_target="tpu_custom_call" | custom-call | tf_op jit(solution)/shard_map/prep/pallas_call | solution.py:83
  3.0 2.5 %collective-permute-start = (bf16[128,512]{1,0:T(8,128)(2,1)}, bf16[128,512]{1,0:T(8,128)(2,1)S(1)}, u32[]{:S(2)}, u32[]{:S(2)}) collective-permute-start(bf16[128,512]{1,0:T(8,128)(2,1)} %get-tuple-element.33), channel_id=1, source_target_pairs={{0,128},{32,160},{64,192},{96,224},{128,0},{160,32},{192,64},{224,... | collective-permute-start | bytes 393224 | tf_op jit(solution)/shard_map/ppermute | solution.py:229
  5.5 3.0 %collective-permute-start.6 = (bf16[256,512]{1,0:T(8,128)(2,1)}, bf16[256,512]{1,0:T(8,128)(2,1)S(1)}, u32[]{:S(2)}, u32[]{:S(2)}) collective-permute-start(bf16[256,512]{1,0:T(8,128)(2,1)} %get-tuple-element.38), channel_id=1, source_target_pairs={{0,2},{2,4},{4,6},{6,0},{1,3},{3,5},{5,7},{7,1},{8,10},{10,12},{12... | collective-permute-start | bytes 786440 | tf_op jit(solution)/shard_map/ppermute | solution.py:214
  8.5 2.1 %collective-permute-start.10 = (bf16[256,512]{1,0:T(8,128)(2,1)}, bf16[256,512]{1,0:T(8,128)(2,1)S(1)}, u32[]{:S(2)}, u32[]{:S(2)}) collective-permute-start(bf16[256,512]{1,0:T(8,128)(2,1)} %get-tuple-element.38), channel_id=1, source_target_pairs={{0,6},{2,0},{4,2},{6,4},{1,7},{3,1},{5,3},{7,5},{8,14},{10,8},{12,... | collective-permute-start | bytes 786440 | tf_op jit(solution)/shard_map/ppermute | solution.py:214
  10.6 0.9 add.9
  11.5 3.0 %collective-permute-start.1 = (bf16[128,512]{1,0:T(8,128)(2,1)S(1)}, bf16[128,512]{1,0:T(8,128)(2,1)S(1)}, u32[]{:S(2)}, u32[]{:S(2)}) collective-permute-start(bf16[128,512]{1,0:T(8,128)(2,1)S(1)} %add.9), channel_id=1, source_target_pairs={{0,64},{32,96},{64,0},{96,32},{128,192},{160,224},{192,128},{224,1... | collective-permute-start | bytes 393224 | tf_op jit(solution)/shard_map/ppermute | solution.py:229
  14.5 2.4 %collective-permute-done.1 = bf16[128,512]{1,0:T(8,128)(2,1)S(1)} collective-permute-done((bf16[128,512]{1,0:T(8,128)(2,1)S(1)}, bf16[128,512]{1,0:T(8,128)(2,1)S(1)}, u32[]{:S(2)}, u32[]{:S(2)}) %collective-permute-start.1) | collective-permute-done | bytes 131104 | tf_op jit(solution)/shard_map/ppermute | solution.py:229
  17.0 1.7 %collective-permute-start.2 = (bf16[128,512]{1,0:T(8,128)(2,1)S(1)}, bf16[128,512]{1,0:T(8,128)(2,1)S(1)}, u32[]{:S(2)}, u32[]{:S(2)}) collective-permute-start(bf16[128,512]{1,0:T(8,128)(2,1)S(1)} %add.10), channel_id=1, source_target_pairs={{0,32},{32,0},{64,96},{96,64},{128,160},{160,128},{192,224},{224,1... | collective-permute-start | bytes 393224 | tf_op jit(solution)/shard_map/ppermute | solution.py:229
  18.7 6.3 %collective-permute-done.6 = bf16[256,512]{1,0:T(8,128)(2,1)S(1)} collective-permute-done((bf16[256,512]{1,0:T(8,128)(2,1)}, bf16[256,512]{1,0:T(8,128)(2,1)S(1)}, u32[]{:S(2)}, u32[]{:S(2)}) %collective-permute-start.6) | collective-permute-done | bytes 262176 | tf_op jit(solution)/shard_map/ppermute | solution.py:214
  25.1 3.6 %collective-permute-start.12 = (bf16[128,512]{1,0:T(8,128)(2,1)S(1)}, bf16[128,512]{1,0:T(8,128)(2,1)S(1)}, u32[]{:S(2)}, u32[]{:S(2)}) collective-permute-start(bf16[128,512]{1,0:T(8,128)(2,1)S(1)} %slice.9), channel_id=1, source_target_pairs={{0,6},{2,0},{4,2},{6,4},{1,7},{3,1},{5,3},{7,5},{8,14},{10,8},{12,... | collective-permute-start | bytes 393224 | tf_op jit(solution)/shard_map/ppermute | solution.py:214
  28.7 1.0 pad_maximum_fusion.refs_2_
  30.4 1.6 %deal.2 = (bf16[4,8,512]{2,1,0:T(8,128)(2,1)}, bf16[4,8,512]{2,1,0:T(8,128)(2,1)}, bf16[4,8,512]{2,1,0:T(8,128)(2,1)}, bf16[4,8,512]{2,1,0:T(8,128)(2,1)}) custom-call(s32[1]{0:T(128)} %bitcast.2.at_ref, bf16[4,4,8,512]{3,2,1,0:T(8,128)(2,1)} %bitcast.15, bf16[4,4,8,512]{3,2,1,0:T(8,128)(2,1)} %bitcast.18), custom_call_target="tpu_custom_call" | custom-call | tf_op jit(solution)/shard_map/deal/pallas_call | solution.py:203
  32.1 1.2 %collective-permute-start.3 = (bf16[4,8,512]{2,1,0:T(8,128)(2,1)}, bf16[4,8,512]{2,1,0:T(8,128)(2,1)S(1)}, u32[]{:S(2)}, u32[]{:S(2)}) collective-permute-start(bf16[4,8,512]{2,1,0:T(8,128)(2,1)} %get-tuple-element.35), channel_id=1, source_target_pairs={{0,8},{8,16},{16,24},{24,0},{1,9},{9,17},{17,25},{25,1},{2,10},{10... | collective-permute-start | bytes 98312 | tf_op jit(solution)/shard_map/ppermute | solution.py:214
  33.3 2.4 %collective-permute-start.4 = (bf16[4,8,512]{2,1,0:T(8,128)(2,1)}, bf16[4,8,512]{2,1,0:T(8,128)(2,1)S(1)}, u32[]{:S(2)}, u32[]{:S(2)}) collective-permute-start(bf16[4,8,512]{2,1,0:T(8,128)(2,1)} %get-tuple-element.36), channel_id=1, source_target_pairs={{0,16},{8,24},{16,0},{24,8},{1,17},{9,25},{17,1},{25,9},{2,18},{10... | collective-permute-start | bytes 98312 | tf_op jit(solution)/shard_map/ppermute | solution.py:214
  35.7 1.2 %collective-permute-start.5 = (bf16[4,8,512]{2,1,0:T(8,128)(2,1)}, bf16[4,8,512]{2,1,0:T(8,128)(2,1)S(1)}, u32[]{:S(2)}, u32[]{:S(2)}) collective-permute-start(bf16[4,8,512]{2,1,0:T(8,128)(2,1)} %get-tuple-element.37), channel_id=1, source_target_pairs={{0,24},{8,0},{16,8},{24,16},{1,25},{9,1},{17,9},{25,17},{2,26},{10... | collective-permute-start | bytes 98312 | tf_op jit(solution)/shard_map/ppermute | solution.py:214
  36.9 0.8 collective-permute-done.4.refs_2_
  37.8 1.2 %collective-permute-done.5.refs_3_ = bf16[4,8,512]{2,1,0:T(8,128)(2,1)S(1)} collective-permute-done((bf16[4,8,512]{2,1,0:T(8,128)(2,1)}, bf16[4,8,512]{2,1,0:T(8,128)(2,1)S(1)}, u32[]{:S(2)}, u32[]{:S(2)}) %collective-permute-start.5) | collective-permute-done | bytes 32800 | tf_op jit(solution)/shard_map/ppermute | solution.py:214
  39.6 1.5 %deal.3 = (bf16[4,8,512]{2,1,0:T(8,128)(2,1)}, bf16[4,8,512]{2,1,0:T(8,128)(2,1)}, bf16[4,8,512]{2,1,0:T(8,128)(2,1)}, bf16[4,8,512]{2,1,0:T(8,128)(2,1)}) custom-call(s32[1]{0:T(128)} %bitcast.1.at_ref, bf16[4,8,512]{2,1,0:T(8,128)(2,1)} %get-tuple-element.39.refs_0_, bf16[4,8,512]{2,1,0:T(8,128)(2,1)} %copy-done.12, bf16[4,8,512]{2,1,0:T(8,128)(2,1)} %copy-done.13, ...), custom_call_target="tpu_custom_call" | custom-call | tf_op jit(solution)/shard_map/deal/pallas_call | solution.py:203
  41.1 1.8 %collective-permute-start.8 = (bf16[4,8,512]{2,1,0:T(8,128)(2,1)}, bf16[4,8,512]{2,1,0:T(8,128)(2,1)S(1)}, u32[]{:S(2)}, u32[]{:S(2)}) collective-permute-start(bf16[4,8,512]{2,1,0:T(8,128)(2,1)} %get-tuple-element.45), channel_id=1, source_target_pairs={{0,4},{2,6},{4,0},{6,2},{1,5},{3,7},{5,1},{7,3},{8,12},{10,14},{12... | collective-permute-start | bytes 98312 | tf_op jit(solution)/shard_map/ppermute | solution.py:214
  42.9 3.1 %collective-permute-start.9 = (bf16[4,8,512]{2,1,0:T(8,128)(2,1)}, bf16[4,8,512]{2,1,0:T(8,128)(2,1)S(1)}, u32[]{:S(2)}, u32[]{:S(2)}) collective-permute-start(bf16[4,8,512]{2,1,0:T(8,128)(2,1)} %get-tuple-element.46), channel_id=1, source_target_pairs={{0,6},{2,0},{4,2},{6,4},{1,7},{3,1},{5,3},{7,5},{8,14},{10,8},{12,... | collective-permute-start | bytes 98312 | tf_op jit(solution)/shard_map/ppermute | solution.py:214
  46.4 2.4 %collective-permute-start.14 = (bf16[2,256,512]{2,1,0:T(8,128)(2,1)S(1)}, bf16[2,256,512]{2,1,0:T(8,128)(2,1)S(1)}, u32[]{:S(2)}, u32[]{:S(2)}) collective-permute-start(bf16[2,256,512]{2,1,0:T(8,128)(2,1)S(1)} %pad_maximum_fusion.refs_2_), channel_id=1, source_target_pairs={{0,24},{8,0},{16,8},{24,16},{1,25},{9,1},{17,9},{25,17},{2,26},{10... | collective-permute-start | bytes 1572872 | tf_op jit(solution)/shard_map/ppermute | solution.py:214
  49.1 2.7 %collective-permute-start.17 = (bf16[2,256,512]{2,1,0:T(8,128)(2,1)S(1)}, bf16[2,256,512]{2,1,0:T(8,128)(2,1)S(1)}, u32[]{:S(2)}, u32[]{:S(2)}) collective-permute-start(bf16[2,256,512]{2,1,0:T(8,128)(2,1)S(1)} %pad_maximum_fusion.1.refs_3_), channel_id=1, source_target_pairs={{0,24},{8,0},{16,8},{24,16},{1,25},{9,1},{17,9},{25,17},{2,26},{10... | collective-permute-start | bytes 1572872 | tf_op jit(solution)/shard_map/ppermute | solution.py:214
  53.2 5.7 %correlate.4.refs_4_ = f32[8,208,256]{2,1,0:T(8,128)} custom-call(s32[1]{0:T(128)} %bitcast.refs_0_, bf16[16,8,512]{2,1,0:T(8,128)(2,1)} %copy-done, bf16[2,256,512]{2,1,0:T(8,128)(2,1)} %copy-done.1, bf16[2,256,512]{2,1,0:T(8,128)(2,1)} %copy-done.2), custom_call_target="tpu_custom_call" | custom-call | tf_op jit(solution)/shard_map/correlate/pallas_call | solution.py:173
  59.9 6.4 %correlate.5.refs_4_ = f32[8,208,256]{2,1,0:T(8,128)} custom-call(s32[1]{0:T(128)} %bitcast.refs_0_, bf16[16,8,512]{2,1,0:T(8,128)(2,1)} %copy-done, bf16[2,256,512]{2,1,0:T(8,128)(2,1)} %copy-done.4, bf16[2,256,512]{2,1,0:T(8,128)(2,1)} %copy-done.5, f32[8,208,256]{2,1,0:T(8,128)} %correlate.4.refs_4_), custom_call_target="tpu_custom_call" | custom-call | tf_op jit(solution)/shard_map/correlate/pallas_call | solution.py:173
  66.3 1.9 %collective-permute-start.18 = (bf16[2,256,512]{2,1,0:T(8,128)(2,1)S(1)}, bf16[2,256,512]{2,1,0:T(8,128)(2,1)S(1)}, u32[]{:S(2)}, u32[]{:S(2)}) collective-permute-start(bf16[2,256,512]{2,1,0:T(8,128)(2,1)S(1)} %collective-permute-done.17.refs_3_), channel_id=1, source_target_pairs={{0,24},{8,0},{16,8},{24,16},{1,25},{9,1},{17,9},{25,17},{2,26},{10... | collective-permute-start | bytes 1572872 | tf_op jit(solution)/shard_map/ppermute | solution.py:214
  68.2 6.4 %correlate.6.refs_4_ = f32[8,208,256]{2,1,0:T(8,128)} custom-call(s32[1]{0:T(128)} %bitcast.refs_0_, bf16[16,8,512]{2,1,0:T(8,128)(2,1)} %copy-done, bf16[2,256,512]{2,1,0:T(8,128)(2,1)} %copy-done.7, bf16[2,256,512]{2,1,0:T(8,128)(2,1)} %copy-done.6, f32[8,208,256]{2,1,0:T(8,128)} %correlate.5.refs_4_), custom_call_target="tpu_custom_call" | custom-call | tf_op jit(solution)/shard_map/correlate/pallas_call | solution.py:173
  75.3 2.1 %collective-permute-done.18.refs_3_ = bf16[2,256,512]{2,1,0:T(8,128)(2,1)S(1)} collective-permute-done((bf16[2,256,512]{2,1,0:T(8,128)(2,1)S(1)}, bf16[2,256,512]{2,1,0:T(8,128)(2,1)S(1)}, u32[]{:S(2)}, u32[]{:S(2)}) %collective-permute-start.18) | collective-permute-done | bytes 524320 | tf_op jit(solution)/shard_map/ppermute | solution.py:214
  78.2 6.5 %correlate.7 = (f32[4,201,256]{2,1,0:T(8,128)}, f32[4,201,256]{2,1,0:T(8,128)}) custom-call(s32[1]{0:T(128)} %bitcast.refs_0_, bf16[16,8,512]{2,1,0:T(8,128)(2,1)} %copy-done, bf16[2,256,512]{2,1,0:T(8,128)(2,1)} %copy-done.9, bf16[2,256,512]{2,1,0:T(8,128)(2,1)} %copy-done.10, f32[8,208,256]{2,1,0:T(8,128)} %correlate.6.refs_4_), custom_call_target="tpu_custom_call" | custom-call | tf_op jit(solution)/shard_map/correlate/pallas_call | solution.py:173
  84.7 1.8 %copy.6 = f32[4,201,256]{2,0,1:T(4,128)S(1)} copy(f32[4,201,256]{2,1,0:T(8,128)} %get-tuple-element.60) | data formatting | bytes 1646592 | tf_op jit(solution)/shard_map/correlate/pallas_call | solution.py:173
  86.5 10.5 %collective-permute-start.19 = (f32[4,201,256]{2,0,1:T(4,128)S(1)}, f32[4,201,256]{2,0,1:T(4,128)S(1)}, u32[]{:S(2)}, u32[]{:S(2)}) collective-permute-start(f32[4,201,256]{2,0,1:T(4,128)S(1)} %copy.6), channel_id=1, source_target_pairs={{0,1},{1,0},{2,3},{3,2},{4,5},{5,4},{6,7},{7,6},{8,9},{9,8},{10,11... | collective-permute-start | bytes 2469896 | tf_op jit(solution)/shard_map/ppermute | solution.py:214
  96.9 2.0 %collective-permute-done.19 = f32[4,201,256]{2,0,1:T(4,128)S(1)} collective-permute-done((f32[4,201,256]{2,0,1:T(4,128)S(1)}, f32[4,201,256]{2,0,1:T(4,128)S(1)}, u32[]{:S(2)}, u32[]{:S(2)}) %collective-permute-start.19) | collective-permute-done | bytes 823328 | tf_op jit(solution)/shard_map/ppermute | solution.py:214
  99.1 1.4 %copy.8 = f32[4,201,256]{2,0,1:T(4,128)} copy(f32[4,201,256]{2,1,0:T(8,128)S(1)} %fusion) | data formatting | bytes 1646592 | tf_op jit(solution)/shard_map/mul | solution.py:260
  (59 shorter events, 6.3 us)
Async XLA Ops:
  3.0 7.6 %collective-permute-start = (bf16[128,512]{1,0:T(8,128)(2,1)}, bf16[128,512]{1,0:T(8,128)(2,1)S(1)}, u32[]{:S(2)}, u32[]{:S(2)}) collective-permute-start(bf16[128,512]{1,0:T(8,128)(2,1)} %get-tuple-element.33), channel_id=1, source_target_pairs={{0,128},{32,160},{64,192},{96,224},{128,0},{160,32},{192,64},{224,... | collective-permute-start | bytes 393224 | tf_op jit(solution)/shard_map/ppermute | solution.py:229
  5.5 19.5 %collective-permute-start.6 = (bf16[256,512]{1,0:T(8,128)(2,1)}, bf16[256,512]{1,0:T(8,128)(2,1)S(1)}, u32[]{:S(2)}, u32[]{:S(2)}) collective-permute-start(bf16[256,512]{1,0:T(8,128)(2,1)} %get-tuple-element.38), channel_id=1, source_target_pairs={{0,2},{2,4},{4,6},{6,0},{1,3},{3,5},{5,7},{7,1},{8,10},{10,12},{12... | collective-permute-start | bytes 786440 | tf_op jit(solution)/shard_map/ppermute | solution.py:214
  8.5 16.6 %collective-permute-start.10 = (bf16[256,512]{1,0:T(8,128)(2,1)}, bf16[256,512]{1,0:T(8,128)(2,1)S(1)}, u32[]{:S(2)}, u32[]{:S(2)}) collective-permute-start(bf16[256,512]{1,0:T(8,128)(2,1)} %get-tuple-element.38), channel_id=1, source_target_pairs={{0,6},{2,0},{4,2},{6,4},{1,7},{3,1},{5,3},{7,5},{8,14},{10,8},{12,... | collective-permute-start | bytes 786440 | tf_op jit(solution)/shard_map/ppermute | solution.py:214
  11.5 5.4 %collective-permute-start.1 = (bf16[128,512]{1,0:T(8,128)(2,1)S(1)}, bf16[128,512]{1,0:T(8,128)(2,1)S(1)}, u32[]{:S(2)}, u32[]{:S(2)}) collective-permute-start(bf16[128,512]{1,0:T(8,128)(2,1)S(1)} %add.9), channel_id=1, source_target_pairs={{0,64},{32,96},{64,0},{96,32},{128,192},{160,224},{192,128},{224,1... | collective-permute-start | bytes 393224 | tf_op jit(solution)/shard_map/ppermute | solution.py:229
  17.0 12.7 %copy-start.8 = (bf16[128,512]{1,0:T(8,128)(2,1)}, bf16[128,512]{1,0:T(8,128)(2,1)S(1)}, u32[]{:S(2)}) copy-start(bf16[128,512]{1,0:T(8,128)(2,1)S(1)} %add.10) | copy-start | bytes 393220
  17.0 12.7 %collective-permute-start.2 = (bf16[128,512]{1,0:T(8,128)(2,1)S(1)}, bf16[128,512]{1,0:T(8,128)(2,1)S(1)}, u32[]{:S(2)}, u32[]{:S(2)}) collective-permute-start(bf16[128,512]{1,0:T(8,128)(2,1)S(1)} %add.10), channel_id=1, source_target_pairs={{0,32},{32,0},{64,96},{96,64},{128,160},{160,128},{192,224},{224,1... | collective-permute-start | bytes 393224 | tf_op jit(solution)/shard_map/ppermute | solution.py:229
  24.9 11.9 %collective-permute-start.11 = (bf16[128,512]{1,0:T(8,128)(2,1)S(1)}, bf16[128,512]{1,0:T(8,128)(2,1)S(1)}, u32[]{:S(2)}, u32[]{:S(2)}) collective-permute-start(bf16[128,512]{1,0:T(8,128)(2,1)S(1)} %slice.8), channel_id=1, source_target_pairs={{0,2},{2,4},{4,6},{6,0},{1,3},{3,5},{5,7},{7,1},{8,10},{10,12},{12... | collective-permute-start | bytes 393224 | tf_op jit(solution)/shard_map/ppermute | solution.py:214
  25.1 11.8 %collective-permute-start.12 = (bf16[128,512]{1,0:T(8,128)(2,1)S(1)}, bf16[128,512]{1,0:T(8,128)(2,1)S(1)}, u32[]{:S(2)}, u32[]{:S(2)}) collective-permute-start(bf16[128,512]{1,0:T(8,128)(2,1)S(1)} %slice.9), channel_id=1, source_target_pairs={{0,6},{2,0},{4,2},{6,4},{1,7},{3,1},{5,3},{7,5},{8,14},{10,8},{12,... | collective-permute-start | bytes 393224 | tf_op jit(solution)/shard_map/ppermute | solution.py:214
  29.7 22.8 %copy-start.1 = (bf16[2,256,512]{2,1,0:T(8,128)(2,1)}, bf16[2,256,512]{2,1,0:T(8,128)(2,1)S(1)}, u32[]{:S(2)}) copy-start(bf16[2,256,512]{2,1,0:T(8,128)(2,1)S(1)} %pad_maximum_fusion.refs_2_) | copy-start | bytes 1572868
  32.1 4.9 %collective-permute-start.3 = (bf16[4,8,512]{2,1,0:T(8,128)(2,1)}, bf16[4,8,512]{2,1,0:T(8,128)(2,1)S(1)}, u32[]{:S(2)}, u32[]{:S(2)}) collective-permute-start(bf16[4,8,512]{2,1,0:T(8,128)(2,1)} %get-tuple-element.35), channel_id=1, source_target_pairs={{0,8},{8,16},{16,24},{24,0},{1,9},{9,17},{17,25},{25,1},{2,10},{10... | collective-permute-start | bytes 98312 | tf_op jit(solution)/shard_map/ppermute | solution.py:214
  33.3 4.5 %collective-permute-start.4 = (bf16[4,8,512]{2,1,0:T(8,128)(2,1)}, bf16[4,8,512]{2,1,0:T(8,128)(2,1)S(1)}, u32[]{:S(2)}, u32[]{:S(2)}) collective-permute-start(bf16[4,8,512]{2,1,0:T(8,128)(2,1)} %get-tuple-element.36), channel_id=1, source_target_pairs={{0,16},{8,24},{16,0},{24,8},{1,17},{9,25},{17,1},{25,9},{2,18},{10... | collective-permute-start | bytes 98312 | tf_op jit(solution)/shard_map/ppermute | solution.py:214
  35.7 3.3 %collective-permute-start.5 = (bf16[4,8,512]{2,1,0:T(8,128)(2,1)}, bf16[4,8,512]{2,1,0:T(8,128)(2,1)S(1)}, u32[]{:S(2)}, u32[]{:S(2)}) collective-permute-start(bf16[4,8,512]{2,1,0:T(8,128)(2,1)} %get-tuple-element.37), channel_id=1, source_target_pairs={{0,24},{8,0},{16,8},{24,16},{1,25},{9,1},{17,9},{25,17},{2,26},{10... | collective-permute-start | bytes 98312 | tf_op jit(solution)/shard_map/ppermute | solution.py:214
  36.9 2.1 %copy-start.12 = (bf16[4,8,512]{2,1,0:T(8,128)(2,1)}, bf16[4,8,512]{2,1,0:T(8,128)(2,1)S(1)}, u32[]{:S(2)}) copy-start(bf16[4,8,512]{2,1,0:T(8,128)(2,1)S(1)} %collective-permute-done.3.refs_1_) | copy-start | bytes 98308
  37.8 1.2 %copy-start.13 = (bf16[4,8,512]{2,1,0:T(8,128)(2,1)}, bf16[4,8,512]{2,1,0:T(8,128)(2,1)S(1)}, u32[]{:S(2)}) copy-start(bf16[4,8,512]{2,1,0:T(8,128)(2,1)S(1)} %collective-permute-done.4.refs_2_) | copy-start | bytes 98308
  41.1 7.7 %collective-permute-start.7 = (bf16[4,8,512]{2,1,0:T(8,128)(2,1)}, bf16[4,8,512]{2,1,0:T(8,128)(2,1)S(1)}, u32[]{:S(2)}, u32[]{:S(2)}) collective-permute-start(bf16[4,8,512]{2,1,0:T(8,128)(2,1)} %get-tuple-element.44), channel_id=1, source_target_pairs={{0,2},{2,4},{4,6},{6,0},{1,3},{3,5},{5,7},{7,1},{8,10},{10,12},{12... | collective-permute-start | bytes 98312 | tf_op jit(solution)/shard_map/ppermute | solution.py:214
  41.1 7.7 %collective-permute-start.8 = (bf16[4,8,512]{2,1,0:T(8,128)(2,1)}, bf16[4,8,512]{2,1,0:T(8,128)(2,1)S(1)}, u32[]{:S(2)}, u32[]{:S(2)}) collective-permute-start(bf16[4,8,512]{2,1,0:T(8,128)(2,1)} %get-tuple-element.45), channel_id=1, source_target_pairs={{0,4},{2,6},{4,0},{6,2},{1,5},{3,7},{5,1},{7,3},{8,12},{10,14},{12... | collective-permute-start | bytes 98312 | tf_op jit(solution)/shard_map/ppermute | solution.py:214
  42.9 5.9 %collective-permute-start.9 = (bf16[4,8,512]{2,1,0:T(8,128)(2,1)}, bf16[4,8,512]{2,1,0:T(8,128)(2,1)S(1)}, u32[]{:S(2)}, u32[]{:S(2)}) collective-permute-start(bf16[4,8,512]{2,1,0:T(8,128)(2,1)} %get-tuple-element.46), channel_id=1, source_target_pairs={{0,6},{2,0},{4,2},{6,4},{1,7},{3,1},{5,3},{7,5},{8,14},{10,8},{12,... | collective-permute-start | bytes 98312 | tf_op jit(solution)/shard_map/ppermute | solution.py:214
  46.0 6.5 %copy-start.2 = (bf16[2,256,512]{2,1,0:T(8,128)(2,1)}, bf16[2,256,512]{2,1,0:T(8,128)(2,1)S(1)}, u32[]{:S(2)}) copy-start(bf16[2,256,512]{2,1,0:T(8,128)(2,1)S(1)} %pad_maximum_fusion.1.refs_3_) | copy-start | bytes 1572868
  46.0 12.9 %collective-permute-start.13 = (bf16[2,256,512]{2,1,0:T(8,128)(2,1)S(1)}, bf16[2,256,512]{2,1,0:T(8,128)(2,1)S(1)}, u32[]{:S(2)}, u32[]{:S(2)}) collective-permute-start(bf16[2,256,512]{2,1,0:T(8,128)(2,1)S(1)} %pad_maximum_fusion.refs_2_), channel_id=1, source_target_pairs={{0,8},{8,16},{16,24},{24,0},{1,9},{9,17},{17,25},{25,1},{2,10},{10... | collective-permute-start | bytes 1572872 | tf_op jit(solution)/shard_map/ppermute | solution.py:214
  46.4 12.5 %collective-permute-start.14 = (bf16[2,256,512]{2,1,0:T(8,128)(2,1)S(1)}, bf16[2,256,512]{2,1,0:T(8,128)(2,1)S(1)}, u32[]{:S(2)}, u32[]{:S(2)}) collective-permute-start(bf16[2,256,512]{2,1,0:T(8,128)(2,1)S(1)} %pad_maximum_fusion.refs_2_), channel_id=1, source_target_pairs={{0,24},{8,0},{16,8},{24,16},{1,25},{9,1},{17,9},{25,17},{2,26},{10... | collective-permute-start | bytes 1572872 | tf_op jit(solution)/shard_map/ppermute | solution.py:214
  48.8 17.5 %collective-permute-start.16 = (bf16[2,256,512]{2,1,0:T(8,128)(2,1)S(1)}, bf16[2,256,512]{2,1,0:T(8,128)(2,1)S(1)}, u32[]{:S(2)}, u32[]{:S(2)}) collective-permute-start(bf16[2,256,512]{2,1,0:T(8,128)(2,1)S(1)} %pad_maximum_fusion.1.refs_3_), channel_id=1, source_target_pairs={{0,8},{8,16},{16,24},{24,0},{1,9},{9,17},{17,25},{25,1},{2,10},{10... | collective-permute-start | bytes 1572872 | tf_op jit(solution)/shard_map/ppermute | solution.py:214
  49.1 17.2 %collective-permute-start.17 = (bf16[2,256,512]{2,1,0:T(8,128)(2,1)S(1)}, bf16[2,256,512]{2,1,0:T(8,128)(2,1)S(1)}, u32[]{:S(2)}, u32[]{:S(2)}) collective-permute-start(bf16[2,256,512]{2,1,0:T(8,128)(2,1)S(1)} %pad_maximum_fusion.1.refs_3_), channel_id=1, source_target_pairs={{0,24},{8,0},{16,8},{24,16},{1,25},{9,1},{17,9},{25,17},{2,26},{10... | collective-permute-start | bytes 1572872 | tf_op jit(solution)/shard_map/ppermute | solution.py:214
  58.9 0.8 copy-start.4
  58.9 1.0 copy-start.5
  58.9 16.4 %collective-permute-start.15 = (bf16[2,256,512]{2,1,0:T(8,128)(2,1)S(1)}, bf16[2,256,512]{2,1,0:T(8,128)(2,1)S(1)}, u32[]{:S(2)}, u32[]{:S(2)}) collective-permute-start(bf16[2,256,512]{2,1,0:T(8,128)(2,1)S(1)} %collective-permute-done.13.refs_2_), channel_id=1, source_target_pairs={{0,8},{8,16},{16,24},{24,0},{1,9},{9,17},{17,25},{25,1},{2,10},{10... | collective-permute-start | bytes 1572872 | tf_op jit(solution)/shard_map/ppermute | solution.py:214
  66.3 1.9 %copy-start.7 = (bf16[2,256,512]{2,1,0:T(8,128)(2,1)}, bf16[2,256,512]{2,1,0:T(8,128)(2,1)S(1)}, u32[]{:S(2)}) copy-start(bf16[2,256,512]{2,1,0:T(8,128)(2,1)S(1)} %collective-permute-done.16.refs_2_) | copy-start | bytes 1572868
  66.3 1.9 %copy-start.6 = (bf16[2,256,512]{2,1,0:T(8,128)(2,1)}, bf16[2,256,512]{2,1,0:T(8,128)(2,1)S(1)}, u32[]{:S(2)}) copy-start(bf16[2,256,512]{2,1,0:T(8,128)(2,1)S(1)} %collective-permute-done.17.refs_3_) | copy-start | bytes 1572868
  66.3 11.1 %collective-permute-start.18 = (bf16[2,256,512]{2,1,0:T(8,128)(2,1)S(1)}, bf16[2,256,512]{2,1,0:T(8,128)(2,1)S(1)}, u32[]{:S(2)}, u32[]{:S(2)}) collective-permute-start(bf16[2,256,512]{2,1,0:T(8,128)(2,1)S(1)} %collective-permute-done.17.refs_3_), channel_id=1, source_target_pairs={{0,24},{8,0},{16,8},{24,16},{1,25},{9,1},{17,9},{25,17},{2,26},{10... | collective-permute-start | bytes 1572872 | tf_op jit(solution)/shard_map/ppermute | solution.py:214
  75.3 2.1 %copy-start.9 = (bf16[2,256,512]{2,1,0:T(8,128)(2,1)}, bf16[2,256,512]{2,1,0:T(8,128)(2,1)S(1)}, u32[]{:S(2)}) copy-start(bf16[2,256,512]{2,1,0:T(8,128)(2,1)S(1)} %collective-permute-done.15.refs_2_) | copy-start | bytes 1572868
  77.4 0.8 copy-start.10
  84.7 14.2 %copy-start.3 = (f32[4,201,256]{2,1,0:T(8,128)S(1)}, f32[4,201,256]{2,1,0:T(8,128)}, u32[]{:S(2)}) copy-start(f32[4,201,256]{2,1,0:T(8,128)} %get-tuple-element.59) | copy-start | bytes 2469892
  86.5 12.4 %collective-permute-start.19 = (f32[4,201,256]{2,0,1:T(4,128)S(1)}, f32[4,201,256]{2,0,1:T(4,128)S(1)}, u32[]{:S(2)}, u32[]{:S(2)}) collective-permute-start(f32[4,201,256]{2,0,1:T(4,128)S(1)} %copy.6), channel_id=1, source_target_pairs={{0,1},{1,0},{2,3},{3,2},{4,5},{5,4},{6,7},{7,6},{8,9},{9,8},{10,11... | collective-permute-start | bytes 2469896 | tf_op jit(solution)/shard_map/ppermute | solution.py:214
  (3 other events, 2.0 us)

commit v4 on v3

--- a/solution.py
+++ b/solution.py
@@ -134,8 +134,9 @@
         @pl.when(window == pl.num_programs(0) - 1)
         def _():
             core = core_ref[0]
-            mine_ref[...] = acc_ref[pl.ds(core * half, half), :NLAG, :]
-            other_ref[...] = acc_ref[pl.ds((1 - core) * half, half), :NLAG, :]
+            for at in range(half):
+                mine_ref[:, at, :] = acc_ref[core * half + at, :NLAG, :]
+                other_ref[:, at, :] = acc_ref[(1 - core) * half + at, :NLAG, :]
 
 
 def correlate(sources, early, late, prev, core, is_last):
@@ -143,7 +144,7 @@
     local_width = early.shape[1]
     acc_shape = (SRC_PAIR, LAGPAD, local_width)
     whole = lambda shape: pl.BlockSpec(shape, lambda w, core: (0,) * len(shape))
-    half_shape = (SRC_PAIR // 2, NLAG, local_width)
+    half_shape = (NLAG, SRC_PAIR // 2, local_width)
 
     def source_at(w, core):
         at_early, at_late = 4 * (early_z + w) + early_x, 4 * (late_z + w - PAIR) + late_x
@@ -222,8 +223,6 @@
     chans, size_x, size_z = lax.axis_size("chan"), lax.axis_size("x"), lax.axis_size("z_hi")
     own, mine = prep(raw_traces[0], fir_taps, source_blocks, valid_counts, chan.reshape(1))
     below, above = shifted(own, "z_hi", 1), shifted(own, "z_hi", -1)
-    half = own.shape[0] // 2
-    opposite = [shifted(below[:half], "z_hi", 1), shifted(above[half:], "z_hi", -1)]
 
     def swap(value, step):
         return lax.ppermute(value, "chan", [(i, i ^ step) for i in range(chans)])
@@ -237,9 +236,11 @@
     parts = [v.reshape(grouped) for v in (mine, swap(mine, step // 2))]
     dealt = deal(at_x.reshape(1), parts)
     dealt = [dealt[0]] + [shifted(dealt[by], "x", by) for by in range(1, 4)]
+    dealt, below, above = lax.optimization_barrier((dealt, below, above))
     low = jnp.stack([own, below])
-    dealt, low = lax.optimization_barrier((dealt, low))
     before_low, after_low = shifted(low, "x", 1), shifted(low, "x", -1)
+    half = own.shape[0] // 2
+    opposite = [shifted(below[:half], "z_hi", 1), shifted(above[half:], "z_hi", -1)]
     high = jnp.stack([above, jnp.concatenate(opposite, axis=0)])
     dealt = deal(at_z.reshape(1), dealt)
     dealt = [dealt[0]] + [shifted(dealt[by], "z_hi", by) for by in range(1, 4)]
@@ -257,7 +258,7 @@
     kept, passed = total
     got = shifted(passed, "core", 1)
     factor = 1.0 / math.sqrt(SAMP * size_x * size_z * 2)
-    return (kept + got) * factor
+    return jnp.transpose((kept + got) * factor, (1, 0, 2))
 
 
 def solution(mesh):

time: 101 us -> 96.5 us (0.955)
  local copies, waits for them, and re-layouts: 7.6 us -> 4.49 us
  waiting for transfers between devices: 15.5 us -> 13.2 us
  other arithmetic: 2.25 us -> 3.39 us
    ppermute x17, waiting for transfers between devices: 13.1 us -> 6.97 us  [shifted(): lax.ppermute(value, axis, [(i, (i + by) % size) for i in range(size)])]
    ppermute x3, waiting for transfers between devices: 2.41 us -> 6.28 us  [swap(): return lax.ppermute(value, 'chan', [(i, i ^ step) for i in range(chans)])]
    transpose x0 -> x1, other arithmetic: none -> 2.3 us  [shards(): return jnp.transpose((kept + got) * factor, (1, 0, 2))]
    pallas_call x1 -> x0, local copies, waits for them, and re-layouts: 1.76 us -> none  [correlate(): pl.pallas_call(body, grid_spec=pltpu.PrefetchScalarGridSpec(num_scalar_pr...]
    mul x1 -> x0, local copies, waits for them, and re-layouts: 1.42 us -> none  [shards(): return (kept + got) * factor]
  transfers between devices with their start and end apart: 20 -> 20, of which waited for: 7 -> 7; matrix products, arithmetic and copies ran while one was open for 3% -> 1% of each run, Pallas kernels for 20% -> 23%
where the time goes in v4:
time: 96.5 us; the launch traced here: 96 us
  starting transfers between devices  43.2 us (45%)
  Pallas kernels  31.5 us (33%)
  waiting for transfers between devices  13.2 us (14%)
  local copies, waits for them, and re-layouts  4.49 us (5%)
  other arithmetic  3.39 us (4%)
    ppermute x17, starting transfers between devices, shifted(): lax.ppermute(value, axis, [(i, (i + by) % size) for i in range(size)])  36.5 us
    pallas_call x4, Pallas kernels, correlate(): pl.pallas_call(body, grid_spec=pltpu.PrefetchScalarGridSpec(num_scalar_pr...  25.4 us
    ppermute x17, waiting for transfers between devices, shifted(): lax.ppermute(value, axis, [(i, (i + by) % size) for i in range(size)])  6.97 us
    ppermute x3, starting transfers between devices, swap(): return lax.ppermute(value, 'chan', [(i, i ^ step) for i in range(chans)])  6.69 us
    ppermute x3, waiting for transfers between devices, swap(): return lax.ppermute(value, 'chan', [(i, i ^ step) for i in range(chans)])  6.28 us
    unnamed x33, local copies, waits for them, and re-layouts  4.46 us
    pallas_call x2, Pallas kernels, deal(): pl.pallas_call(deal_body, in_specs=[smem] + [vmem] * len(arrays), out_spe...  3.1 us
    pallas_call x1, Pallas kernels, prep(): pl.pallas_call(prep_body, in_specs=[smem, smem, vmem, vmem, vmem], out_sp...  3 us
  transfers between devices with their start and end apart: 20, of which 7 were waited for; matrix products, arithmetic and copies ran while one was open for 1% of the time, Pallas kernels for 23%

profile of v4, /device:TPU:1, one launch (start us, length us, event | category | flops | bytes accessed | tf_op | source)
XLA Modules:
  0.0 96.0 jit_solution(4356877922515191290)
XLA Ops:
  0.0 3.0 %prep.1 = (bf16[256,512]{1,0:T(8,128)(2,1)}, bf16[128,512]{1,0:T(8,128)(2,1)}) custom-call(s32[2]{0:T(128)} %blocks_ref.1, s32[1]{0:T(128)} %bitcast.3.chan_ref, bf16[256,512]{1,0:T(8,128)(2,1)} %bitcast.18, f32[1,65]{1,0:T(1,128)} %bitcast.21, s32[1,256]{1,0:T(1,128)} %counts_ref.1), custom_call_target="tpu_custom_call" | custom-call | tf_op jit(solution)/shard_map/prep/pallas_call | solution.py:83
  3.0 2.5 %collective-permute-start = (bf16[128,512]{1,0:T(8,128)(2,1)}, bf16[128,512]{1,0:T(8,128)(2,1)S(1)}, u32[]{:S(2)}, u32[]{:S(2)}) collective-permute-start(bf16[128,512]{1,0:T(8,128)(2,1)} %get-tuple-element.34), channel_id=1, source_target_pairs={{0,128},{32,160},{64,192},{96,224},{128,0},{160,32},{192,64},{224,... | collective-permute-start | bytes 393224 | tf_op jit(solution)/shard_map/ppermute | solution.py:228
  5.5 2.6 %collective-permute-done = bf16[128,512]{1,0:T(8,128)(2,1)S(1)} collective-permute-done((bf16[128,512]{1,0:T(8,128)(2,1)}, bf16[128,512]{1,0:T(8,128)(2,1)S(1)}, u32[]{:S(2)}, u32[]{:S(2)}) %collective-permute-start) | collective-permute-done | bytes 131104 | tf_op jit(solution)/shard_map/ppermute | solution.py:228
  8.0 0.9 add.9
  9.0 3.7 %collective-permute-start.1 = (bf16[128,512]{1,0:T(8,128)(2,1)S(1)}, bf16[128,512]{1,0:T(8,128)(2,1)S(1)}, u32[]{:S(2)}, u32[]{:S(2)}) collective-permute-start(bf16[128,512]{1,0:T(8,128)(2,1)S(1)} %add.9), channel_id=1, source_target_pairs={{0,64},{32,96},{64,0},{96,32},{128,192},{160,224},{192,128},{224,1... | collective-permute-start | bytes 393224 | tf_op jit(solution)/shard_map/ppermute | solution.py:228
  12.7 3.0 %collective-permute-start.6 = (bf16[256,512]{1,0:T(8,128)(2,1)}, bf16[256,512]{1,0:T(8,128)(2,1)S(1)}, u32[]{:S(2)}, u32[]{:S(2)}) collective-permute-start(bf16[256,512]{1,0:T(8,128)(2,1)} %get-tuple-element.39), channel_id=1, source_target_pairs={{0,2},{2,4},{4,6},{6,0},{1,3},{3,5},{5,7},{7,1},{8,10},{10,12},{12... | collective-permute-start | bytes 786440 | tf_op jit(solution)/shard_map/ppermute | solution.py:215
  15.7 2.7 %collective-permute-start.7 = (bf16[256,512]{1,0:T(8,128)(2,1)}, bf16[256,512]{1,0:T(8,128)(2,1)S(1)}, u32[]{:S(2)}, u32[]{:S(2)}) collective-permute-start(bf16[256,512]{1,0:T(8,128)(2,1)} %get-tuple-element.39), channel_id=1, source_target_pairs={{0,6},{2,0},{4,2},{6,4},{1,7},{3,1},{5,3},{7,5},{8,14},{10,8},{12,... | collective-permute-start | bytes 786440 | tf_op jit(solution)/shard_map/ppermute | solution.py:215
  18.9 3.7 %collective-permute-done.2 = bf16[128,512]{1,0:T(8,128)(2,1)S(1)} collective-permute-done((bf16[128,512]{1,0:T(8,128)(2,1)S(1)}, bf16[128,512]{1,0:T(8,128)(2,1)S(1)}, u32[]{:S(2)}, u32[]{:S(2)}) %collective-permute-start.2) | collective-permute-done | bytes 131104 | tf_op jit(solution)/shard_map/ppermute | solution.py:228
  23.3 1.6 %deal.2 = (bf16[4,8,512]{2,1,0:T(8,128)(2,1)}, bf16[4,8,512]{2,1,0:T(8,128)(2,1)}, bf16[4,8,512]{2,1,0:T(8,128)(2,1)}, bf16[4,8,512]{2,1,0:T(8,128)(2,1)}) custom-call(s32[1]{0:T(128)} %bitcast.2.at_ref, bf16[4,4,8,512]{3,2,1,0:T(8,128)(2,1)} %bitcast.17, bf16[4,4,8,512]{3,2,1,0:T(8,128)(2,1)} %bitcast.20), custom_call_target="tpu_custom_call" | custom-call | tf_op jit(solution)/shard_map/deal/pallas_call | solution.py:204
  24.9 1.2 %collective-permute-start.3 = (bf16[4,8,512]{2,1,0:T(8,128)(2,1)}, bf16[4,8,512]{2,1,0:T(8,128)(2,1)S(1)}, u32[]{:S(2)}, u32[]{:S(2)}) collective-permute-start(bf16[4,8,512]{2,1,0:T(8,128)(2,1)} %get-tuple-element.36), channel_id=1, source_target_pairs={{0,8},{8,16},{16,24},{24,0},{1,9},{9,17},{17,25},{25,1},{2,10},{10... | collective-permute-start | bytes 98312 | tf_op jit(solution)/shard_map/ppermute | solution.py:215
  26.1 2.4 %collective-permute-start.4 = (bf16[4,8,512]{2,1,0:T(8,128)(2,1)}, bf16[4,8,512]{2,1,0:T(8,128)(2,1)S(1)}, u32[]{:S(2)}, u32[]{:S(2)}) collective-permute-start(bf16[4,8,512]{2,1,0:T(8,128)(2,1)} %get-tuple-element.37), channel_id=1, source_target_pairs={{0,16},{8,24},{16,0},{24,8},{1,17},{9,25},{17,1},{25,9},{2,18},{10... | collective-permute-start | bytes 98312 | tf_op jit(solution)/shard_map/ppermute | solution.py:215
  28.6 1.2 %collective-permute-start.5 = (bf16[4,8,512]{2,1,0:T(8,128)(2,1)}, bf16[4,8,512]{2,1,0:T(8,128)(2,1)S(1)}, u32[]{:S(2)}, u32[]{:S(2)}) collective-permute-start(bf16[4,8,512]{2,1,0:T(8,128)(2,1)} %get-tuple-element.38), channel_id=1, source_target_pairs={{0,24},{8,0},{16,8},{24,16},{1,25},{9,1},{17,9},{25,17},{2,26},{10... | collective-permute-start | bytes 98312 | tf_op jit(solution)/shard_map/ppermute | solution.py:215
  29.7 1.9 %collective-permute-done.7 = bf16[256,512]{1,0:T(8,128)(2,1)S(1)} collective-permute-done((bf16[256,512]{1,0:T(8,128)(2,1)}, bf16[256,512]{1,0:T(8,128)(2,1)S(1)}, u32[]{:S(2)}, u32[]{:S(2)}) %collective-permute-start.7) | collective-permute-done | bytes 262176 | tf_op jit(solution)/shard_map/ppermute | solution.py:215
  31.9 2.5 %collective-permute-start.11 = (bf16[128,512]{1,0:T(8,128)(2,1)S(1)}, bf16[128,512]{1,0:T(8,128)(2,1)S(1)}, u32[]{:S(2)}, u32[]{:S(2)}) collective-permute-start(bf16[128,512]{1,0:T(8,128)(2,1)S(1)} %slice.6), channel_id=1, source_target_pairs={{0,2},{2,4},{4,6},{6,0},{1,3},{3,5},{5,7},{7,1},{8,10},{10,12},{12... | collective-permute-start | bytes 393224 | tf_op jit(solution)/shard_map/ppermute | solution.py:215
  34.4 1.2 %collective-permute-start.12 = (bf16[128,512]{1,0:T(8,128)(2,1)S(1)}, bf16[128,512]{1,0:T(8,128)(2,1)S(1)}, u32[]{:S(2)}, u32[]{:S(2)}) collective-permute-start(bf16[128,512]{1,0:T(8,128)(2,1)S(1)} %slice.7), channel_id=1, source_target_pairs={{0,6},{2,0},{4,2},{6,4},{1,7},{3,1},{5,3},{7,5},{8,14},{10,8},{12,... | collective-permute-start | bytes 393224 | tf_op jit(solution)/shard_map/ppermute | solution.py:215
  35.7 1.1 %collective-permute-start.13 = (bf16[2,256,512]{2,1,0:T(8,128)(2,1)S(1)}, bf16[2,256,512]{2,1,0:T(8,128)(2,1)S(1)}, u32[]{:S(2)}, u32[]{:S(2)}) collective-permute-start(bf16[2,256,512]{2,1,0:T(8,128)(2,1)S(1)} %pad_maximum_fusion.1.refs_2_), channel_id=1, source_target_pairs={{0,8},{8,16},{16,24},{24,0},{1,9},{9,17},{17,25},{25,1},{2,10},{10... | collective-permute-start | bytes 1572872 | tf_op jit(solution)/shard_map/ppermute | solution.py:215
  36.8 1.6 %collective-permute-start.14 = (bf16[2,256,512]{2,1,0:T(8,128)(2,1)S(1)}, bf16[2,256,512]{2,1,0:T(8,128)(2,1)S(1)}, u32[]{:S(2)}, u32[]{:S(2)}) collective-permute-start(bf16[2,256,512]{2,1,0:T(8,128)(2,1)S(1)} %pad_maximum_fusion.1.refs_2_), channel_id=1, source_target_pairs={{0,24},{8,0},{16,8},{24,16},{1,25},{9,1},{17,9},{25,17},{2,26},{10... | collective-permute-start | bytes 1572872 | tf_op jit(solution)/shard_map/ppermute | solution.py:215
  38.4 1.5 %deal.3 = (bf16[4,8,512]{2,1,0:T(8,128)(2,1)}, bf16[4,8,512]{2,1,0:T(8,128)(2,1)}, bf16[4,8,512]{2,1,0:T(8,128)(2,1)}, bf16[4,8,512]{2,1,0:T(8,128)(2,1)}) custom-call(s32[1]{0:T(128)} %bitcast.1.at_ref, bf16[4,8,512]{2,1,0:T(8,128)(2,1)} %get-tuple-element.40.refs_0_, bf16[4,8,512]{2,1,0:T(8,128)(2,1)} %copy-done.12, bf16[4,8,512]{2,1,0:T(8,128)(2,1)} %copy-done.13, ...), custom_call_target="tpu_custom_call" | custom-call | tf_op jit(solution)/shard_map/deal/pallas_call | solution.py:204
  39.9 1.2 %collective-permute-start.10 = (bf16[4,8,512]{2,1,0:T(8,128)(2,1)}, bf16[4,8,512]{2,1,0:T(8,128)(2,1)S(1)}, u32[]{:S(2)}, u32[]{:S(2)}) collective-permute-start(bf16[4,8,512]{2,1,0:T(8,128)(2,1)} %get-tuple-element.47), channel_id=1, source_target_pairs={{0,6},{2,0},{4,2},{6,4},{1,7},{3,1},{5,3},{7,5},{8,14},{10,8},{12,... | collective-permute-start | bytes 98312 | tf_op jit(solution)/shard_map/ppermute | solution.py:215
  41.1 1.2 %collective-permute-start.8 = (bf16[4,8,512]{2,1,0:T(8,128)(2,1)}, bf16[4,8,512]{2,1,0:T(8,128)(2,1)S(1)}, u32[]{:S(2)}, u32[]{:S(2)}) collective-permute-start(bf16[4,8,512]{2,1,0:T(8,128)(2,1)} %get-tuple-element.45), channel_id=1, source_target_pairs={{0,2},{2,4},{4,6},{6,0},{1,3},{3,5},{5,7},{7,1},{8,10},{10,12},{12... | collective-permute-start | bytes 98312 | tf_op jit(solution)/shard_map/ppermute | solution.py:215
  42.3 4.2 %collective-permute-start.9 = (bf16[4,8,512]{2,1,0:T(8,128)(2,1)}, bf16[4,8,512]{2,1,0:T(8,128)(2,1)S(1)}, u32[]{:S(2)}, u32[]{:S(2)}) collective-permute-start(bf16[4,8,512]{2,1,0:T(8,128)(2,1)} %get-tuple-element.46), channel_id=1, source_target_pairs={{0,4},{2,6},{4,0},{6,2},{1,5},{3,7},{5,1},{7,3},{8,12},{10,14},{12... | collective-permute-start | bytes 98312 | tf_op jit(solution)/shard_map/ppermute | solution.py:215
  46.5 2.6 %collective-permute-done.9 = bf16[4,8,512]{2,1,0:T(8,128)(2,1)S(1)} collective-permute-done((bf16[4,8,512]{2,1,0:T(8,128)(2,1)}, bf16[4,8,512]{2,1,0:T(8,128)(2,1)S(1)}, u32[]{:S(2)}, u32[]{:S(2)}) %collective-permute-start.9) | collective-permute-done | bytes 32800 | tf_op jit(solution)/shard_map/ppermute | solution.py:215
  49.2 2.7 %collective-permute-start.17 = (bf16[2,256,512]{2,1,0:T(8,128)(2,1)S(1)}, bf16[2,256,512]{2,1,0:T(8,128)(2,1)S(1)}, u32[]{:S(2)}, u32[]{:S(2)}) collective-permute-start(bf16[2,256,512]{2,1,0:T(8,128)(2,1)S(1)} %pad_maximum_fusion.refs_3_), channel_id=1, source_target_pairs={{0,24},{8,0},{16,8},{24,16},{1,25},{9,1},{17,9},{25,17},{2,26},{10... | collective-permute-start | bytes 1572872 | tf_op jit(solution)/shard_map/ppermute | solution.py:215
  53.3 5.7 %correlate.4.refs_4_ = f32[8,208,256]{2,1,0:T(8,128)} custom-call(s32[1]{0:T(128)} %bitcast.refs_0_, bf16[16,8,512]{2,1,0:T(8,128)(2,1)} %copy-done, bf16[2,256,512]{2,1,0:T(8,128)(2,1)} %copy-done.1, bf16[2,256,512]{2,1,0:T(8,128)(2,1)} %copy-done.2), custom_call_target="tpu_custom_call" | custom-call | tf_op jit(solution)/shard_map/correlate/pallas_call | solution.py:174
  60.0 6.4 %correlate.5.refs_4_ = f32[8,208,256]{2,1,0:T(8,128)} custom-call(s32[1]{0:T(128)} %bitcast.refs_0_, bf16[16,8,512]{2,1,0:T(8,128)(2,1)} %copy-done, bf16[2,256,512]{2,1,0:T(8,128)(2,1)} %copy-done.3, bf16[2,256,512]{2,1,0:T(8,128)(2,1)} %copy-done.4, f32[8,208,256]{2,1,0:T(8,128)} %correlate.4.refs_4_), custom_call_target="tpu_custom_call" | custom-call | tf_op jit(solution)/shard_map/correlate/pallas_call | solution.py:174
  66.4 1.9 %collective-permute-start.18 = (bf16[2,256,512]{2,1,0:T(8,128)(2,1)S(1)}, bf16[2,256,512]{2,1,0:T(8,128)(2,1)S(1)}, u32[]{:S(2)}, u32[]{:S(2)}) collective-permute-start(bf16[2,256,512]{2,1,0:T(8,128)(2,1)S(1)} %collective-permute-done.17.refs_3_), channel_id=1, source_target_pairs={{0,24},{8,0},{16,8},{24,16},{1,25},{9,1},{17,9},{25,17},{2,26},{10... | collective-permute-start | bytes 1572872 | tf_op jit(solution)/shard_map/ppermute | solution.py:215
  68.3 6.4 %correlate.6.refs_4_ = f32[8,208,256]{2,1,0:T(8,128)} custom-call(s32[1]{0:T(128)} %bitcast.refs_0_, bf16[16,8,512]{2,1,0:T(8,128)(2,1)} %copy-done, bf16[2,256,512]{2,1,0:T(8,128)(2,1)} %copy-done.6, bf16[2,256,512]{2,1,0:T(8,128)(2,1)} %copy-done.5, f32[8,208,256]{2,1,0:T(8,128)} %correlate.5.refs_4_), custom_call_target="tpu_custom_call" | custom-call | tf_op jit(solution)/shard_map/correlate/pallas_call | solution.py:174
  75.5 0.8 copy-done.9
  76.3 6.9 %correlate.7 = (f32[201,4,256]{2,1,0:T(4,128)}, f32[201,4,256]{2,1,0:T(4,128)}) custom-call(s32[1]{0:T(128)} %bitcast.refs_0_, bf16[16,8,512]{2,1,0:T(8,128)(2,1)} %copy-done, bf16[2,256,512]{2,1,0:T(8,128)(2,1)} %copy-done.8, bf16[2,256,512]{2,1,0:T(8,128)(2,1)} %copy-done.9, f32[8,208,256]{2,1,0:T(8,128)} %correlate.6.refs_4_), custom_call_target="tpu_custom_call" | custom-call | tf_op jit(solution)/shard_map/correlate/pallas_call | solution.py:174
  83.2 8.3 %collective-permute-start.19 = (f32[201,4,256]{2,1,0:T(4,128)}, f32[201,4,256]{2,1,0:T(4,128)S(1)}, u32[]{:S(2)}, u32[]{:S(2)}) collective-permute-start(f32[201,4,256]{2,1,0:T(4,128)} %get-tuple-element.62), channel_id=1, source_target_pairs={{0,1},{1,0},{2,3},{3,2},{4,5},{5,4},{6,7},{7,6},{8,9},{9,8},{10,11... | collective-permute-start | bytes 2469896 | tf_op jit(solution)/shard_map/ppermute | solution.py:215
  91.5 2.2 %collective-permute-done.19 = f32[201,4,256]{2,1,0:T(4,128)S(1)} collective-permute-done((f32[201,4,256]{2,1,0:T(4,128)}, f32[201,4,256]{2,1,0:T(4,128)S(1)}, u32[]{:S(2)}, u32[]{:S(2)}) %collective-permute-start.19) | collective-permute-done | bytes 823328 | tf_op jit(solution)/shard_map/ppermute | solution.py:215
  93.7 2.3 %multiply_bitcast_fusion = f32[4,201,256]{2,0,1:T(4,128)} fusion(f32[201,4,256]{2,1,0:T(4,128)} %get-tuple-element.61, f32[201,4,256]{2,1,0:T(4,128)S(1)} %collective-permute-done.19), kind=kLoop, calls=%fused_computation | loop fusion | flops 411648 | bytes 2469888 | tf_op jit(solution)/shard_map/transpose | solution.py:261
  (57 shorter events, 4.7 us)
Async XLA Ops:
  3.0 32.6 %copy-start.10 = (bf16[256,512]{1,0:T(8,128)(2,1)S(1)}, bf16[256,512]{1,0:T(8,128)(2,1)}, u32[]{:S(2)}) copy-start(bf16[256,512]{1,0:T(8,128)(2,1)} %get-tuple-element.39) | copy-start | bytes 786436
  3.0 5.0 %collective-permute-start = (bf16[128,512]{1,0:T(8,128)(2,1)}, bf16[128,512]{1,0:T(8,128)(2,1)S(1)}, u32[]{:S(2)}, u32[]{:S(2)}) collective-permute-start(bf16[128,512]{1,0:T(8,128)(2,1)} %get-tuple-element.34), channel_id=1, source_target_pairs={{0,128},{32,160},{64,192},{96,224},{128,0},{160,32},{192,64},{224,... | collective-permute-start | bytes 393224 | tf_op jit(solution)/shard_map/ppermute | solution.py:228
  9.0 9.4 %collective-permute-start.1 = (bf16[128,512]{1,0:T(8,128)(2,1)S(1)}, bf16[128,512]{1,0:T(8,128)(2,1)S(1)}, u32[]{:S(2)}, u32[]{:S(2)}) collective-permute-start(bf16[128,512]{1,0:T(8,128)(2,1)S(1)} %add.9), channel_id=1, source_target_pairs={{0,64},{32,96},{64,0},{96,32},{128,192},{160,224},{192,128},{224,1... | collective-permute-start | bytes 393224 | tf_op jit(solution)/shard_map/ppermute | solution.py:228
  12.7 17.0 %collective-permute-start.6 = (bf16[256,512]{1,0:T(8,128)(2,1)}, bf16[256,512]{1,0:T(8,128)(2,1)S(1)}, u32[]{:S(2)}, u32[]{:S(2)}) collective-permute-start(bf16[256,512]{1,0:T(8,128)(2,1)} %get-tuple-element.39), channel_id=1, source_target_pairs={{0,2},{2,4},{4,6},{6,0},{1,3},{3,5},{5,7},{7,1},{8,10},{10,12},{12... | collective-permute-start | bytes 786440 | tf_op jit(solution)/shard_map/ppermute | solution.py:215
  15.7 15.9 %collective-permute-start.7 = (bf16[256,512]{1,0:T(8,128)(2,1)}, bf16[256,512]{1,0:T(8,128)(2,1)S(1)}, u32[]{:S(2)}, u32[]{:S(2)}) collective-permute-start(bf16[256,512]{1,0:T(8,128)(2,1)} %get-tuple-element.39), channel_id=1, source_target_pairs={{0,6},{2,0},{4,2},{6,4},{1,7},{3,1},{5,3},{7,5},{8,14},{10,8},{12,... | collective-permute-start | bytes 786440 | tf_op jit(solution)/shard_map/ppermute | solution.py:215
  18.4 4.2 %copy-start.7 = (bf16[128,512]{1,0:T(8,128)(2,1)}, bf16[128,512]{1,0:T(8,128)(2,1)S(1)}, u32[]{:S(2)}) copy-start(bf16[128,512]{1,0:T(8,128)(2,1)S(1)} %add.10) | copy-start | bytes 393220
  18.4 4.2 %collective-permute-start.2 = (bf16[128,512]{1,0:T(8,128)(2,1)S(1)}, bf16[128,512]{1,0:T(8,128)(2,1)S(1)}, u32[]{:S(2)}, u32[]{:S(2)}) collective-permute-start(bf16[128,512]{1,0:T(8,128)(2,1)S(1)} %add.10), channel_id=1, source_target_pairs={{0,32},{32,0},{64,96},{96,64},{128,160},{160,128},{192,224},{224,1... | collective-permute-start | bytes 393224 | tf_op jit(solution)/shard_map/ppermute | solution.py:228
  24.9 6.7 %collective-permute-start.3 = (bf16[4,8,512]{2,1,0:T(8,128)(2,1)}, bf16[4,8,512]{2,1,0:T(8,128)(2,1)S(1)}, u32[]{:S(2)}, u32[]{:S(2)}) collective-permute-start(bf16[4,8,512]{2,1,0:T(8,128)(2,1)} %get-tuple-element.36), channel_id=1, source_target_pairs={{0,8},{8,16},{16,24},{24,0},{1,9},{9,17},{17,25},{25,1},{2,10},{10... | collective-permute-start | bytes 98312 | tf_op jit(solution)/shard_map/ppermute | solution.py:215
  26.1 5.5 %collective-permute-start.4 = (bf16[4,8,512]{2,1,0:T(8,128)(2,1)}, bf16[4,8,512]{2,1,0:T(8,128)(2,1)S(1)}, u32[]{:S(2)}, u32[]{:S(2)}) collective-permute-start(bf16[4,8,512]{2,1,0:T(8,128)(2,1)} %get-tuple-element.37), channel_id=1, source_target_pairs={{0,16},{8,24},{16,0},{24,8},{1,17},{9,25},{17,1},{25,9},{2,18},{10... | collective-permute-start | bytes 98312 | tf_op jit(solution)/shard_map/ppermute | solution.py:215
  28.6 3.3 %collective-permute-start.5 = (bf16[4,8,512]{2,1,0:T(8,128)(2,1)}, bf16[4,8,512]{2,1,0:T(8,128)(2,1)S(1)}, u32[]{:S(2)}, u32[]{:S(2)}) collective-permute-start(bf16[4,8,512]{2,1,0:T(8,128)(2,1)} %get-tuple-element.38), channel_id=1, source_target_pairs={{0,24},{8,0},{16,8},{24,16},{1,25},{9,1},{17,9},{25,17},{2,26},{10... | collective-permute-start | bytes 98312 | tf_op jit(solution)/shard_map/ppermute | solution.py:215
  31.6 6.8 %copy-start.12 = (bf16[4,8,512]{2,1,0:T(8,128)(2,1)}, bf16[4,8,512]{2,1,0:T(8,128)(2,1)S(1)}, u32[]{:S(2)}) copy-start(bf16[4,8,512]{2,1,0:T(8,128)(2,1)S(1)} %collective-permute-done.3.refs_1_) | copy-start | bytes 98308
  31.6 6.8 %copy-start.13 = (bf16[4,8,512]{2,1,0:T(8,128)(2,1)}, bf16[4,8,512]{2,1,0:T(8,128)(2,1)S(1)}, u32[]{:S(2)}) copy-start(bf16[4,8,512]{2,1,0:T(8,128)(2,1)S(1)} %collective-permute-done.4.refs_2_) | copy-start | bytes 98308
  31.8 6.6 %copy-start.14 = (bf16[4,8,512]{2,1,0:T(8,128)(2,1)}, bf16[4,8,512]{2,1,0:T(8,128)(2,1)S(1)}, u32[]{:S(2)}) copy-start(bf16[4,8,512]{2,1,0:T(8,128)(2,1)S(1)} %collective-permute-done.5.refs_3_) | copy-start | bytes 98308
  31.9 9.2 %collective-permute-start.11 = (bf16[128,512]{1,0:T(8,128)(2,1)S(1)}, bf16[128,512]{1,0:T(8,128)(2,1)S(1)}, u32[]{:S(2)}, u32[]{:S(2)}) collective-permute-start(bf16[128,512]{1,0:T(8,128)(2,1)S(1)} %slice.6), channel_id=1, source_target_pairs={{0,2},{2,4},{4,6},{6,0},{1,3},{3,5},{5,7},{7,1},{8,10},{10,12},{12... | collective-permute-start | bytes 393224 | tf_op jit(solution)/shard_map/ppermute | solution.py:215
  34.4 7.9 %collective-permute-start.12 = (bf16[128,512]{1,0:T(8,128)(2,1)S(1)}, bf16[128,512]{1,0:T(8,128)(2,1)S(1)}, u32[]{:S(2)}, u32[]{:S(2)}) collective-permute-start(bf16[128,512]{1,0:T(8,128)(2,1)S(1)} %slice.7), channel_id=1, source_target_pairs={{0,6},{2,0},{4,2},{6,4},{1,7},{3,1},{5,3},{7,5},{8,14},{10,8},{12,... | collective-permute-start | bytes 393224 | tf_op jit(solution)/shard_map/ppermute | solution.py:215
  35.7 17.0 %copy-start.1 = (bf16[2,256,512]{2,1,0:T(8,128)(2,1)}, bf16[2,256,512]{2,1,0:T(8,128)(2,1)S(1)}, u32[]{:S(2)}) copy-start(bf16[2,256,512]{2,1,0:T(8,128)(2,1)S(1)} %pad_maximum_fusion.1.refs_2_) | copy-start | bytes 1572868
  35.7 23.3 %collective-permute-start.13 = (bf16[2,256,512]{2,1,0:T(8,128)(2,1)S(1)}, bf16[2,256,512]{2,1,0:T(8,128)(2,1)S(1)}, u32[]{:S(2)}, u32[]{:S(2)}) collective-permute-start(bf16[2,256,512]{2,1,0:T(8,128)(2,1)S(1)} %pad_maximum_fusion.1.refs_2_), channel_id=1, source_target_pairs={{0,8},{8,16},{16,24},{24,0},{1,9},{9,17},{17,25},{25,1},{2,10},{10... | collective-permute-start | bytes 1572872 | tf_op jit(solution)/shard_map/ppermute | solution.py:215
  36.8 22.2 %collective-permute-start.14 = (bf16[2,256,512]{2,1,0:T(8,128)(2,1)S(1)}, bf16[2,256,512]{2,1,0:T(8,128)(2,1)S(1)}, u32[]{:S(2)}, u32[]{:S(2)}) collective-permute-start(bf16[2,256,512]{2,1,0:T(8,128)(2,1)S(1)} %pad_maximum_fusion.1.refs_2_), channel_id=1, source_target_pairs={{0,24},{8,0},{16,8},{24,16},{1,25},{9,1},{17,9},{25,17},{2,26},{10... | collective-permute-start | bytes 1572872 | tf_op jit(solution)/shard_map/ppermute | solution.py:215
  39.9 6.6 %collective-permute-start.10 = (bf16[4,8,512]{2,1,0:T(8,128)(2,1)}, bf16[4,8,512]{2,1,0:T(8,128)(2,1)S(1)}, u32[]{:S(2)}, u32[]{:S(2)}) collective-permute-start(bf16[4,8,512]{2,1,0:T(8,128)(2,1)} %get-tuple-element.47), channel_id=1, source_target_pairs={{0,6},{2,0},{4,2},{6,4},{1,7},{3,1},{5,3},{7,5},{8,14},{10,8},{12,... | collective-permute-start | bytes 98312 | tf_op jit(solution)/shard_map/ppermute | solution.py:215
  41.1 5.4 %collective-permute-start.8 = (bf16[4,8,512]{2,1,0:T(8,128)(2,1)}, bf16[4,8,512]{2,1,0:T(8,128)(2,1)S(1)}, u32[]{:S(2)}, u32[]{:S(2)}) collective-permute-start(bf16[4,8,512]{2,1,0:T(8,128)(2,1)} %get-tuple-element.45), channel_id=1, source_target_pairs={{0,2},{2,4},{4,6},{6,0},{1,3},{3,5},{5,7},{7,1},{8,10},{10,12},{12... | collective-permute-start | bytes 98312 | tf_op jit(solution)/shard_map/ppermute | solution.py:215
  42.3 6.9 %collective-permute-start.9 = (bf16[4,8,512]{2,1,0:T(8,128)(2,1)}, bf16[4,8,512]{2,1,0:T(8,128)(2,1)S(1)}, u32[]{:S(2)}, u32[]{:S(2)}) collective-permute-start(bf16[4,8,512]{2,1,0:T(8,128)(2,1)} %get-tuple-element.46), channel_id=1, source_target_pairs={{0,4},{2,6},{4,0},{6,2},{1,5},{3,7},{5,1},{7,3},{8,12},{10,14},{12... | collective-permute-start | bytes 98312 | tf_op jit(solution)/shard_map/ppermute | solution.py:215
  46.5 6.1 %copy-start.2 = (bf16[2,256,512]{2,1,0:T(8,128)(2,1)}, bf16[2,256,512]{2,1,0:T(8,128)(2,1)S(1)}, u32[]{:S(2)}) copy-start(bf16[2,256,512]{2,1,0:T(8,128)(2,1)S(1)} %pad_maximum_fusion.refs_3_) | copy-start | bytes 1572868
  49.1 17.2 %collective-permute-start.16 = (bf16[2,256,512]{2,1,0:T(8,128)(2,1)S(1)}, bf16[2,256,512]{2,1,0:T(8,128)(2,1)S(1)}, u32[]{:S(2)}, u32[]{:S(2)}) collective-permute-start(bf16[2,256,512]{2,1,0:T(8,128)(2,1)S(1)} %pad_maximum_fusion.refs_3_), channel_id=1, source_target_pairs={{0,8},{8,16},{16,24},{24,0},{1,9},{9,17},{17,25},{25,1},{2,10},{10... | collective-permute-start | bytes 1572872 | tf_op jit(solution)/shard_map/ppermute | solution.py:215
  49.2 17.2 %collective-permute-start.17 = (bf16[2,256,512]{2,1,0:T(8,128)(2,1)S(1)}, bf16[2,256,512]{2,1,0:T(8,128)(2,1)S(1)}, u32[]{:S(2)}, u32[]{:S(2)}) collective-permute-start(bf16[2,256,512]{2,1,0:T(8,128)(2,1)S(1)} %pad_maximum_fusion.refs_3_), channel_id=1, source_target_pairs={{0,24},{8,0},{16,8},{24,16},{1,25},{9,1},{17,9},{25,17},{2,26},{10... | collective-permute-start | bytes 1572872 | tf_op jit(solution)/shard_map/ppermute | solution.py:215
  59.0 0.8 copy-start.3
  59.0 1.0 %copy-start.4 = (bf16[2,256,512]{2,1,0:T(8,128)(2,1)}, bf16[2,256,512]{2,1,0:T(8,128)(2,1)S(1)}, u32[]{:S(2)}) copy-start(bf16[2,256,512]{2,1,0:T(8,128)(2,1)S(1)} %collective-permute-done.14.refs_3_) | copy-start | bytes 1572868
  59.0 15.7 %collective-permute-start.15 = (bf16[2,256,512]{2,1,0:T(8,128)(2,1)S(1)}, bf16[2,256,512]{2,1,0:T(8,128)(2,1)S(1)}, u32[]{:S(2)}, u32[]{:S(2)}) collective-permute-start(bf16[2,256,512]{2,1,0:T(8,128)(2,1)S(1)} %collective-permute-done.13.refs_2_), channel_id=1, source_target_pairs={{0,8},{8,16},{16,24},{24,0},{1,9},{9,17},{17,25},{25,1},{2,10},{10... | collective-permute-start | bytes 1572872 | tf_op jit(solution)/shard_map/ppermute | solution.py:215
  66.3 1.9 %copy-start.6 = (bf16[2,256,512]{2,1,0:T(8,128)(2,1)}, bf16[2,256,512]{2,1,0:T(8,128)(2,1)S(1)}, u32[]{:S(2)}) copy-start(bf16[2,256,512]{2,1,0:T(8,128)(2,1)S(1)} %collective-permute-done.16.refs_2_) | copy-start | bytes 1572868
  66.4 1.9 %copy-start.5 = (bf16[2,256,512]{2,1,0:T(8,128)(2,1)}, bf16[2,256,512]{2,1,0:T(8,128)(2,1)S(1)}, u32[]{:S(2)}) copy-start(bf16[2,256,512]{2,1,0:T(8,128)(2,1)S(1)} %collective-permute-done.17.refs_3_) | copy-start | bytes 1572868
  66.4 8.4 %collective-permute-start.18 = (bf16[2,256,512]{2,1,0:T(8,128)(2,1)S(1)}, bf16[2,256,512]{2,1,0:T(8,128)(2,1)S(1)}, u32[]{:S(2)}, u32[]{:S(2)}) collective-permute-start(bf16[2,256,512]{2,1,0:T(8,128)(2,1)S(1)} %collective-permute-done.17.refs_3_), channel_id=1, source_target_pairs={{0,24},{8,0},{16,8},{24,16},{1,25},{9,1},{17,9},{25,17},{2,26},{10... | collective-permute-start | bytes 1572872 | tf_op jit(solution)/shard_map/ppermute | solution.py:215
  75.5 0.8 copy-start.9
  83.2 10.5 %collective-permute-start.19 = (f32[201,4,256]{2,1,0:T(4,128)}, f32[201,4,256]{2,1,0:T(4,128)S(1)}, u32[]{:S(2)}, u32[]{:S(2)}) collective-permute-start(f32[201,4,256]{2,1,0:T(4,128)} %get-tuple-element.62), channel_id=1, source_target_pairs={{0,1},{1,0},{2,3},{3,2},{4,5},{5,4},{6,7},{7,6},{8,9},{9,8},{10,11... | collective-permute-start | bytes 2469896 | tf_op jit(solution)/shard_map/ppermute | solution.py:215
  (3 other events, 2.1 us)

commit v5 on v4

--- a/solution.py
+++ b/solution.py
@@ -106,10 +106,10 @@
         lagged_ref[at * LAGPAD + 128 : (at + 1) * LAGPAD, :] = rolled[: LAGPAD - 128, :SAMP]
 
 
-def correlate_body(has_prev, is_last, *refs):
+def correlate_body(pieces, has_prev, is_last, *refs):
     refs = list(refs)
-    core_ref, src_ref, early_ref, late_ref = refs[:4]
-    refs = refs[4:]
+    core_ref, src_ref = refs[:2]
+    recv_refs, refs = refs[2 : 2 + pieces], refs[2 + pieces :]
     prev_ref = refs.pop(0) if has_prev else None
     if is_last:
         mine_ref, other_ref, acc_ref, first_ref, second_ref = refs
@@ -122,7 +122,9 @@
         acc_ref[...] = prev_ref[...] if has_prev else jnp.zeros(acc_ref.shape, jnp.float32)
 
     rows = src_ref[0].astype(jnp.float32)
-    receivers = jnp.where(window < PAIR, early_ref[0], late_ref[0])
+    receivers = recv_refs[-1][0]
+    for number in reversed(range(pieces - 1)):
+        receivers = jnp.where(window < PAIR * (number + 1), recv_refs[number][0], receivers)
     half = SRC_PAIR // 2
     for number, lagged_ref in enumerate((first_ref, second_ref)):
         fill_lagged(rows, number * half, lagged_ref)
@@ -139,23 +141,26 @@
                 other_ref[:, at, :] = acc_ref[(1 - core) * half + at, :NLAG, :]
 
 
-def correlate(sources, early, late, prev, core, is_last):
-    (early_x, early_z, early), (late_x, late_z, late) = early, late
-    local_width = early.shape[1]
+def correlate(sources, pieces, prev, core, is_last):
+    local_width = pieces[0][2].shape[1]
     acc_shape = (SRC_PAIR, LAGPAD, local_width)
     whole = lambda shape: pl.BlockSpec(shape, lambda w, core: (0,) * len(shape))
     half_shape = (NLAG, SRC_PAIR // 2, local_width)
 
     def source_at(w, core):
-        at_early, at_late = 4 * (early_z + w) + early_x, 4 * (late_z + w - PAIR) + late_x
-        return jnp.where(w < PAIR, at_early, at_late), 0, 0
-
-    in_specs = [
-        pl.BlockSpec((1, SRC_PAIR, SAMP), source_at),
-        pl.BlockSpec((1, local_width, SAMP), lambda w, core: (jnp.minimum(w, PAIR - 1), 0, 0)),
-        pl.BlockSpec((1, local_width, SAMP), lambda w, core: (jnp.maximum(w - PAIR, 0), 0, 0)),
-    ]
-    operands = [sources, early, late]
+        at = 0
+        for number, (x_back, z_at, _) in reversed(list(enumerate(pieces))):
+            here = 4 * (z_at + w - PAIR * number) + x_back
+            at = jnp.where(w < PAIR * (number + 1), here, at)
+        return at, 0, 0
+
+    def piece_at(number):
+        return lambda w, core: (jnp.clip(w - PAIR * number, 0, PAIR - 1), 0, 0)
+
+    in_specs = [pl.BlockSpec((1, SRC_PAIR, SAMP), source_at)]
+    for number in range(len(pieces)):
+        in_specs.append(pl.BlockSpec((1, local_width, SAMP), piece_at(number)))
+    operands = [sources] + [piece for _, _, piece in pieces]
     if prev is not None:
         in_specs.append(whole(acc_shape))
         operands.append(prev)
@@ -169,13 +174,13 @@
         out_shape = jax.ShapeDtypeStruct(acc_shape, jnp.float32)
 
     def body(*refs):
-        correlate_body(prev is not None, is_last, *refs)
+        correlate_body(len(pieces), prev is not None, is_last, *refs)
 
     return pl.pallas_call(
         body,
         grid_spec=pltpu.PrefetchScalarGridSpec(
             num_scalar_prefetch=1,
-            grid=(2 * PAIR,),
+            grid=(len(pieces) * PAIR,),
             in_specs=in_specs,
             out_specs=out_specs,
             scratch_shapes=scratch,
@@ -247,14 +252,14 @@
     dealt, high = lax.optimization_barrier((dealt, high))
     before_high, after_high = shifted(high, "x", 1), shifted(high, "x", -1)
     sources = jnp.concatenate([dealt[0], dealt[1], dealt[3], dealt[2]], axis=0)
-    total = correlate(sources, (0, 0, low), (0, 2, high), None, core, False)
-    total, before_low, after_low = lax.optimization_barrier((total, before_low, after_low))
+    sources, before_low, after_low = lax.optimization_barrier((sources, before_low, after_low))
     far_low = shifted(before_low, "x", 1)
-    total = correlate(sources, (1, 0, before_low), (3, 0, after_low), total, core, False)
+    near = [(0, 0, low), (0, 2, high), (1, 0, before_low), (3, 0, after_low)]
+    total = correlate(sources, near, None, core, False)
     total, before_high, after_high = lax.optimization_barrier((total, before_high, after_high))
     far_high = shifted(after_high, "x", -1)
-    total = correlate(sources, (1, 2, before_high), (3, 2, after_high), total, core, False)
-    total = correlate(sources, (2, 0, far_low), (2, 2, far_high), total, core, True)
+    total = correlate(sources, [(1, 2, before_high), (3, 2, after_high)], total, core, False)
+    total = correlate(sources, [(2, 0, far_low), (2, 2, far_high)], total, core, True)
     kept, passed = total
     got = shifted(passed, "core", 1)
     factor = 1.0 / math.sqrt(SAMP * size_x * size_z * 2)

time: 96.5 us -> 93.4 us (0.968)
  Pallas kernels: 31.5 us -> 28.9 us
  local copies, waits for them, and re-layouts: 4.49 us -> 2.38 us
  other arithmetic: 3.39 us -> 4.84 us
    pallas_call x4 -> x3, Pallas kernels: 25.4 us -> 22.7 us  [correlate(): pl.pallas_call(body, grid_spec=pltpu.PrefetchScalarGridSpec(num_scalar_pr...]
    unnamed x33 -> x26, local copies, waits for them, and re-layouts: 4.46 us -> 2.36 us
    concatenate x0 -> x1, other arithmetic: none -> 1.44 us  [shards(): sources = jnp.concatenate([dealt[0], dealt[1], dealt[3], dealt[2]], axis=0)]
  transfers between devices with their start and end apart: 20 -> 20, of which waited for: 7 -> 7; matrix products, arithmetic and copies ran while one was open for 1% -> 2% of each run, Pallas kernels for 23% -> 20%
where the time goes in v5:
time: 93.4 us; the launch traced here: 92.9 us
  starting transfers between devices  43.4 us (46%)
  Pallas kernels  28.9 us (31%)
  waiting for transfers between devices  13.4 us (14%)
  other arithmetic  4.84 us (5%)
  local copies, waits for them, and re-layouts  2.38 us (3%)
    ppermute x17, starting transfers between devices, shifted(): lax.ppermute(value, axis, [(i, (i + by) % size) for i in range(size)])  36.7 us
    pallas_call x3, Pallas kernels, correlate(): pl.pallas_call(body, grid_spec=pltpu.PrefetchScalarGridSpec(num_scalar_pr...  22.7 us
    ppermute x17, waiting for transfers between devices, shifted(): lax.ppermute(value, axis, [(i, (i + by) % size) for i in range(size)])  7.08 us
    ppermute x3, starting transfers between devices, swap(): return lax.ppermute(value, 'chan', [(i, i ^ step) for i in range(chans)])  6.69 us
    ppermute x3, waiting for transfers between devices, swap(): return lax.ppermute(value, 'chan', [(i, i ^ step) for i in range(chans)])  6.28 us
    pallas_call x2, Pallas kernels, deal(): pl.pallas_call(deal_body, in_specs=[smem] + [vmem] * len(arrays), out_spe...  3.11 us
    pallas_call x1, Pallas kernels, prep(): pl.pallas_call(prep_body, in_specs=[smem, smem, vmem, vmem, vmem], out_sp...  3.01 us
    unnamed x26, local copies, waits for them, and re-layouts  2.36 us
  transfers between devices with their start and end apart: 20, of which 7 were waited for; matrix products, arithmetic and copies ran while one was open for 2% of the time, Pallas kernels for 20%

profile of v5, /device:TPU:1, one launch (start us, length us, event | category | flops | bytes accessed | tf_op | source)
XLA Modules:
  0.0 92.9 jit_solution(3049944022422487810)
XLA Ops:
  0.0 3.0 %prep.1 = (bf16[256,512]{1,0:T(8,128)(2,1)}, bf16[128,512]{1,0:T(8,128)(2,1)}) custom-call(s32[2]{0:T(128)} %blocks_ref.1, s32[1]{0:T(128)} %bitcast.3.chan_ref, bf16[256,512]{1,0:T(8,128)(2,1)} %bitcast.18, f32[1,65]{1,0:T(1,128)} %bitcast.21, s32[1,256]{1,0:T(1,128)} %counts_ref.1), custom_call_target="tpu_custom_call" | custom-call | tf_op jit(solution)/shard_map/prep/pallas_call | solution.py:83
  3.0 2.5 %collective-permute-start = (bf16[128,512]{1,0:T(8,128)(2,1)}, bf16[128,512]{1,0:T(8,128)(2,1)S(1)}, u32[]{:S(2)}, u32[]{:S(2)}) collective-permute-start(bf16[128,512]{1,0:T(8,128)(2,1)} %get-tuple-element.34), channel_id=1, source_target_pairs={{0,128},{32,160},{64,192},{96,224},{128,0},{160,32},{192,64},{224,... | collective-permute-start | bytes 393224 | tf_op jit(solution)/shard_map/ppermute | solution.py:233
  5.5 2.6 %collective-permute-done = bf16[128,512]{1,0:T(8,128)(2,1)S(1)} collective-permute-done((bf16[128,512]{1,0:T(8,128)(2,1)}, bf16[128,512]{1,0:T(8,128)(2,1)S(1)}, u32[]{:S(2)}, u32[]{:S(2)}) %collective-permute-start) | collective-permute-done | bytes 131104 | tf_op jit(solution)/shard_map/ppermute | solution.py:233
  8.0 0.9 %add.9 = bf16[128,512]{1,0:T(8,128)(2,1)S(1)} add(bf16[128,512]{1,0:T(8,128)(2,1)} %get-tuple-element.34, bf16[128,512]{1,0:T(8,128)(2,1)S(1)} %collective-permute-done) | non-fusion elementwise | flops 65536 | bytes 393216 | tf_op jit(solution)/shard_map/add | solution.py:236
  9.0 3.7 %collective-permute-start.1 = (bf16[128,512]{1,0:T(8,128)(2,1)S(1)}, bf16[128,512]{1,0:T(8,128)(2,1)S(1)}, u32[]{:S(2)}, u32[]{:S(2)}) collective-permute-start(bf16[128,512]{1,0:T(8,128)(2,1)S(1)} %add.9), channel_id=1, source_target_pairs={{0,64},{32,96},{64,0},{96,32},{128,192},{160,224},{192,128},{224,1... | collective-permute-start | bytes 393224 | tf_op jit(solution)/shard_map/ppermute | solution.py:233
  12.7 3.0 %collective-permute-start.6 = (bf16[256,512]{1,0:T(8,128)(2,1)}, bf16[256,512]{1,0:T(8,128)(2,1)S(1)}, u32[]{:S(2)}, u32[]{:S(2)}) collective-permute-start(bf16[256,512]{1,0:T(8,128)(2,1)} %get-tuple-element.39), channel_id=1, source_target_pairs={{0,2},{2,4},{4,6},{6,0},{1,3},{3,5},{5,7},{7,1},{8,10},{10,12},{12... | collective-permute-start | bytes 786440 | tf_op jit(solution)/shard_map/ppermute | solution.py:220
  15.7 2.7 %collective-permute-start.7 = (bf16[256,512]{1,0:T(8,128)(2,1)}, bf16[256,512]{1,0:T(8,128)(2,1)S(1)}, u32[]{:S(2)}, u32[]{:S(2)}) collective-permute-start(bf16[256,512]{1,0:T(8,128)(2,1)} %get-tuple-element.39), channel_id=1, source_target_pairs={{0,6},{2,0},{4,2},{6,4},{1,7},{3,1},{5,3},{7,5},{8,14},{10,8},{12,... | collective-permute-start | bytes 786440 | tf_op jit(solution)/shard_map/ppermute | solution.py:220
  18.9 3.7 %collective-permute-done.2 = bf16[128,512]{1,0:T(8,128)(2,1)S(1)} collective-permute-done((bf16[128,512]{1,0:T(8,128)(2,1)S(1)}, bf16[128,512]{1,0:T(8,128)(2,1)S(1)}, u32[]{:S(2)}, u32[]{:S(2)}) %collective-permute-start.2) | collective-permute-done | bytes 131104 | tf_op jit(solution)/shard_map/ppermute | solution.py:233
  23.3 1.6 %deal.2 = (bf16[4,8,512]{2,1,0:T(8,128)(2,1)}, bf16[4,8,512]{2,1,0:T(8,128)(2,1)}, bf16[4,8,512]{2,1,0:T(8,128)(2,1)}, bf16[4,8,512]{2,1,0:T(8,128)(2,1)}) custom-call(s32[1]{0:T(128)} %bitcast.2.at_ref, bf16[4,4,8,512]{3,2,1,0:T(8,128)(2,1)} %bitcast.17, bf16[4,4,8,512]{3,2,1,0:T(8,128)(2,1)} %bitcast.20), custom_call_target="tpu_custom_call" | custom-call | tf_op jit(solution)/shard_map/deal/pallas_call | solution.py:209
  24.9 1.2 %collective-permute-start.3 = (bf16[4,8,512]{2,1,0:T(8,128)(2,1)}, bf16[4,8,512]{2,1,0:T(8,128)(2,1)S(1)}, u32[]{:S(2)}, u32[]{:S(2)}) collective-permute-start(bf16[4,8,512]{2,1,0:T(8,128)(2,1)} %get-tuple-element.36), channel_id=1, source_target_pairs={{0,8},{8,16},{16,24},{24,0},{1,9},{9,17},{17,25},{25,1},{2,10},{10... | collective-permute-start | bytes 98312 | tf_op jit(solution)/shard_map/ppermute | solution.py:220
  26.1 2.4 %collective-permute-start.4 = (bf16[4,8,512]{2,1,0:T(8,128)(2,1)}, bf16[4,8,512]{2,1,0:T(8,128)(2,1)S(1)}, u32[]{:S(2)}, u32[]{:S(2)}) collective-permute-start(bf16[4,8,512]{2,1,0:T(8,128)(2,1)} %get-tuple-element.37), channel_id=1, source_target_pairs={{0,16},{8,24},{16,0},{24,8},{1,17},{9,25},{17,1},{25,9},{2,18},{10... | collective-permute-start | bytes 98312 | tf_op jit(solution)/shard_map/ppermute | solution.py:220
  28.6 1.2 %collective-permute-start.5 = (bf16[4,8,512]{2,1,0:T(8,128)(2,1)}, bf16[4,8,512]{2,1,0:T(8,128)(2,1)S(1)}, u32[]{:S(2)}, u32[]{:S(2)}) collective-permute-start(bf16[4,8,512]{2,1,0:T(8,128)(2,1)} %get-tuple-element.38), channel_id=1, source_target_pairs={{0,24},{8,0},{16,8},{24,16},{1,25},{9,1},{17,9},{25,17},{2,26},{10... | collective-permute-start | bytes 98312 | tf_op jit(solution)/shard_map/ppermute | solution.py:220
  29.7 1.9 %collective-permute-done.7 = bf16[256,512]{1,0:T(8,128)(2,1)S(1)} collective-permute-done((bf16[256,512]{1,0:T(8,128)(2,1)}, bf16[256,512]{1,0:T(8,128)(2,1)S(1)}, u32[]{:S(2)}, u32[]{:S(2)}) %collective-permute-start.7) | collective-permute-done | bytes 262176 | tf_op jit(solution)/shard_map/ppermute | solution.py:220
  31.9 2.5 %collective-permute-start.11 = (bf16[128,512]{1,0:T(8,128)(2,1)S(1)}, bf16[128,512]{1,0:T(8,128)(2,1)S(1)}, u32[]{:S(2)}, u32[]{:S(2)}) collective-permute-start(bf16[128,512]{1,0:T(8,128)(2,1)S(1)} %slice.6), channel_id=1, source_target_pairs={{0,2},{2,4},{4,6},{6,0},{1,3},{3,5},{5,7},{7,1},{8,10},{10,12},{12... | collective-permute-start | bytes 393224 | tf_op jit(solution)/shard_map/ppermute | solution.py:220
  34.4 1.2 %collective-permute-start.12 = (bf16[128,512]{1,0:T(8,128)(2,1)S(1)}, bf16[128,512]{1,0:T(8,128)(2,1)S(1)}, u32[]{:S(2)}, u32[]{:S(2)}) collective-permute-start(bf16[128,512]{1,0:T(8,128)(2,1)S(1)} %slice.7), channel_id=1, source_target_pairs={{0,6},{2,0},{4,2},{6,4},{1,7},{3,1},{5,3},{7,5},{8,14},{10,8},{12,... | collective-permute-start | bytes 393224 | tf_op jit(solution)/shard_map/ppermute | solution.py:220
  35.7 1.1 %collective-permute-start.13 = (bf16[2,256,512]{2,1,0:T(8,128)(2,1)S(1)}, bf16[2,256,512]{2,1,0:T(8,128)(2,1)S(1)}, u32[]{:S(2)}, u32[]{:S(2)}) collective-permute-start(bf16[2,256,512]{2,1,0:T(8,128)(2,1)S(1)} %pad_maximum_fusion.1.refs_2_), channel_id=1, source_target_pairs={{0,8},{8,16},{16,24},{24,0},{1,9},{9,17},{17,25},{25,1},{2,10},{10... | collective-permute-start | bytes 1572872 | tf_op jit(solution)/shard_map/ppermute | solution.py:220
  36.8 1.6 %collective-permute-start.14 = (bf16[2,256,512]{2,1,0:T(8,128)(2,1)S(1)}, bf16[2,256,512]{2,1,0:T(8,128)(2,1)S(1)}, u32[]{:S(2)}, u32[]{:S(2)}) collective-permute-start(bf16[2,256,512]{2,1,0:T(8,128)(2,1)S(1)} %pad_maximum_fusion.1.refs_2_), channel_id=1, source_target_pairs={{0,24},{8,0},{16,8},{24,16},{1,25},{9,1},{17,9},{25,17},{2,26},{10... | collective-permute-start | bytes 1572872 | tf_op jit(solution)/shard_map/ppermute | solution.py:220
  38.4 1.5 %deal.3 = (bf16[4,8,512]{2,1,0:T(8,128)(2,1)}, bf16[4,8,512]{2,1,0:T(8,128)(2,1)}, bf16[4,8,512]{2,1,0:T(8,128)(2,1)}, bf16[4,8,512]{2,1,0:T(8,128)(2,1)}) custom-call(s32[1]{0:T(128)} %bitcast.1.at_ref, bf16[4,8,512]{2,1,0:T(8,128)(2,1)} %get-tuple-element.40.refs_0_, bf16[4,8,512]{2,1,0:T(8,128)(2,1)} %copy-done.10, bf16[4,8,512]{2,1,0:T(8,128)(2,1)} %copy-done.11, ...), custom_call_target="tpu_custom_call" | custom-call | tf_op jit(solution)/shard_map/deal/pallas_call | solution.py:209
  39.9 1.2 %collective-permute-start.10 = (bf16[4,8,512]{2,1,0:T(8,128)(2,1)}, bf16[4,8,512]{2,1,0:T(8,128)(2,1)S(1)}, u32[]{:S(2)}, u32[]{:S(2)}) collective-permute-start(bf16[4,8,512]{2,1,0:T(8,128)(2,1)} %get-tuple-element.47), channel_id=1, source_target_pairs={{0,6},{2,0},{4,2},{6,4},{1,7},{3,1},{5,3},{7,5},{8,14},{10,8},{12,... | collective-permute-start | bytes 98312 | tf_op jit(solution)/shard_map/ppermute | solution.py:220
  41.1 1.2 %collective-permute-start.8 = (bf16[4,8,512]{2,1,0:T(8,128)(2,1)}, bf16[4,8,512]{2,1,0:T(8,128)(2,1)S(1)}, u32[]{:S(2)}, u32[]{:S(2)}) collective-permute-start(bf16[4,8,512]{2,1,0:T(8,128)(2,1)} %get-tuple-element.45), channel_id=1, source_target_pairs={{0,2},{2,4},{4,6},{6,0},{1,3},{3,5},{5,7},{7,1},{8,10},{10,12},{12... | collective-permute-start | bytes 98312 | tf_op jit(solution)/shard_map/ppermute | solution.py:220
  42.3 4.2 %collective-permute-start.9 = (bf16[4,8,512]{2,1,0:T(8,128)(2,1)}, bf16[4,8,512]{2,1,0:T(8,128)(2,1)S(1)}, u32[]{:S(2)}, u32[]{:S(2)}) collective-permute-start(bf16[4,8,512]{2,1,0:T(8,128)(2,1)} %get-tuple-element.46), channel_id=1, source_target_pairs={{0,4},{2,6},{4,0},{6,2},{1,5},{3,7},{5,1},{7,3},{8,12},{10,14},{12... | collective-permute-start | bytes 98312 | tf_op jit(solution)/shard_map/ppermute | solution.py:220
  46.6 2.6 %collective-permute-done.9 = bf16[4,8,512]{2,1,0:T(8,128)(2,1)S(1)} collective-permute-done((bf16[4,8,512]{2,1,0:T(8,128)(2,1)}, bf16[4,8,512]{2,1,0:T(8,128)(2,1)S(1)}, u32[]{:S(2)}, u32[]{:S(2)}) %collective-permute-start.9) | collective-permute-done | bytes 32800 | tf_op jit(solution)/shard_map/ppermute | solution.py:220
  49.2 2.7 %collective-permute-start.17 = (bf16[2,256,512]{2,1,0:T(8,128)(2,1)S(1)}, bf16[2,256,512]{2,1,0:T(8,128)(2,1)S(1)}, u32[]{:S(2)}, u32[]{:S(2)}) collective-permute-start(bf16[2,256,512]{2,1,0:T(8,128)(2,1)S(1)} %pad_maximum_fusion.refs_3_), channel_id=1, source_target_pairs={{0,24},{8,0},{16,8},{24,16},{1,25},{9,1},{17,9},{25,17},{2,26},{10... | collective-permute-start | bytes 1572872 | tf_op jit(solution)/shard_map/ppermute | solution.py:220
  51.8 1.4 %pad_maximum_fusion.2.refs_1_ = bf16[16,8,512]{2,1,0:T(8,128)(2,1)} fusion(bf16[4,8,512]{2,1,0:T(8,128)(2,1)S(1)} %collective-permute-done.9, bf16[4,8,512]{2,1,0:T(8,128)(2,1)S(1)} %collective-permute-done.10, bf16[4,8,512]{2,1,0:T(8,128)(2,1)S(1)} %collective-permute-done.8, bf16[4,8,512]{2,1,0:T(8,128)(2,1)} %get-tuple-element.50), kind=kLoop, calls=%fused_computation.4 | loop fusion | flops 196608 | bytes 262144 | tf_op jit(solution)/shard_map/concatenate | solution.py:254
  54.3 9.4 %correlate.3.refs_4_ = f32[8,208,256]{2,1,0:T(8,128)} custom-call(s32[1]{0:T(128)} %bitcast.refs_0_, bf16[16,8,512]{2,1,0:T(8,128)(2,1)} %pad_maximum_fusion.2.refs_1_, bf16[2,256,512]{2,1,0:T(8,128)(2,1)} %copy-done, bf16[2,256,512]{2,1,0:T(8,128)(2,1)} %copy-done.1, bf16[2,256,512]{2,1,0:T(8,128)(2,1)} %copy-done.2, bf16[2,256,512]{2,1,0:T(8,128)(2,1)} %copy-done.3), custom_call_target="tpu_custom_call" | custom-call | tf_op jit(solution)/shard_map/correlate/pallas_call | solution.py:179
  63.8 1.9 %collective-permute-start.18 = (bf16[2,256,512]{2,1,0:T(8,128)(2,1)S(1)}, bf16[2,256,512]{2,1,0:T(8,128)(2,1)S(1)}, u32[]{:S(2)}, u32[]{:S(2)}) collective-permute-start(bf16[2,256,512]{2,1,0:T(8,128)(2,1)S(1)} %collective-permute-done.17.refs_3_), channel_id=1, source_target_pairs={{0,24},{8,0},{16,8},{24,16},{1,25},{9,1},{17,9},{25,17},{2,26},{10... | collective-permute-start | bytes 1572872 | tf_op jit(solution)/shard_map/ppermute | solution.py:220
  65.7 6.4 %correlate.4.refs_4_ = f32[8,208,256]{2,1,0:T(8,128)} custom-call(s32[1]{0:T(128)} %bitcast.refs_0_, bf16[16,8,512]{2,1,0:T(8,128)(2,1)} %pad_maximum_fusion.2.refs_1_, bf16[2,256,512]{2,1,0:T(8,128)(2,1)} %copy-done.5, bf16[2,256,512]{2,1,0:T(8,128)(2,1)} %copy-done.4, f32[8,208,256]{2,1,0:T(8,128)} %correlate.3.refs_4_), custom_call_target="tpu_custom_call" | custom-call | tf_op jit(solution)/shard_map/correlate/pallas_call | solution.py:179
  72.3 0.8 copy-done.7
  73.1 6.9 %correlate.5 = (f32[201,4,256]{2,1,0:T(4,128)}, f32[201,4,256]{2,1,0:T(4,128)}) custom-call(s32[1]{0:T(128)} %bitcast.refs_0_, bf16[16,8,512]{2,1,0:T(8,128)(2,1)} %pad_maximum_fusion.2.refs_1_, bf16[2,256,512]{2,1,0:T(8,128)(2,1)} %collective-permute-done.15.refs_2_, bf16[2,256,512]{2,1,0:T(8,128)(2,1)} %copy-done.7, f32[8,208,256]{2,1,0:T(8,128)} %correlate.4.refs_4_), custom_call_target="tpu_custom_call" | custom-call | tf_op jit(solution)/shard_map/correlate/pallas_call | solution.py:179
  79.9 8.5 %collective-permute-start.19 = (f32[201,4,256]{2,1,0:T(4,128)}, f32[201,4,256]{2,1,0:T(4,128)S(1)}, u32[]{:S(2)}, u32[]{:S(2)}) collective-permute-start(f32[201,4,256]{2,1,0:T(4,128)} %get-tuple-element.62), channel_id=1, source_target_pairs={{0,1},{1,0},{2,3},{3,2},{4,5},{5,4},{6,7},{7,6},{8,9},{9,8},{10,11... | collective-permute-start | bytes 2469896 | tf_op jit(solution)/shard_map/ppermute | solution.py:220
  88.5 2.2 %collective-permute-done.19 = f32[201,4,256]{2,1,0:T(4,128)S(1)} collective-permute-done((f32[201,4,256]{2,1,0:T(4,128)}, f32[201,4,256]{2,1,0:T(4,128)S(1)}, u32[]{:S(2)}, u32[]{:S(2)}) %collective-permute-start.19) | collective-permute-done | bytes 823328 | tf_op jit(solution)/shard_map/ppermute | solution.py:220
  90.6 2.3 %multiply_bitcast_fusion = f32[4,201,256]{2,0,1:T(4,128)} fusion(f32[201,4,256]{2,1,0:T(4,128)} %get-tuple-element.61, f32[201,4,256]{2,1,0:T(4,128)S(1)} %collective-permute-done.19), kind=kLoop, calls=%fused_computation | loop fusion | flops 411648 | bytes 2469888 | tf_op jit(solution)/shard_map/transpose | solution.py:266
  (49 shorter events, 2.7 us)
Async XLA Ops:
  3.0 32.6 %copy-start.8 = (bf16[256,512]{1,0:T(8,128)(2,1)S(1)}, bf16[256,512]{1,0:T(8,128)(2,1)}, u32[]{:S(2)}) copy-start(bf16[256,512]{1,0:T(8,128)(2,1)} %get-tuple-element.39) | copy-start | bytes 786436
  3.0 5.0 %collective-permute-start = (bf16[128,512]{1,0:T(8,128)(2,1)}, bf16[128,512]{1,0:T(8,128)(2,1)S(1)}, u32[]{:S(2)}, u32[]{:S(2)}) collective-permute-start(bf16[128,512]{1,0:T(8,128)(2,1)} %get-tuple-element.34), channel_id=1, source_target_pairs={{0,128},{32,160},{64,192},{96,224},{128,0},{160,32},{192,64},{224,... | collective-permute-start | bytes 393224 | tf_op jit(solution)/shard_map/ppermute | solution.py:233
  9.0 9.4 %collective-permute-start.1 = (bf16[128,512]{1,0:T(8,128)(2,1)S(1)}, bf16[128,512]{1,0:T(8,128)(2,1)S(1)}, u32[]{:S(2)}, u32[]{:S(2)}) collective-permute-start(bf16[128,512]{1,0:T(8,128)(2,1)S(1)} %add.9), channel_id=1, source_target_pairs={{0,64},{32,96},{64,0},{96,32},{128,192},{160,224},{192,128},{224,1... | collective-permute-start | bytes 393224 | tf_op jit(solution)/shard_map/ppermute | solution.py:233
  12.7 17.0 %collective-permute-start.6 = (bf16[256,512]{1,0:T(8,128)(2,1)}, bf16[256,512]{1,0:T(8,128)(2,1)S(1)}, u32[]{:S(2)}, u32[]{:S(2)}) collective-permute-start(bf16[256,512]{1,0:T(8,128)(2,1)} %get-tuple-element.39), channel_id=1, source_target_pairs={{0,2},{2,4},{4,6},{6,0},{1,3},{3,5},{5,7},{7,1},{8,10},{10,12},{12... | collective-permute-start | bytes 786440 | tf_op jit(solution)/shard_map/ppermute | solution.py:220
  15.7 15.9 %collective-permute-start.7 = (bf16[256,512]{1,0:T(8,128)(2,1)}, bf16[256,512]{1,0:T(8,128)(2,1)S(1)}, u32[]{:S(2)}, u32[]{:S(2)}) collective-permute-start(bf16[256,512]{1,0:T(8,128)(2,1)} %get-tuple-element.39), channel_id=1, source_target_pairs={{0,6},{2,0},{4,2},{6,4},{1,7},{3,1},{5,3},{7,5},{8,14},{10,8},{12,... | collective-permute-start | bytes 786440 | tf_op jit(solution)/shard_map/ppermute | solution.py:220
  18.4 4.2 %copy-start.6 = (bf16[128,512]{1,0:T(8,128)(2,1)}, bf16[128,512]{1,0:T(8,128)(2,1)S(1)}, u32[]{:S(2)}) copy-start(bf16[128,512]{1,0:T(8,128)(2,1)S(1)} %add.10) | copy-start | bytes 393220
  18.4 4.2 %collective-permute-start.2 = (bf16[128,512]{1,0:T(8,128)(2,1)S(1)}, bf16[128,512]{1,0:T(8,128)(2,1)S(1)}, u32[]{:S(2)}, u32[]{:S(2)}) collective-permute-start(bf16[128,512]{1,0:T(8,128)(2,1)S(1)} %add.10), channel_id=1, source_target_pairs={{0,32},{32,0},{64,96},{96,64},{128,160},{160,128},{192,224},{224,1... | collective-permute-start | bytes 393224 | tf_op jit(solution)/shard_map/ppermute | solution.py:233
  24.9 6.7 %collective-permute-start.3 = (bf16[4,8,512]{2,1,0:T(8,128)(2,1)}, bf16[4,8,512]{2,1,0:T(8,128)(2,1)S(1)}, u32[]{:S(2)}, u32[]{:S(2)}) collective-permute-start(bf16[4,8,512]{2,1,0:T(8,128)(2,1)} %get-tuple-element.36), channel_id=1, source_target_pairs={{0,8},{8,16},{16,24},{24,0},{1,9},{9,17},{17,25},{25,1},{2,10},{10... | collective-permute-start | bytes 98312 | tf_op jit(solution)/shard_map/ppermute | solution.py:220
  26.1 5.5 %collective-permute-start.4 = (bf16[4,8,512]{2,1,0:T(8,128)(2,1)}, bf16[4,8,512]{2,1,0:T(8,128)(2,1)S(1)}, u32[]{:S(2)}, u32[]{:S(2)}) collective-permute-start(bf16[4,8,512]{2,1,0:T(8,128)(2,1)} %get-tuple-element.37), channel_id=1, source_target_pairs={{0,16},{8,24},{16,0},{24,8},{1,17},{9,25},{17,1},{25,9},{2,18},{10... | collective-permute-start | bytes 98312 | tf_op jit(solution)/shard_map/ppermute | solution.py:220
  28.6 3.3 %collective-permute-start.5 = (bf16[4,8,512]{2,1,0:T(8,128)(2,1)}, bf16[4,8,512]{2,1,0:T(8,128)(2,1)S(1)}, u32[]{:S(2)}, u32[]{:S(2)}) collective-permute-start(bf16[4,8,512]{2,1,0:T(8,128)(2,1)} %get-tuple-element.38), channel_id=1, source_target_pairs={{0,24},{8,0},{16,8},{24,16},{1,25},{9,1},{17,9},{25,17},{2,26},{10... | collective-permute-start | bytes 98312 | tf_op jit(solution)/shard_map/ppermute | solution.py:220
  31.6 6.8 %copy-start.10 = (bf16[4,8,512]{2,1,0:T(8,128)(2,1)}, bf16[4,8,512]{2,1,0:T(8,128)(2,1)S(1)}, u32[]{:S(2)}) copy-start(bf16[4,8,512]{2,1,0:T(8,128)(2,1)S(1)} %collective-permute-done.3.refs_1_) | copy-start | bytes 98308
  31.6 6.8 %copy-start.11 = (bf16[4,8,512]{2,1,0:T(8,128)(2,1)}, bf16[4,8,512]{2,1,0:T(8,128)(2,1)S(1)}, u32[]{:S(2)}) copy-start(bf16[4,8,512]{2,1,0:T(8,128)(2,1)S(1)} %collective-permute-done.4.refs_2_) | copy-start | bytes 98308
  31.8 6.6 %copy-start.12 = (bf16[4,8,512]{2,1,0:T(8,128)(2,1)}, bf16[4,8,512]{2,1,0:T(8,128)(2,1)S(1)}, u32[]{:S(2)}) copy-start(bf16[4,8,512]{2,1,0:T(8,128)(2,1)S(1)} %collective-permute-done.5.refs_3_) | copy-start | bytes 98308
  31.9 9.2 %collective-permute-start.11 = (bf16[128,512]{1,0:T(8,128)(2,1)S(1)}, bf16[128,512]{1,0:T(8,128)(2,1)S(1)}, u32[]{:S(2)}, u32[]{:S(2)}) collective-permute-start(bf16[128,512]{1,0:T(8,128)(2,1)S(1)} %slice.6), channel_id=1, source_target_pairs={{0,2},{2,4},{4,6},{6,0},{1,3},{3,5},{5,7},{7,1},{8,10},{10,12},{12... | collective-permute-start | bytes 393224 | tf_op jit(solution)/shard_map/ppermute | solution.py:220
  34.4 7.9 %collective-permute-start.12 = (bf16[128,512]{1,0:T(8,128)(2,1)S(1)}, bf16[128,512]{1,0:T(8,128)(2,1)S(1)}, u32[]{:S(2)}, u32[]{:S(2)}) collective-permute-start(bf16[128,512]{1,0:T(8,128)(2,1)S(1)} %slice.7), channel_id=1, source_target_pairs={{0,6},{2,0},{4,2},{6,4},{1,7},{3,1},{5,3},{7,5},{8,14},{10,8},{12,... | collective-permute-start | bytes 393224 | tf_op jit(solution)/shard_map/ppermute | solution.py:220
  35.7 17.7 %copy-start = (bf16[2,256,512]{2,1,0:T(8,128)(2,1)}, bf16[2,256,512]{2,1,0:T(8,128)(2,1)S(1)}, u32[]{:S(2)}) copy-start(bf16[2,256,512]{2,1,0:T(8,128)(2,1)S(1)} %pad_maximum_fusion.1.refs_2_) | copy-start | bytes 1572868
  35.7 17.6 %collective-permute-start.13 = (bf16[2,256,512]{2,1,0:T(8,128)(2,1)S(1)}, bf16[2,256,512]{2,1,0:T(8,128)(2,1)S(1)}, u32[]{:S(2)}, u32[]{:S(2)}) collective-permute-start(bf16[2,256,512]{2,1,0:T(8,128)(2,1)S(1)} %pad_maximum_fusion.1.refs_2_), channel_id=1, source_target_pairs={{0,8},{8,16},{16,24},{24,0},{1,9},{9,17},{17,25},{25,1},{2,10},{10... | collective-permute-start | bytes 1572872 | tf_op jit(solution)/shard_map/ppermute | solution.py:220
  36.8 16.5 %collective-permute-start.14 = (bf16[2,256,512]{2,1,0:T(8,128)(2,1)S(1)}, bf16[2,256,512]{2,1,0:T(8,128)(2,1)S(1)}, u32[]{:S(2)}, u32[]{:S(2)}) collective-permute-start(bf16[2,256,512]{2,1,0:T(8,128)(2,1)S(1)} %pad_maximum_fusion.1.refs_2_), channel_id=1, source_target_pairs={{0,24},{8,0},{16,8},{24,16},{1,25},{9,1},{17,9},{25,17},{2,26},{10... | collective-permute-start | bytes 1572872 | tf_op jit(solution)/shard_map/ppermute | solution.py:220
  39.9 6.6 %collective-permute-start.10 = (bf16[4,8,512]{2,1,0:T(8,128)(2,1)}, bf16[4,8,512]{2,1,0:T(8,128)(2,1)S(1)}, u32[]{:S(2)}, u32[]{:S(2)}) collective-permute-start(bf16[4,8,512]{2,1,0:T(8,128)(2,1)} %get-tuple-element.47), channel_id=1, source_target_pairs={{0,6},{2,0},{4,2},{6,4},{1,7},{3,1},{5,3},{7,5},{8,14},{10,8},{12,... | collective-permute-start | bytes 98312 | tf_op jit(solution)/shard_map/ppermute | solution.py:220
  41.1 5.4 %collective-permute-start.8 = (bf16[4,8,512]{2,1,0:T(8,128)(2,1)}, bf16[4,8,512]{2,1,0:T(8,128)(2,1)S(1)}, u32[]{:S(2)}, u32[]{:S(2)}) collective-permute-start(bf16[4,8,512]{2,1,0:T(8,128)(2,1)} %get-tuple-element.45), channel_id=1, source_target_pairs={{0,2},{2,4},{4,6},{6,0},{1,3},{3,5},{5,7},{7,1},{8,10},{10,12},{12... | collective-permute-start | bytes 98312 | tf_op jit(solution)/shard_map/ppermute | solution.py:220
  42.3 6.9 %collective-permute-start.9 = (bf16[4,8,512]{2,1,0:T(8,128)(2,1)}, bf16[4,8,512]{2,1,0:T(8,128)(2,1)S(1)}, u32[]{:S(2)}, u32[]{:S(2)}) collective-permute-start(bf16[4,8,512]{2,1,0:T(8,128)(2,1)} %get-tuple-element.46), channel_id=1, source_target_pairs={{0,4},{2,6},{4,0},{6,2},{1,5},{3,7},{5,1},{7,3},{8,12},{10,14},{12... | collective-permute-start | bytes 98312 | tf_op jit(solution)/shard_map/ppermute | solution.py:220
  46.5 6.9 %copy-start.1 = (bf16[2,256,512]{2,1,0:T(8,128)(2,1)}, bf16[2,256,512]{2,1,0:T(8,128)(2,1)S(1)}, u32[]{:S(2)}) copy-start(bf16[2,256,512]{2,1,0:T(8,128)(2,1)S(1)} %pad_maximum_fusion.refs_3_) | copy-start | bytes 1572868
  49.2 14.6 %collective-permute-start.16 = (bf16[2,256,512]{2,1,0:T(8,128)(2,1)S(1)}, bf16[2,256,512]{2,1,0:T(8,128)(2,1)S(1)}, u32[]{:S(2)}, u32[]{:S(2)}) collective-permute-start(bf16[2,256,512]{2,1,0:T(8,128)(2,1)S(1)} %pad_maximum_fusion.refs_3_), channel_id=1, source_target_pairs={{0,8},{8,16},{16,24},{24,0},{1,9},{9,17},{17,25},{25,1},{2,10},{10... | collective-permute-start | bytes 1572872 | tf_op jit(solution)/shard_map/ppermute | solution.py:220
  49.2 14.6 %collective-permute-start.17 = (bf16[2,256,512]{2,1,0:T(8,128)(2,1)S(1)}, bf16[2,256,512]{2,1,0:T(8,128)(2,1)S(1)}, u32[]{:S(2)}, u32[]{:S(2)}) collective-permute-start(bf16[2,256,512]{2,1,0:T(8,128)(2,1)S(1)} %pad_maximum_fusion.refs_3_), channel_id=1, source_target_pairs={{0,24},{8,0},{16,8},{24,16},{1,25},{9,1},{17,9},{25,17},{2,26},{10... | collective-permute-start | bytes 1572872 | tf_op jit(solution)/shard_map/ppermute | solution.py:220
  53.3 0.8 copy-start.2
  53.3 1.0 %copy-start.3 = (bf16[2,256,512]{2,1,0:T(8,128)(2,1)}, bf16[2,256,512]{2,1,0:T(8,128)(2,1)S(1)}, u32[]{:S(2)}) copy-start(bf16[2,256,512]{2,1,0:T(8,128)(2,1)S(1)} %collective-permute-done.14.refs_5_) | copy-start | bytes 1572868
  53.3 18.8 %collective-permute-start.15 = (bf16[2,256,512]{2,1,0:T(8,128)(2,1)S(1)}, bf16[2,256,512]{2,1,0:T(8,128)(2,1)}, u32[]{:S(2)}, u32[]{:S(2)}) collective-permute-start(bf16[2,256,512]{2,1,0:T(8,128)(2,1)S(1)} %collective-permute-done.13.refs_4_), channel_id=1, source_target_pairs={{0,8},{8,16},{16,24},{24,0},{1,9},{9,17},{17,25},{25,1},{2,10},{10... | collective-permute-start | bytes 1572872 | tf_op jit(solution)/shard_map/ppermute | solution.py:220
  63.7 1.9 %copy-start.5 = (bf16[2,256,512]{2,1,0:T(8,128)(2,1)}, bf16[2,256,512]{2,1,0:T(8,128)(2,1)S(1)}, u32[]{:S(2)}) copy-start(bf16[2,256,512]{2,1,0:T(8,128)(2,1)S(1)} %collective-permute-done.16.refs_2_) | copy-start | bytes 1572868
  63.8 1.9 %copy-start.4 = (bf16[2,256,512]{2,1,0:T(8,128)(2,1)}, bf16[2,256,512]{2,1,0:T(8,128)(2,1)S(1)}, u32[]{:S(2)}) copy-start(bf16[2,256,512]{2,1,0:T(8,128)(2,1)S(1)} %collective-permute-done.17.refs_3_) | copy-start | bytes 1572868
  63.8 8.5 %collective-permute-start.18 = (bf16[2,256,512]{2,1,0:T(8,128)(2,1)S(1)}, bf16[2,256,512]{2,1,0:T(8,128)(2,1)S(1)}, u32[]{:S(2)}, u32[]{:S(2)}) collective-permute-start(bf16[2,256,512]{2,1,0:T(8,128)(2,1)S(1)} %collective-permute-done.17.refs_3_), channel_id=1, source_target_pairs={{0,24},{8,0},{16,8},{24,16},{1,25},{9,1},{17,9},{25,17},{2,26},{10... | collective-permute-start | bytes 1572872 | tf_op jit(solution)/shard_map/ppermute | solution.py:220
  72.3 0.8 copy-start.7
  79.9 10.7 %collective-permute-start.19 = (f32[201,4,256]{2,1,0:T(4,128)}, f32[201,4,256]{2,1,0:T(4,128)S(1)}, u32[]{:S(2)}, u32[]{:S(2)}) collective-permute-start(f32[201,4,256]{2,1,0:T(4,128)} %get-tuple-element.62), channel_id=1, source_target_pairs={{0,1},{1,0},{2,3},{3,2},{4,5},{5,4},{6,7},{7,6},{8,9},{9,8},{10,11... | collective-permute-start | bytes 2469896 | tf_op jit(solution)/shard_map/ppermute | solution.py:220
  (1 other events, 0.7 us)

commit v6 on v5

--- a/solution.py
+++ b/solution.py
@@ -108,8 +108,8 @@
 
 def correlate_body(pieces, has_prev, is_last, *refs):
     refs = list(refs)
-    core_ref, src_ref = refs[:2]
-    recv_refs, refs = refs[2 : 2 + pieces], refs[2 + pieces :]
+    _, core_ref, src_ref = refs[:3]
+    recv_refs, refs = refs[3 : 3 + pieces], refs[3 + pieces :]
     prev_ref = refs.pop(0) if has_prev else None
     if is_last:
         mine_ref, other_ref, acc_ref, first_ref, second_ref = refs
@@ -141,21 +141,21 @@
                 other_ref[:, at, :] = acc_ref[(1 - core) * half + at, :NLAG, :]
 
 
-def correlate(sources, pieces, prev, core, is_last):
+def correlate(table, sources, pieces, prev, core, is_last):
     local_width = pieces[0][2].shape[1]
     acc_shape = (SRC_PAIR, LAGPAD, local_width)
-    whole = lambda shape: pl.BlockSpec(shape, lambda w, core: (0,) * len(shape))
+    whole = lambda shape: pl.BlockSpec(shape, lambda w, table, core: (0,) * len(shape))
     half_shape = (NLAG, SRC_PAIR // 2, local_width)
 
-    def source_at(w, core):
+    def source_at(w, table, core):
         at = 0
         for number, (x_back, z_at, _) in reversed(list(enumerate(pieces))):
             here = 4 * (z_at + w - PAIR * number) + x_back
             at = jnp.where(w < PAIR * (number + 1), here, at)
-        return at, 0, 0
+        return table[at], 0, 0
 
     def piece_at(number):
-        return lambda w, core: (jnp.clip(w - PAIR * number, 0, PAIR - 1), 0, 0)
+        return lambda w, table, core: (jnp.clip(w - PAIR * number, 0, PAIR - 1), 0, 0)
 
     in_specs = [pl.BlockSpec((1, SRC_PAIR, SAMP), source_at)]
     for number in range(len(pieces)):
@@ -179,7 +179,7 @@
     return pl.pallas_call(
         body,
         grid_spec=pltpu.PrefetchScalarGridSpec(
-            num_scalar_prefetch=1,
+            num_scalar_prefetch=2,
             grid=(len(pieces) * PAIR,),
             in_specs=in_specs,
             out_specs=out_specs,
@@ -187,32 +187,7 @@
         ),
         out_shape=out_shape,
         name="correlate",
-    )(core, *operands)
-
-
-def deal_body(at_ref, *refs):
-    at = at_ref[0]
-    in_refs, out_refs = refs[:-4], refs[-4:]
-    for by, out_ref in enumerate(out_refs):
-        picked = (at + by) & 3
-        if len(in_refs) == 2:
-            both = [ref[picked].astype(jnp.float32) for ref in in_refs]
-            out_ref[...] = (both[0] + both[1]).astype(jnp.bfloat16)
-        else:
-            for number, ref in enumerate(in_refs):
-                out_ref[number] = ref[picked]
-
-
-def deal(at, arrays):
-    smem = pl.BlockSpec(memory_space=pltpu.SMEM)
-    vmem = pl.BlockSpec(memory_space=pltpu.VMEM)
-    return pl.pallas_call(
-        deal_body,
-        in_specs=[smem] + [vmem] * len(arrays),
-        out_specs=[vmem] * 4,
-        out_shape=[jax.ShapeDtypeStruct((4, SRC_PAIR, SAMP), jnp.bfloat16)] * 4,
-        name="deal",
-    )(at, *arrays)
+    )(table, core, *operands)
 
 
 def shifted(value, axis, by):
@@ -237,29 +212,28 @@
     while step > 2:
         step //= 2
         mine = mine + swap(mine, step)
-    grouped = (size_x, size_z, SRC_PAIR, SAMP)
-    parts = [v.reshape(grouped) for v in (mine, swap(mine, step // 2))]
-    dealt = deal(at_x.reshape(1), parts)
-    dealt = [dealt[0]] + [shifted(dealt[by], "x", by) for by in range(1, 4)]
-    dealt, below, above = lax.optimization_barrier((dealt, below, above))
+    mine = mine + swap(mine, step // 2)
+    mine = mine.reshape(size_x * size_z, SRC_PAIR, SAMP)
+    sources = lax.all_to_all(mine, ("x", "z_hi"), split_axis=0, concat_axis=0, tiled=True)
+    sources, below, above = lax.optimization_barrier((sources, below, above))
+    places = jnp.arange(size_x * size_z, dtype=jnp.int32)
+    z_at, x_back = places >> 2, places & 3
+    z_off = jnp.where(z_at == 3, 2, jnp.where(z_at == 2, 1, -z_at))
+    table = ((at_x - x_back) & (size_x - 1)) * size_z + ((at_z + z_off) & (size_z - 1))
     low = jnp.stack([own, below])
     before_low, after_low = shifted(low, "x", 1), shifted(low, "x", -1)
     half = own.shape[0] // 2
     opposite = [shifted(below[:half], "z_hi", 1), shifted(above[half:], "z_hi", -1)]
     high = jnp.stack([above, jnp.concatenate(opposite, axis=0)])
-    dealt = deal(at_z.reshape(1), dealt)
-    dealt = [dealt[0]] + [shifted(dealt[by], "z_hi", by) for by in range(1, 4)]
-    dealt, high = lax.optimization_barrier((dealt, high))
     before_high, after_high = shifted(high, "x", 1), shifted(high, "x", -1)
-    sources = jnp.concatenate([dealt[0], dealt[1], dealt[3], dealt[2]], axis=0)
     sources, before_low, after_low = lax.optimization_barrier((sources, before_low, after_low))
     far_low = shifted(before_low, "x", 1)
     near = [(0, 0, low), (0, 2, high), (1, 0, before_low), (3, 0, after_low)]
-    total = correlate(sources, near, None, core, False)
+    total = correlate(table, sources, near, None, core, False)
     total, before_high, after_high = lax.optimization_barrier((total, before_high, after_high))
     far_high = shifted(after_high, "x", -1)
-    total = correlate(sources, [(1, 2, before_high), (3, 2, after_high)], total, core, False)
-    total = correlate(sources, [(2, 0, far_low), (2, 2, far_high)], total, core, True)
+    total = correlate(table, sources, [(1, 2, before_high), (3, 2, after_high)], total, core, False)
+    total = correlate(table, sources, [(2, 0, far_low), (2, 2, far_high)], total, core, True)
     kept, passed = total
     got = shifted(passed, "core", 1)
     factor = 1.0 / math.sqrt(SAMP * size_x * size_z * 2)

time: 93.4 us -> 101 us (1.081)
  waiting for transfers between devices: 13.4 us -> 20.8 us
  starting transfers between devices: 43.4 us -> 45.1 us
  Pallas kernels: 28.9 us -> 27.8 us
    all_to_all x0 -> x1, starting transfers between devices: none -> 8.3 us  [shards(): lax.all_to_all(mine, ('x', 'z_hi'), split_axis=0, concat_axis=0, tiled=True)]
    ppermute x17 -> x11, starting transfers between devices: 36.7 us -> 29.2 us  [shifted(): lax.ppermute(value, axis, [(i, (i + by) % size) for i in range(size)])]
    all_to_all x0 -> x1, waiting for transfers between devices: none -> 5.25 us  [shards(): lax.all_to_all(mine, ('x', 'z_hi'), split_axis=0, concat_axis=0, tiled=True)]
    ppermute x17 -> x11, waiting for transfers between devices: 7.08 us -> 10.7 us  [shifted(): lax.ppermute(value, axis, [(i, (i + by) % size) for i in range(size)])]
    pallas_call x2 -> x0, Pallas kernels: 3.11 us -> none  [deal(): pl.pallas_call(deal_body, in_specs=[smem] + [vmem] * len(arrays), out_spe...]
    pallas_call x3, Pallas kernels: 22.7 us -> 24.8 us  [correlate(): pl.pallas_call(body, grid_spec=pltpu.PrefetchScalarGridSpec(num_scalar_pr...]
    concatenate x1 -> x0, other arithmetic: 1.44 us -> none  [shards(): sources = jnp.concatenate([dealt[0], dealt[1], dealt[3], dealt[2]], axis=0)]
    ppermute x3, waiting for transfers between devices: 6.28 us -> 4.93 us  [swap(): return lax.ppermute(value, 'chan', [(i, i ^ step) for i in range(chans)])]
  transfers between devices with their start and end apart: 20 -> 15, of which waited for: 7 -> 8; matrix products, arithmetic and copies ran while one was open for 2% -> 1% of each run, Pallas kernels for 20% -> 17%
where the time goes in v6:
time: 101 us; the launch traced here: 100 us
  starting transfers between devices  45.1 us (45%)
  Pallas kernels  27.8 us (28%)
  waiting for transfers between devices  20.8 us (21%)
  other arithmetic  4.57 us (5%)
  local copies, waits for them, and re-layouts  1.75 us (2%)
    ppermute x11, starting transfers between devices, shifted(): lax.ppermute(value, axis, [(i, (i + by) % size) for i in range(size)])  29.2 us
    pallas_call x3, Pallas kernels, correlate(): pl.pallas_call(body, grid_spec=pltpu.PrefetchScalarGridSpec(num_scalar_pr...  24.8 us
    ppermute x11, waiting for transfers between devices, shifted(): lax.ppermute(value, axis, [(i, (i + by) % size) for i in range(size)])  10.7 us
    all_to_all x1, starting transfers between devices, shards(): lax.all_to_all(mine, ('x', 'z_hi'), split_axis=0, concat_axis=0, tiled=True)  8.3 us
    ppermute x3, starting transfers between devices, swap(): return lax.ppermute(value, 'chan', [(i, i ^ step) for i in range(chans)])  7.64 us
    all_to_all x1, waiting for transfers between devices, shards(): lax.all_to_all(mine, ('x', 'z_hi'), split_axis=0, concat_axis=0, tiled=True)  5.25 us
    ppermute x3, waiting for transfers between devices, swap(): return lax.ppermute(value, 'chan', [(i, i ^ step) for i in range(chans)])  4.93 us
    pallas_call x1, Pallas kernels, prep(): pl.pallas_call(prep_body, in_specs=[smem, smem, vmem, vmem, vmem], out_sp...  3.01 us
  transfers between devices with their start and end apart: 15, of which 8 were waited for; matrix products, arithmetic and copies ran while one was open for 1% of the time, Pallas kernels for 17%

profile of v6, /device:TPU:1, one launch (start us, length us, event | category | flops | bytes accessed | tf_op | source)
XLA Modules:
  0.0 100.2 jit_solution(15474394774666481811)
XLA Ops:
  0.0 3.0 %prep.1 = (bf16[256,512]{1,0:T(8,128)(2,1)}, bf16[128,512]{1,0:T(8,128)(2,1)}) custom-call(s32[2]{0:T(128)} %blocks_ref.1, s32[1]{0:T(128)} %bitcast.1.chan_ref, bf16[256,512]{1,0:T(8,128)(2,1)} %bitcast.15, f32[1,65]{1,0:T(1,128)} %bitcast.17, s32[1,256]{1,0:T(1,128)} %counts_ref.1), custom_call_target="tpu_custom_call" | custom-call | tf_op jit(solution)/shard_map/prep/pallas_call | solution.py:83
  3.0 2.5 %collective-permute-start = (bf16[128,512]{1,0:T(8,128)(2,1)}, bf16[128,512]{1,0:T(8,128)(2,1)S(1)}, u32[]{:S(2)}, u32[]{:S(2)}) collective-permute-start(bf16[128,512]{1,0:T(8,128)(2,1)} %get-tuple-element.18), channel_id=1, source_target_pairs={{0,128},{32,160},{64,192},{96,224},{128,0},{160,32},{192,64},{224,... | collective-permute-start | bytes 393224 | tf_op jit(solution)/shard_map/ppermute | solution.py:208
  5.5 2.6 %collective-permute-done = bf16[128,512]{1,0:T(8,128)(2,1)S(1)} collective-permute-done((bf16[128,512]{1,0:T(8,128)(2,1)}, bf16[128,512]{1,0:T(8,128)(2,1)S(1)}, u32[]{:S(2)}, u32[]{:S(2)}) %collective-permute-start) | collective-permute-done | bytes 131104 | tf_op jit(solution)/shard_map/ppermute | solution.py:208
  8.0 0.9 add.24
  9.0 3.7 %collective-permute-start.1 = (bf16[128,512]{1,0:T(8,128)(2,1)S(1)}, bf16[128,512]{1,0:T(8,128)(2,1)S(1)}, u32[]{:S(2)}, u32[]{:S(2)}) collective-permute-start(bf16[128,512]{1,0:T(8,128)(2,1)S(1)} %add.24), channel_id=1, source_target_pairs={{0,64},{32,96},{64,0},{96,32},{128,192},{160,224},{192,128},{224,1... | collective-permute-start | bytes 393224 | tf_op jit(solution)/shard_map/ppermute | solution.py:208
  12.7 2.4 %collective-permute-done.1 = bf16[128,512]{1,0:T(8,128)(2,1)S(1)} collective-permute-done((bf16[128,512]{1,0:T(8,128)(2,1)S(1)}, bf16[128,512]{1,0:T(8,128)(2,1)S(1)}, u32[]{:S(2)}, u32[]{:S(2)}) %collective-permute-start.1) | collective-permute-done | bytes 131104 | tf_op jit(solution)/shard_map/ppermute | solution.py:208
  15.1 1.4 %collective-permute-start.2 = (bf16[128,512]{1,0:T(8,128)(2,1)S(1)}, bf16[128,512]{1,0:T(8,128)(2,1)S(1)}, u32[]{:S(2)}, u32[]{:S(2)}) collective-permute-start(bf16[128,512]{1,0:T(8,128)(2,1)S(1)} %add.25), channel_id=1, source_target_pairs={{0,32},{32,0},{64,96},{96,64},{128,160},{160,128},{192,224},{224,1... | collective-permute-start | bytes 393224 | tf_op jit(solution)/shard_map/ppermute | solution.py:208
  16.6 3.0 %collective-permute-start.3 = (bf16[256,512]{1,0:T(8,128)(2,1)}, bf16[256,512]{1,0:T(8,128)(2,1)S(1)}, u32[]{:S(2)}, u32[]{:S(2)}) collective-permute-start(bf16[256,512]{1,0:T(8,128)(2,1)} %get-tuple-element.19), channel_id=1, source_target_pairs={{0,2},{2,4},{4,6},{6,0},{1,3},{3,5},{5,7},{7,1},{8,10},{10,12},{12... | collective-permute-start | bytes 786440 | tf_op jit(solution)/shard_map/ppermute | solution.py:195
  19.5 2.7 %collective-permute-start.4 = (bf16[256,512]{1,0:T(8,128)(2,1)}, bf16[256,512]{1,0:T(8,128)(2,1)S(1)}, u32[]{:S(2)}, u32[]{:S(2)}) collective-permute-start(bf16[256,512]{1,0:T(8,128)(2,1)} %get-tuple-element.19), channel_id=1, source_target_pairs={{0,6},{2,0},{4,2},{6,4},{1,7},{3,1},{5,3},{7,5},{8,14},{10,8},{12,... | collective-permute-start | bytes 786440 | tf_op jit(solution)/shard_map/ppermute | solution.py:195
  22.2 0.7 add_bitcast_fusion
  22.9 8.3 %all-to-all-start = ((bf16[16,8,512]{2,1,0:T(8,128)(2,1)}), bf16[16,8,512]{2,1,0:T(8,128)(2,1)S(1)}, u32[]{:S(2)}, u32[]{:S(2)}) async-start(bf16[16,8,512]{2,1,0:T(8,128)(2,1)} %add_bitcast_fusion), calls=%async_computation | async-start | bytes 262144 | tf_op jit(solution)/shard_map/all_to_all | solution.py:217
  31.2 4.2 %collective-permute-done.4 = bf16[256,512]{1,0:T(8,128)(2,1)S(1)} collective-permute-done((bf16[256,512]{1,0:T(8,128)(2,1)}, bf16[256,512]{1,0:T(8,128)(2,1)S(1)}, u32[]{:S(2)}, u32[]{:S(2)}) %collective-permute-start.4) | collective-permute-done | bytes 262176 | tf_op jit(solution)/shard_map/ppermute | solution.py:195
  35.5 5.3 %all-to-all-done.refs_2_ = bf16[16,8,512]{2,1,0:T(8,128)(2,1)S(1)} async-done(((bf16[16,8,512]{2,1,0:T(8,128)(2,1)}), bf16[16,8,512]{2,1,0:T(8,128)(2,1)S(1)}, u32[]{:S(2)}, u32[]{:S(2)}) %all-to-all-start) | async-done | bytes 131104 | tf_op jit(solution)/shard_map/all_to_all | solution.py:217
  40.7 0.7 collective-permute-start.8
  41.4 3.1 %collective-permute-start.9 = (bf16[128,512]{1,0:T(8,128)(2,1)S(1)}, bf16[128,512]{1,0:T(8,128)(2,1)S(1)}, u32[]{:S(2)}, u32[]{:S(2)}) collective-permute-start(bf16[128,512]{1,0:T(8,128)(2,1)S(1)} %slice.7), channel_id=1, source_target_pairs={{0,6},{2,0},{4,2},{6,4},{1,7},{3,1},{5,3},{7,5},{8,14},{10,8},{12,... | collective-permute-start | bytes 393224 | tf_op jit(solution)/shard_map/ppermute | solution.py:195
  44.5 0.1 collective-permute-start.5
  44.6 2.7 %collective-permute-start.6 = (bf16[2,256,512]{2,1,0:T(8,128)(2,1)S(1)}, bf16[2,256,512]{2,1,0:T(8,128)(2,1)S(1)}, u32[]{:S(2)}, u32[]{:S(2)}) collective-permute-start(bf16[2,256,512]{2,1,0:T(8,128)(2,1)S(1)} %pad_maximum_fusion.refs_3_), channel_id=1, source_target_pairs={{0,24},{8,0},{16,8},{24,16},{1,25},{9,1},{17,9},{25,17},{2,26},{10... | collective-permute-start | bytes 1572872 | tf_op jit(solution)/shard_map/ppermute | solution.py:195
  47.3 0.9 collective-permute-done.8
  48.4 2.7 %collective-permute-start.11 = (bf16[2,256,512]{2,1,0:T(8,128)(2,1)S(1)}, bf16[2,256,512]{2,1,0:T(8,128)(2,1)S(1)}, u32[]{:S(2)}, u32[]{:S(2)}) collective-permute-start(bf16[2,256,512]{2,1,0:T(8,128)(2,1)S(1)} %pad_maximum_fusion.1.refs_4_), channel_id=1, source_target_pairs={{0,24},{8,0},{16,8},{24,16},{1,25},{9,1},{17,9},{25,17},{2,26},{10... | collective-permute-start | bytes 1572872 | tf_op jit(solution)/shard_map/ppermute | solution.py:195
  51.0 0.5 and_add_fusion.refs_0_
  51.6 2.3 %collective-permute-done.5.refs_5_ = bf16[2,256,512]{2,1,0:T(8,128)(2,1)S(1)} collective-permute-done((bf16[2,256,512]{2,1,0:T(8,128)(2,1)S(1)}, bf16[2,256,512]{2,1,0:T(8,128)(2,1)S(1)}, u32[]{:S(2)}, u32[]{:S(2)}) %collective-permute-start.5) | collective-permute-done | bytes 524320 | tf_op jit(solution)/shard_map/ppermute | solution.py:195
  54.0 0.7 copy-done.3
  54.7 0.2 copy-done.4
  54.9 10.2 %correlate.3.refs_5_ = f32[8,208,256]{2,1,0:T(8,128)} custom-call(s32[16]{0:T(128)} %and_add_fusion.refs_0_, s32[1]{0:T(128)} %bitcast.refs_1_, bf16[16,8,512]{2,1,0:T(8,128)(2,1)} %copy-done.2, bf16[2,256,512]{2,1,0:T(8,128)(2,1)} %copy-done, bf16[2,256,512]{2,1,0:T(8,128)(2,1)} %copy-done.1, bf16[2,256,512]{2,1,0:T(8,128)(2,1)} %copy-done.3, ...), custom_call_target="tpu_custom_call" | custom-call | tf_op jit(solution)/shard_map/correlate/pallas_call | solution.py:179
  65.1 2.7 %collective-permute-start.12 = (bf16[2,256,512]{2,1,0:T(8,128)(2,1)S(1)}, bf16[2,256,512]{2,1,0:T(8,128)(2,1)S(1)}, u32[]{:S(2)}, u32[]{:S(2)}) collective-permute-start(bf16[2,256,512]{2,1,0:T(8,128)(2,1)S(1)} %collective-permute-done.11.refs_4_), channel_id=1, source_target_pairs={{0,24},{8,0},{16,8},{24,16},{1,25},{9,1},{17,9},{25,17},{2,26},{10... | collective-permute-start | bytes 1572872 | tf_op jit(solution)/shard_map/ppermute | solution.py:195
  67.8 7.1 %correlate.4.refs_5_ = f32[8,208,256]{2,1,0:T(8,128)} custom-call(s32[16]{0:T(128)} %and_add_fusion.refs_0_, s32[1]{0:T(128)} %bitcast.refs_1_, bf16[16,8,512]{2,1,0:T(8,128)(2,1)} %copy-done.2, bf16[2,256,512]{2,1,0:T(8,128)(2,1)} %copy-done.6, bf16[2,256,512]{2,1,0:T(8,128)(2,1)} %copy-done.5, f32[8,208,256]{2,1,0:T(8,128)} %correlate.3.refs_5_), custom_call_target="tpu_custom_call" | custom-call | tf_op jit(solution)/shard_map/correlate/pallas_call | solution.py:179
  74.9 1.0 %collective-permute-done.7.refs_3_ = bf16[2,256,512]{2,1,0:T(8,128)(2,1)} collective-permute-done((bf16[2,256,512]{2,1,0:T(8,128)(2,1)S(1)}, bf16[2,256,512]{2,1,0:T(8,128)(2,1)}, u32[]{:S(2)}, u32[]{:S(2)}) %collective-permute-start.7) | collective-permute-done | bytes 524320 | tf_op jit(solution)/shard_map/ppermute | solution.py:195
  75.9 0.8 copy-done.7
  76.7 7.6 %correlate.5 = (f32[201,4,256]{2,1,0:T(4,128)}, f32[201,4,256]{2,1,0:T(4,128)}) custom-call(s32[16]{0:T(128)} %and_add_fusion.refs_0_, s32[1]{0:T(128)} %bitcast.refs_1_, bf16[16,8,512]{2,1,0:T(8,128)(2,1)} %copy-done.2, bf16[2,256,512]{2,1,0:T(8,128)(2,1)} %collective-permute-done.7.refs_3_, bf16[2,256,512]{2,1,0:T(8,128)(2,1)} %copy-done.7, ...), custom_call_target="tpu_custom_call" | custom-call | tf_op jit(solution)/shard_map/correlate/pallas_call | solution.py:179
  84.3 11.5 %collective-permute-start.13 = (f32[201,4,256]{2,1,0:T(4,128)}, f32[201,4,256]{2,1,0:T(4,128)S(1)}, u32[]{:S(2)}, u32[]{:S(2)}) collective-permute-start(f32[201,4,256]{2,1,0:T(4,128)} %get-tuple-element.30), channel_id=1, source_target_pairs={{0,1},{1,0},{2,3},{3,2},{4,5},{5,4},{6,7},{7,6},{8,9},{9,8},{10,11... | collective-permute-start | bytes 2469896 | tf_op jit(solution)/shard_map/ppermute | solution.py:195
  95.7 2.2 %collective-permute-done.13 = f32[201,4,256]{2,1,0:T(4,128)S(1)} collective-permute-done((f32[201,4,256]{2,1,0:T(4,128)}, f32[201,4,256]{2,1,0:T(4,128)S(1)}, u32[]{:S(2)}, u32[]{:S(2)}) %collective-permute-start.13) | collective-permute-done | bytes 823328 | tf_op jit(solution)/shard_map/ppermute | solution.py:195
  97.9 2.3 %multiply_bitcast_fusion = f32[4,201,256]{2,0,1:T(4,128)} fusion(f32[201,4,256]{2,1,0:T(4,128)} %get-tuple-element.29, f32[201,4,256]{2,1,0:T(4,128)S(1)} %collective-permute-done.13), kind=kLoop, calls=%fused_computation | loop fusion | flops 411648 | bytes 2469888 | tf_op jit(solution)/shard_map/transpose | solution.py:240
  (30 shorter events, 0.4 us)
Async XLA Ops:
  3.0 41.5 %copy-start.8 = (bf16[256,512]{1,0:T(8,128)(2,1)S(1)}, bf16[256,512]{1,0:T(8,128)(2,1)}, u32[]{:S(2)}) copy-start(bf16[256,512]{1,0:T(8,128)(2,1)} %get-tuple-element.19) | copy-start | bytes 786436
  3.0 5.0 %collective-permute-start = (bf16[128,512]{1,0:T(8,128)(2,1)}, bf16[128,512]{1,0:T(8,128)(2,1)S(1)}, u32[]{:S(2)}, u32[]{:S(2)}) collective-permute-start(bf16[128,512]{1,0:T(8,128)(2,1)} %get-tuple-element.18), channel_id=1, source_target_pairs={{0,128},{32,160},{64,192},{96,224},{128,0},{160,32},{192,64},{224,... | collective-permute-start | bytes 393224 | tf_op jit(solution)/shard_map/ppermute | solution.py:208
  9.0 6.1 %collective-permute-start.1 = (bf16[128,512]{1,0:T(8,128)(2,1)S(1)}, bf16[128,512]{1,0:T(8,128)(2,1)S(1)}, u32[]{:S(2)}, u32[]{:S(2)}) collective-permute-start(bf16[128,512]{1,0:T(8,128)(2,1)S(1)} %add.24), channel_id=1, source_target_pairs={{0,64},{32,96},{64,0},{96,32},{128,192},{160,224},{192,128},{224,1... | collective-permute-start | bytes 393224 | tf_op jit(solution)/shard_map/ppermute | solution.py:208
  15.1 7.1 %collective-permute-start.2 = (bf16[128,512]{1,0:T(8,128)(2,1)S(1)}, bf16[128,512]{1,0:T(8,128)(2,1)S(1)}, u32[]{:S(2)}, u32[]{:S(2)}) collective-permute-start(bf16[128,512]{1,0:T(8,128)(2,1)S(1)} %add.25), channel_id=1, source_target_pairs={{0,32},{32,0},{64,96},{96,64},{128,160},{160,128},{192,224},{224,1... | collective-permute-start | bytes 393224 | tf_op jit(solution)/shard_map/ppermute | solution.py:208
  16.6 14.6 %collective-permute-start.3 = (bf16[256,512]{1,0:T(8,128)(2,1)}, bf16[256,512]{1,0:T(8,128)(2,1)S(1)}, u32[]{:S(2)}, u32[]{:S(2)}) collective-permute-start(bf16[256,512]{1,0:T(8,128)(2,1)} %get-tuple-element.19), channel_id=1, source_target_pairs={{0,2},{2,4},{4,6},{6,0},{1,3},{3,5},{5,7},{7,1},{8,10},{10,12},{12... | collective-permute-start | bytes 786440 | tf_op jit(solution)/shard_map/ppermute | solution.py:195
  19.5 15.9 %collective-permute-start.4 = (bf16[256,512]{1,0:T(8,128)(2,1)}, bf16[256,512]{1,0:T(8,128)(2,1)S(1)}, u32[]{:S(2)}, u32[]{:S(2)}) collective-permute-start(bf16[256,512]{1,0:T(8,128)(2,1)} %get-tuple-element.19), channel_id=1, source_target_pairs={{0,6},{2,0},{4,2},{6,4},{1,7},{3,1},{5,3},{7,5},{8,14},{10,8},{12,... | collective-permute-start | bytes 786440 | tf_op jit(solution)/shard_map/ppermute | solution.py:195
  22.9 17.8 %all-to-all-start = ((bf16[16,8,512]{2,1,0:T(8,128)(2,1)}), bf16[16,8,512]{2,1,0:T(8,128)(2,1)S(1)}, u32[]{:S(2)}, u32[]{:S(2)}) async-start(bf16[16,8,512]{2,1,0:T(8,128)(2,1)} %add_bitcast_fusion), calls=%async_computation | async-start | bytes 262144 | tf_op jit(solution)/shard_map/all_to_all | solution.py:217
  40.7 13.2 %copy-start.2 = (bf16[16,8,512]{2,1,0:T(8,128)(2,1)}, bf16[16,8,512]{2,1,0:T(8,128)(2,1)S(1)}, u32[]{:S(2)}) copy-start(bf16[16,8,512]{2,1,0:T(8,128)(2,1)S(1)} %all-to-all-done.refs_2_) | copy-start | bytes 393220
  40.7 7.5 %collective-permute-start.8 = (bf16[128,512]{1,0:T(8,128)(2,1)S(1)}, bf16[128,512]{1,0:T(8,128)(2,1)S(1)}, u32[]{:S(2)}, u32[]{:S(2)}) collective-permute-start(bf16[128,512]{1,0:T(8,128)(2,1)S(1)} %slice.6), channel_id=1, source_target_pairs={{0,2},{2,4},{4,6},{6,0},{1,3},{3,5},{5,7},{7,1},{8,10},{10,12},{12... | collective-permute-start | bytes 393224 | tf_op jit(solution)/shard_map/ppermute | solution.py:195
  41.4 6.8 %collective-permute-start.9 = (bf16[128,512]{1,0:T(8,128)(2,1)S(1)}, bf16[128,512]{1,0:T(8,128)(2,1)S(1)}, u32[]{:S(2)}, u32[]{:S(2)}) collective-permute-start(bf16[128,512]{1,0:T(8,128)(2,1)S(1)} %slice.7), channel_id=1, source_target_pairs={{0,6},{2,0},{4,2},{6,4},{1,7},{3,1},{5,3},{7,5},{8,14},{10,8},{12,... | collective-permute-start | bytes 393224 | tf_op jit(solution)/shard_map/ppermute | solution.py:195
  44.5 9.4 %copy-start = (bf16[2,256,512]{2,1,0:T(8,128)(2,1)}, bf16[2,256,512]{2,1,0:T(8,128)(2,1)S(1)}, u32[]{:S(2)}) copy-start(bf16[2,256,512]{2,1,0:T(8,128)(2,1)S(1)} %pad_maximum_fusion.refs_3_) | copy-start | bytes 1572868
  44.5 9.3 %collective-permute-start.5 = (bf16[2,256,512]{2,1,0:T(8,128)(2,1)S(1)}, bf16[2,256,512]{2,1,0:T(8,128)(2,1)S(1)}, u32[]{:S(2)}, u32[]{:S(2)}) collective-permute-start(bf16[2,256,512]{2,1,0:T(8,128)(2,1)S(1)} %pad_maximum_fusion.refs_3_), channel_id=1, source_target_pairs={{0,8},{8,16},{16,24},{24,0},{1,9},{9,17},{17,25},{25,1},{2,10},{10... | collective-permute-start | bytes 1572872 | tf_op jit(solution)/shard_map/ppermute | solution.py:195
  44.6 9.2 %collective-permute-start.6 = (bf16[2,256,512]{2,1,0:T(8,128)(2,1)S(1)}, bf16[2,256,512]{2,1,0:T(8,128)(2,1)S(1)}, u32[]{:S(2)}, u32[]{:S(2)}) collective-permute-start(bf16[2,256,512]{2,1,0:T(8,128)(2,1)S(1)} %pad_maximum_fusion.refs_3_), channel_id=1, source_target_pairs={{0,24},{8,0},{16,8},{24,16},{1,25},{9,1},{17,9},{25,17},{2,26},{10... | collective-permute-start | bytes 1572872 | tf_op jit(solution)/shard_map/ppermute | solution.py:195
  48.3 5.7 %copy-start.1 = (bf16[2,256,512]{2,1,0:T(8,128)(2,1)}, bf16[2,256,512]{2,1,0:T(8,128)(2,1)S(1)}, u32[]{:S(2)}) copy-start(bf16[2,256,512]{2,1,0:T(8,128)(2,1)S(1)} %pad_maximum_fusion.1.refs_4_) | copy-start | bytes 1572868
  48.3 16.8 %collective-permute-start.10 = (bf16[2,256,512]{2,1,0:T(8,128)(2,1)S(1)}, bf16[2,256,512]{2,1,0:T(8,128)(2,1)S(1)}, u32[]{:S(2)}, u32[]{:S(2)}) collective-permute-start(bf16[2,256,512]{2,1,0:T(8,128)(2,1)S(1)} %pad_maximum_fusion.1.refs_4_), channel_id=1, source_target_pairs={{0,8},{8,16},{16,24},{24,0},{1,9},{9,17},{17,25},{25,1},{2,10},{10... | collective-permute-start | bytes 1572872 | tf_op jit(solution)/shard_map/ppermute | solution.py:195
  48.4 16.7 %collective-permute-start.11 = (bf16[2,256,512]{2,1,0:T(8,128)(2,1)S(1)}, bf16[2,256,512]{2,1,0:T(8,128)(2,1)S(1)}, u32[]{:S(2)}, u32[]{:S(2)}) collective-permute-start(bf16[2,256,512]{2,1,0:T(8,128)(2,1)S(1)} %pad_maximum_fusion.1.refs_4_), channel_id=1, source_target_pairs={{0,24},{8,0},{16,8},{24,16},{1,25},{9,1},{17,9},{25,17},{2,26},{10... | collective-permute-start | bytes 1572872 | tf_op jit(solution)/shard_map/ppermute | solution.py:195
  53.8 0.8 copy-start.3
  53.9 1.0 %copy-start.4 = (bf16[2,256,512]{2,1,0:T(8,128)(2,1)}, bf16[2,256,512]{2,1,0:T(8,128)(2,1)S(1)}, u32[]{:S(2)}) copy-start(bf16[2,256,512]{2,1,0:T(8,128)(2,1)S(1)} %collective-permute-done.6.refs_6_) | copy-start | bytes 1572868
  53.9 22.1 %collective-permute-start.7 = (bf16[2,256,512]{2,1,0:T(8,128)(2,1)S(1)}, bf16[2,256,512]{2,1,0:T(8,128)(2,1)}, u32[]{:S(2)}, u32[]{:S(2)}) collective-permute-start(bf16[2,256,512]{2,1,0:T(8,128)(2,1)S(1)} %collective-permute-done.5.refs_5_), channel_id=1, source_target_pairs={{0,8},{8,16},{16,24},{24,0},{1,9},{9,17},{17,25},{25,1},{2,10},{10... | collective-permute-start | bytes 1572872 | tf_op jit(solution)/shard_map/ppermute | solution.py:195
  65.1 2.8 %copy-start.6 = (bf16[2,256,512]{2,1,0:T(8,128)(2,1)}, bf16[2,256,512]{2,1,0:T(8,128)(2,1)S(1)}, u32[]{:S(2)}) copy-start(bf16[2,256,512]{2,1,0:T(8,128)(2,1)S(1)} %collective-permute-done.10.refs_3_) | copy-start | bytes 1572868
  65.1 2.7 %copy-start.5 = (bf16[2,256,512]{2,1,0:T(8,128)(2,1)}, bf16[2,256,512]{2,1,0:T(8,128)(2,1)S(1)}, u32[]{:S(2)}) copy-start(bf16[2,256,512]{2,1,0:T(8,128)(2,1)S(1)} %collective-permute-done.11.refs_4_) | copy-start | bytes 1572868
  65.1 10.8 %collective-permute-start.12 = (bf16[2,256,512]{2,1,0:T(8,128)(2,1)S(1)}, bf16[2,256,512]{2,1,0:T(8,128)(2,1)S(1)}, u32[]{:S(2)}, u32[]{:S(2)}) collective-permute-start(bf16[2,256,512]{2,1,0:T(8,128)(2,1)S(1)} %collective-permute-done.11.refs_4_), channel_id=1, source_target_pairs={{0,24},{8,0},{16,8},{24,16},{1,25},{9,1},{17,9},{25,17},{2,26},{10... | collective-permute-start | bytes 1572872 | tf_op jit(solution)/shard_map/ppermute | solution.py:195
  75.9 0.8 copy-start.7
  84.3 13.6 %collective-permute-start.13 = (f32[201,4,256]{2,1,0:T(4,128)}, f32[201,4,256]{2,1,0:T(4,128)S(1)}, u32[]{:S(2)}, u32[]{:S(2)}) collective-permute-start(f32[201,4,256]{2,1,0:T(4,128)} %get-tuple-element.30), channel_id=1, source_target_pairs={{0,1},{1,0},{2,3},{3,2},{4,5},{5,4},{6,7},{7,6},{8,9},{9,8},{10,11... | collective-permute-start | bytes 2469896 | tf_op jit(solution)/shard_map/ppermute | solution.py:195
